TPU v7x, 32 devices: a whole 2x2x4 slice. The times are simulated.
32 devices in a mesh: expert: 8 (over z, x), fsdp: 4 (over y, core).
Axes of the slice: x: 2, y: 2, z: 4, core: 2. Of those that a mesh axis runs over, the one named last changes fastest.
Arguments:
- tokens: bfloat16 [160, 197, 512], P(('expert', 'fsdp')), may hold values from -6 to 6
- ln1_gain: bfloat16 [512], P('fsdp'), may hold values from 0.5 to 1.5
- ln1_bias: bfloat16 [512], P('fsdp'), may hold values from -1.796875 to 1.796875
- w_qkv: bfloat16 [512, 1536], P('fsdp'), may hold values from -0.25 to 0.25
- q_bias: bfloat16 [512], P('fsdp'), may hold values from -1.796875 to 1.796875
- v_bias: bfloat16 [512], P('fsdp'), may hold values from -1.796875 to 1.796875
- w_out: bfloat16 [512, 512], P('fsdp'), may hold values from -1.5 to 1.5
- out_bias: bfloat16 [512], P('fsdp'), may hold values from -1.796875 to 1.796875
- ln2_gain: bfloat16 [512], P('fsdp'), may hold values from 0.5 to 1.5
- ln2_bias: bfloat16 [512], P('fsdp'), may hold values from -1.796875 to 1.796875
- w_router: bfloat16 [512, 8], P('fsdp'), may hold values from -0.1875 to 0.1875
- expert_w1: bfloat16 [8, 512, 2048], P('expert', 'fsdp'), may hold values from -0.25 to 0.25
- expert_b1: bfloat16 [8, 2048], P('expert', 'fsdp'), may hold values from -1.796875 to 1.796875
- expert_w2: bfloat16 [8, 2048, 512], P('expert', 'fsdp'), may hold values from -0.75 to 0.75
- expert_b2: bfloat16 [8, 512], P('expert', 'fsdp'), may hold values from -6 to 6
- route_ids: int32 [31520, 2], P(('expert', 'fsdp')), may hold values from 0 to 7, all different within a row; in each aligned block of 985 rows (0 to 984, 985 to 1969, ...) at most 432 rows name the same one
- clip_threshold: int32 [8], replicated, may hold values from 2 to 4
- grad_output: bfloat16 [160, 197, 512], P(('expert', 'fsdp')), may hold values from -6 to 6
Outputs:
- output: bfloat16 [160, 197, 512], P(('expert', 'fsdp'))
- input_grad: float32 [160, 197, 512], P(('expert', 'fsdp'))
- grad_ln1_gain: float32 [512], P('fsdp')
- grad_ln1_bias: float32 [512], P('fsdp')
- grad_w_qkv: float32 [512, 1536], P('fsdp')
- grad_q_bias: float32 [512], P('fsdp')
- grad_v_bias: float32 [512], P('fsdp')
- grad_w_out: float32 [512, 512], P('fsdp')
- grad_out_bias: float32 [512], P('fsdp')
- grad_ln2_gain: float32 [512], P('fsdp')
- grad_ln2_bias: float32 [512], P('fsdp')
- grad_w_router: float32 [512, 8], P('fsdp')
- grad_expert_w1: float32 [8, 512, 2048], P('expert', 'fsdp')
- grad_expert_b1: float32 [8, 2048], P('expert', 'fsdp')
- grad_expert_w2: float32 [8, 2048, 512], P('expert', 'fsdp')
- grad_expert_b2: float32 [8, 512], P('expert', 'fsdp')
- clipped_qkv: bfloat16 [512, 1536], P('fsdp')
Inputs may be any that keep to these rules, and one draw needn't show every extreme that they name: `route_ids`: each row names 2 different experts; among the 985 rows of one device no expert is named by more than 432 rows, and in some device's rows one expert is named by exactly 432.
All inputs are finite; a program needn't handle non-finite values.
Results may differ from a plain program's by a relative error of at most 0.024.
Values may be sent and summed in bfloat16 or wider, within the bound.
No kernel may reach another device: no remote copies, remote signals or barrier semaphores. Data moves between devices by JAX's collectives and lax.ppermute only.
A program may use at most 256 MiB of HBM per device.

v0:
```python
import jax
import jax.numpy as jnp
from jax import lax
from jax.sharding import PartitionSpec as P

HEADS = 8


norm_eps = 1e-06
highest = lax.Precision.HIGHEST


def layer_norm(matrix, norm_gain, norm_shift):
    centred = matrix - jnp.mean(matrix, axis=1, keepdims=True)
    inverse = lax.rsqrt(jnp.mean(centred * centred, axis=1, keepdims=True) + norm_eps)
    normed = centred * inverse
    return (normed * norm_gain + norm_shift, normed, inverse)


def norm_backward(upstream, norm_gain, normed, inverse):
    scaled = upstream * norm_gain
    spread = (
        scaled
        - jnp.mean(scaled, axis=1, keepdims=True)
        - normed * jnp.mean(scaled * normed, axis=1, keepdims=True)
    )
    return (spread * inverse, jnp.sum(upstream * normed, axis=0), jnp.sum(upstream, axis=0))


def gelu_exact(values):
    return jax.nn.gelu(values, approximate=False)


def shards(
    tokens,
    ln1_gain,
    ln1_bias,
    w_qkv,
    q_bias,
    v_bias,
    w_out,
    out_bias,
    ln2_gain,
    ln2_bias,
    w_router,
    expert_w1,
    expert_b1,
    expert_w2,
    expert_b2,
    route_ids,
    clip_threshold,
    grad_output,
):
    gathered = (
        lax.all_gather(ln1_gain, "fsdp", axis=0, tiled=True),
        lax.all_gather(ln1_bias, "fsdp", axis=0, tiled=True),
        lax.all_gather(w_qkv, "fsdp", axis=0, tiled=True),
        lax.all_gather(q_bias, "fsdp", axis=0, tiled=True),
        lax.all_gather(v_bias, "fsdp", axis=0, tiled=True),
        lax.all_gather(w_out, "fsdp", axis=0, tiled=True),
        lax.all_gather(out_bias, "fsdp", axis=0, tiled=True),
        lax.all_gather(ln2_gain, "fsdp", axis=0, tiled=True),
        lax.all_gather(ln2_bias, "fsdp", axis=0, tiled=True),
        lax.all_gather(w_router, "fsdp", axis=0, tiled=True),
        lax.all_gather(expert_w1, "fsdp", axis=1, tiled=True),
        lax.all_gather(expert_b1, "fsdp", axis=1, tiled=True),
        lax.all_gather(expert_w2, "fsdp", axis=1, tiled=True),
        lax.all_gather(expert_b2, "fsdp", axis=1, tiled=True),
    )
    gain_one = gathered[0].astype(jnp.float32)
    shift_one = gathered[1].astype(jnp.float32)
    qkv_weight = gathered[2]
    query_bias = gathered[3].astype(jnp.float32)
    value_bias = gathered[4].astype(jnp.float32)
    out_weight = gathered[5]
    out_shift = gathered[6].astype(jnp.float32)
    gain_two = gathered[7].astype(jnp.float32)
    shift_two = gathered[8].astype(jnp.float32)
    router_weight = gathered[9].astype(jnp.float32)
    first_weight = gathered[10][0]
    first_bias = gathered[11][0].astype(jnp.float32)
    second_weight = gathered[12][0]
    second_bias = gathered[13][0].astype(jnp.float32)
    image_count, sequence, feature_width = tokens.shape
    token_count = image_count * sequence
    head_count = HEADS
    head_size = feature_width // head_count
    score_scale = head_size ** (-0.5)
    route_top = route_ids.shape[1]
    expert_total = router_weight.shape[1]
    capacity = (7 * token_count // (2 * expert_total) + 7) // 8 * 8
    head_shape = (image_count, sequence, head_count, head_size)
    residual = tokens.astype(jnp.float32).reshape(token_count, feature_width)
    normed_in, hat_one, inverse_one = layer_norm(residual, gain_one, shift_one)
    normed_low = normed_in.astype(jnp.bfloat16)
    projected = jnp.dot(normed_low, qkv_weight, preferred_element_type=jnp.float32)
    queries = (projected[:, :feature_width] + query_bias).astype(jnp.bfloat16).reshape(head_shape)
    key_rows = (
        projected[:, feature_width : 2 * feature_width].astype(jnp.bfloat16).reshape(head_shape)
    )
    value_rows = (
        (projected[:, 2 * feature_width :] + value_bias).astype(jnp.bfloat16).reshape(head_shape)
    )
    scores = (
        jnp.einsum("bqhd,bkhd->bhqk", queries, key_rows, preferred_element_type=jnp.float32)
        * score_scale
    )
    head_peak = jnp.max(scores, axis=(0, 2, 3))
    row_top = jnp.max(scores, axis=3, keepdims=True)
    log_total = row_top + jnp.log(jnp.sum(jnp.exp(scores - row_top), axis=3, keepdims=True))
    attn_low = jnp.exp(scores - log_total).astype(jnp.bfloat16)
    mixed_rows = jnp.einsum(
        "bhqk,bkhd->bqhd", attn_low, value_rows, preferred_element_type=jnp.float32
    )
    mixed_low = mixed_rows.astype(jnp.bfloat16).reshape(token_count, feature_width)
    hidden = (
        residual + jnp.dot(mixed_low, out_weight, preferred_element_type=jnp.float32) + out_shift
    )
    normed_mid, hat_two, inverse_two = layer_norm(hidden, gain_two, shift_two)
    route_prob = jax.nn.softmax(jnp.dot(normed_mid, router_weight, precision=highest), axis=1)
    picked = (
        route_ids[:, :, None] == lax.broadcasted_iota(jnp.int32, (1, 1, expert_total), 2)
    ).astype(jnp.int32)
    picked_float = picked.astype(jnp.float32)
    gate_values = jnp.sum(picked_float * route_prob[:, None, :], axis=2)
    picked_flat = picked.reshape(token_count * route_top, expert_total)
    slot_rank = jnp.sum(
        (jnp.cumsum(picked_flat, axis=0, dtype=jnp.int32) - picked_flat) * picked_flat,
        axis=1,
        dtype=jnp.int32,
    )
    slot_index = route_ids.reshape(-1) * capacity + slot_rank
    mid_low = normed_mid.astype(jnp.bfloat16)
    slot_rows = jnp.broadcast_to(
        mid_low[:, None, :], (token_count, route_top, feature_width)
    ).reshape(token_count * route_top, feature_width)
    outgoing = (
        jnp.zeros((expert_total * capacity, feature_width), jnp.bfloat16)
        .at[slot_index]
        .set(slot_rows)
        .reshape(expert_total, capacity, feature_width)
    )
    arrived = lax.all_to_all(outgoing, "expert", split_axis=0, concat_axis=0, tiled=True)
    flat_in = arrived.reshape(-1, feature_width)
    activation = gelu_exact(
        jnp.dot(flat_in, first_weight, preferred_element_type=jnp.float32) + first_bias
    ).astype(jnp.bfloat16)
    result = (
        jnp.dot(activation, second_weight, preferred_element_type=jnp.float32) + second_bias
    ).astype(jnp.bfloat16)
    produced = result.reshape(arrived.shape)
    returned = lax.all_to_all(produced, "expert", split_axis=0, concat_axis=0, tiled=True)
    slot_out = (
        returned.reshape(expert_total * capacity, feature_width)[slot_index]
        .astype(jnp.float32)
        .reshape(token_count, route_top, feature_width)
    )
    output = (
        (hidden + jnp.sum(gate_values[:, :, None] * slot_out, axis=1))
        .astype(jnp.bfloat16)
        .reshape(tokens.shape)
    )
    upstream = grad_output.astype(jnp.float32).reshape(token_count, feature_width)
    gate_grad = jnp.sum(slot_out * upstream[:, None, :], axis=2)
    slot_grad = (
        (gate_values[:, :, None] * upstream[:, None, :])
        .astype(jnp.bfloat16)
        .reshape(token_count * route_top, feature_width)
    )
    grad_buffer = (
        jnp.zeros((expert_total * capacity, feature_width), jnp.bfloat16)
        .at[slot_index]
        .set(slot_grad)
        .reshape(expert_total, capacity, feature_width)
    )
    grad_arrived = lax.all_to_all(grad_buffer, "expert", split_axis=0, concat_axis=0, tiled=True)
    flat_rows = arrived.reshape(-1, feature_width)
    flat_grad = grad_arrived.reshape(-1, feature_width)
    activation, gelu_back = jax.vjp(
        gelu_exact,
        jnp.dot(flat_rows, first_weight, preferred_element_type=jnp.float32) + first_bias,
    )
    act_low = activation.astype(jnp.bfloat16)
    grad_second = jnp.einsum("rh,rd->hd", act_low, flat_grad, preferred_element_type=jnp.float32)
    grad_second_bias = jnp.sum(flat_grad, axis=0, dtype=jnp.float32)
    act_grad = jnp.einsum("rd,hd->rh", flat_grad, second_weight, preferred_element_type=jnp.float32)
    pre_grad = gelu_back(act_grad)[0].astype(jnp.bfloat16)
    grad_first = jnp.einsum("rd,rh->dh", flat_rows, pre_grad, preferred_element_type=jnp.float32)
    grad_first_bias = jnp.sum(pre_grad, axis=0, dtype=jnp.float32)
    row_grad = (
        jnp.einsum("rh,dh->rd", pre_grad, first_weight, preferred_element_type=jnp.float32)
        .astype(jnp.bfloat16)
        .reshape(grad_arrived.shape)
    )
    row_back = lax.all_to_all(row_grad, "expert", split_axis=0, concat_axis=0, tiled=True)
    slot_back = (
        row_back.reshape(expert_total * capacity, feature_width)[slot_index]
        .astype(jnp.float32)
        .reshape(token_count, route_top, feature_width)
    )
    prob_grad = jnp.sum(picked_float * gate_grad[:, :, None], axis=1)
    logit_grad = route_prob * (prob_grad - jnp.sum(route_prob * prob_grad, axis=1, keepdims=True))
    mid_grad = jnp.sum(slot_back, axis=1) + jnp.einsum(
        "re,de->rd", logit_grad, router_weight, precision=highest
    )
    grad_router = jnp.einsum("rd,re->de", normed_mid, logit_grad, precision=highest)
    norm_part, grad_gain_two, grad_shift_two = norm_backward(
        mid_grad, gain_two, hat_two, inverse_two
    )
    hidden_grad = upstream + norm_part
    branch_low = hidden_grad.astype(jnp.bfloat16)
    grad_out_weight = jnp.einsum(
        "rd,re->de", mixed_low, branch_low, preferred_element_type=jnp.float32
    )
    grad_out_shift = jnp.sum(branch_low, axis=0, dtype=jnp.float32)
    mixed_grad = (
        jnp.einsum("re,de->rd", branch_low, out_weight, preferred_element_type=jnp.float32)
        .astype(jnp.bfloat16)
        .reshape(head_shape)
    )
    score_again = (
        jnp.einsum("bqhd,bkhd->bhqk", queries, key_rows, preferred_element_type=jnp.float32)
        * score_scale
    )
    attn_prob = jnp.exp(score_again - log_total)
    value_grad = jnp.einsum(
        "bhqk,bqhd->bkhd",
        attn_prob.astype(jnp.bfloat16),
        mixed_grad,
        preferred_element_type=jnp.float32,
    ).astype(jnp.bfloat16)
    weight_grad = jnp.einsum(
        "bqhd,bkhd->bhqk", mixed_grad, value_rows, preferred_element_type=jnp.float32
    )
    score_grad = (
        attn_prob * (weight_grad - jnp.sum(attn_prob * weight_grad, axis=3, keepdims=True))
    ).astype(jnp.bfloat16)
    query_grad = (
        jnp.einsum("bhqk,bkhd->bqhd", score_grad, key_rows, preferred_element_type=jnp.float32)
        * score_scale
    ).astype(jnp.bfloat16)
    key_grad = (
        jnp.einsum("bhqk,bqhd->bkhd", score_grad, queries, preferred_element_type=jnp.float32)
        * score_scale
    ).astype(jnp.bfloat16)
    qkv_grad = jnp.concatenate(
        [
            query_grad.reshape(token_count, feature_width),
            key_grad.reshape(token_count, feature_width),
            value_grad.reshape(token_count, feature_width),
        ],
        axis=1,
    )
    grad_qkv = jnp.einsum("rd,re->de", normed_low, qkv_grad, preferred_element_type=jnp.float32)
    grad_query_bias = jnp.sum(qkv_grad[:, :feature_width], axis=0, dtype=jnp.float32)
    grad_value_bias = jnp.sum(qkv_grad[:, 2 * feature_width :], axis=0, dtype=jnp.float32)
    in_grad = jnp.einsum("re,de->rd", qkv_grad, qkv_weight, preferred_element_type=jnp.float32)
    input_part, grad_gain_one, grad_shift_one = norm_backward(
        in_grad, gain_one, hat_one, inverse_one
    )
    input_grad = (hidden_grad + input_part).reshape(tokens.shape)
    shares = (
        lax.psum_scatter(
            grad_gain_one.astype(jnp.bfloat16), "fsdp", scatter_dimension=0, tiled=True
        ).astype(jnp.float32),
        lax.psum_scatter(
            grad_shift_one.astype(jnp.bfloat16), "fsdp", scatter_dimension=0, tiled=True
        ).astype(jnp.float32),
        lax.psum_scatter(
            grad_qkv.astype(jnp.bfloat16), "fsdp", scatter_dimension=0, tiled=True
        ).astype(jnp.float32),
        lax.psum_scatter(
            grad_query_bias.astype(jnp.bfloat16), "fsdp", scatter_dimension=0, tiled=True
        ).astype(jnp.float32),
        lax.psum_scatter(
            grad_value_bias.astype(jnp.bfloat16), "fsdp", scatter_dimension=0, tiled=True
        ).astype(jnp.float32),
        lax.psum_scatter(
            grad_out_weight.astype(jnp.bfloat16), "fsdp", scatter_dimension=0, tiled=True
        ).astype(jnp.float32),
        lax.psum_scatter(
            grad_out_shift.astype(jnp.bfloat16), "fsdp", scatter_dimension=0, tiled=True
        ).astype(jnp.float32),
        lax.psum_scatter(
            grad_gain_two.astype(jnp.bfloat16), "fsdp", scatter_dimension=0, tiled=True
        ).astype(jnp.float32),
        lax.psum_scatter(
            grad_shift_two.astype(jnp.bfloat16), "fsdp", scatter_dimension=0, tiled=True
        ).astype(jnp.float32),
        lax.psum_scatter(
            grad_router.astype(jnp.bfloat16), "fsdp", scatter_dimension=0, tiled=True
        ).astype(jnp.float32),
    )
    summed = (
        lax.psum(shares[0].astype(jnp.bfloat16), "expert").astype(jnp.float32),
        lax.psum(shares[1].astype(jnp.bfloat16), "expert").astype(jnp.float32),
        lax.psum(shares[2].astype(jnp.bfloat16), "expert").astype(jnp.float32),
        lax.psum(shares[3].astype(jnp.bfloat16), "expert").astype(jnp.float32),
        lax.psum(shares[4].astype(jnp.bfloat16), "expert").astype(jnp.float32),
        lax.psum(shares[5].astype(jnp.bfloat16), "expert").astype(jnp.float32),
        lax.psum(shares[6].astype(jnp.bfloat16), "expert").astype(jnp.float32),
        lax.psum(shares[7].astype(jnp.bfloat16), "expert").astype(jnp.float32),
        lax.psum(shares[8].astype(jnp.bfloat16), "expert").astype(jnp.float32),
        lax.psum(shares[9].astype(jnp.bfloat16), "expert").astype(jnp.float32),
    )
    expert_summed = (
        lax.psum_scatter(
            grad_first[None].astype(jnp.bfloat16), "fsdp", scatter_dimension=1, tiled=True
        ).astype(jnp.float32),
        lax.psum_scatter(
            grad_first_bias[None].astype(jnp.bfloat16), "fsdp", scatter_dimension=1, tiled=True
        ).astype(jnp.float32),
        lax.psum_scatter(
            grad_second[None].astype(jnp.bfloat16), "fsdp", scatter_dimension=1, tiled=True
        ).astype(jnp.float32),
        lax.psum_scatter(
            grad_second_bias[None].astype(jnp.bfloat16), "fsdp", scatter_dimension=1, tiled=True
        ).astype(jnp.float32),
    )
    peak_logit = lax.pmax(head_peak, ("expert", "fsdp"))
    limit_value = clip_threshold.astype(jnp.float32)
    root_factor = jnp.sqrt(limit_value / jnp.maximum(peak_logit, limit_value))
    column_scale = jnp.concatenate(
        [
            jnp.repeat(root_factor, head_size),
            jnp.repeat(root_factor, head_size),
            jnp.ones((feature_width,), jnp.float32),
        ]
    )
    clipped_qkv = (w_qkv.astype(jnp.float32) * column_scale).astype(jnp.bfloat16)
    return (
        output,
        input_grad,
        summed[0],
        summed[1],
        summed[2],
        summed[3],
        summed[4],
        summed[5],
        summed[6],
        summed[7],
        summed[8],
        summed[9],
        expert_summed[0],
        expert_summed[1],
        expert_summed[2],
        expert_summed[3],
        clipped_qkv,
    )


def solution(mesh):
    placed = (
        P(("expert", "fsdp"), None, None),
        P("fsdp"),
        P("fsdp"),
        P("fsdp", None),
        P("fsdp"),
        P("fsdp"),
        P("fsdp", None),
        P("fsdp"),
        P("fsdp"),
        P("fsdp"),
        P("fsdp", None),
        P("expert", "fsdp", None),
        P("expert", "fsdp"),
        P("expert", "fsdp", None),
        P("expert", "fsdp"),
        P(("expert", "fsdp"), None),
        P(),
        P(("expert", "fsdp"), None, None),
    )
    return jax.shard_map(
        shards,
        mesh=mesh,
        in_specs=placed,
        out_specs=(
            P(("expert", "fsdp"), None, None),
            P(("expert", "fsdp"), None, None),
            P("fsdp"),
            P("fsdp"),
            P("fsdp", None),
            P("fsdp"),
            P("fsdp"),
            P("fsdp", None),
            P("fsdp"),
            P("fsdp"),
            P("fsdp"),
            P("fsdp", None),
            P("expert", "fsdp", None),
            P("expert", "fsdp"),
            P("expert", "fsdp", None),
            P("expert", "fsdp"),
            P("fsdp", None),
        ),
        check_vma=False,
    )
```

profile of v0, /device:TPU:0, one launch (start us, length us, event | category | flops | bytes accessed | tf_op | source)
XLA Modules:
  0.0 718.8 jit_solution(18381751544721613083)
XLA Ops:
  11.8 6.0 all-gather
  17.8 5.3 all-gather.1
  52.3 7.9 %all_gather.47 = bf16[512,512]{1,0:T(8,128)(2,1)} all-gather(bf16[128,512]{1,0:T(8,128)(2,1)S(1)} %copy-done.46), channel_id=1, replica_groups=mesh['expert'=8,'fsdp'=4] {'fsdp'}, dimensions={0}, use_global_device_ids=true | all-gather | bytes 655360 | tf_op jit(solution)/shard_map/all_gather | solution.py:60
  85.4 5.5 fusion.26
  102.7 5.6 reshape.330
  108.3 13.3 %scatter_custom_fusion = bf16[3456,512]{1,0:T(8,128)(2,1)} fusion(s32[1970]{0:T(1024)S(1)} %bitcast.131, bf16[1970,512]{1,0:T(8,128)(2,1)} %reshape.330, bf16[]{:T(256)} %constant.17.clone.1), kind=kCustom, calls=%fused_computation.69 | custom fusion | bytes 3539456 | tf_op jit(solution)/shard_map/scatter | solution.py:140
  121.6 6.0 all-to-all-start
  135.5 6.1 mul.252
  141.6 5.2 all_gather.53
  152.4 5.6 all_gather.51
  161.2 18.5 %scatter_custom_fusion.1 = bf16[3456,512]{1,0:T(8,128)(2,1)} fusion(s32[1970]{0:T(1024)S(1)} %bitcast.132, f32[1970,512]{1,0:T(8,128)} %mul.252, f32[1970]{0:T(1024)S(1)} %mul.249, bf16[]{:T(256)} %constant.17.clone.1), kind=kCustom, calls=%fused_computation.63 | custom fusion | flops 2017280 | bytes 7581698 | tf_op jit(solution)/shard_map/scatter | solution.py:173
  179.8 27.6 %all-to-all-done = bf16[8,432,512]{2,1,0:T(8,128)(2,1)} async-done(((bf16[8,432,512]{2,1,0:T(8,128)(2,1)}), bf16[8,432,512]{2,1,0:T(8,128)(2,1)}, u32[]{:S(2)}, u32[]{:S(2)}) %all-to-all-start) | async-done | bytes 3538976 | tf_op jit(solution)/shard_map/all_to_all | solution.py:143
  212.0 70.8 %multiply_convert_fusion = (bf16[3456,2048]{1,0:T(8,128)(2,1)}, f32[3456,2048]{1,0:T(8,128)}, f32[3456,2048]{1,0:T(8,128)}) fusion(f32[2048]{0:T(1024)S(1)} %bitcast.142, bf16[3456,512]{1,0:T(8,128)(2,1)} %bitcast.19, bf16[1,512,2048]{2,1,0:T(8,128)(2,1)} %all-gather.13.cloned.1.call-done), kind=kOutput, calls=%fused_computation.7 | convolution fusion | flops 7714897920 | bytes 76423168 | tf_op jit(solution)/shard_map/dot_general | solution.py:146
  282.8 12.5 %add_convert_fusion.1 = bf16[3456,512]{1,0:T(8,128)(2,1)} fusion(bf16[3456,2048]{1,0:T(8,128)(2,1)} %get-tuple-element.48, f32[512]{0:T(512)S(1)} %bitcast.144, bf16[1,2048,512]{2,1,0:T(8,128)(2,1)} %all-gather.15.cloned.1.call-done), kind=kOutput, calls=%fused_computation.25 | convolution fusion | flops 7251296256 | bytes 19793920 | tf_op jit(solution)/shard_map/dot_general | solution.py:149
  295.4 6.0 all-to-all-start.1
  305.0 31.9 %fusion.50 = (bf16[2048]{0:T(1024)(128)(2,1)S(1)}, bf16[3456,2048]{1,0:T(8,128)(2,1)}) fusion(f32[3456,2048]{1,0:T(8,128)} %get-tuple-element.49, bf16[3456,512]{1,0:T(8,128)(2,1)} %bitcast.27, bf16[1,2048,512]{2,1,0:T(8,128)(2,1)} %all-gather.15.cloned.1.call-done, f32[3456,2048]{1,0:T(8,128)} %get-tuple-element.57, f32[2048]{0:T(1024)S(1)} %bitcast.143), kind=kOutput, calls=%fused_computation.138 | convolution fusion | flops 7361001472 | bytes 76427264 | tf_op jit(solution)/shard_map/rd,hd->rh/dot_general | solution.py:186
  338.1 12.6 %convolution_convert_fusion = bf16[3456,512]{1,0:T(8,128)(2,1)} fusion(bf16[3456,2048]{1,0:T(8,128)(2,1)} %get-tuple-element.68, bf16[1,512,2048]{2,1,0:T(8,128)(2,1)} %all-gather.13.cloned.1.call-done), kind=kOutput, calls=%fused_computation.28 | convolution fusion | flops 7249526784 | bytes 19791872 | tf_op jit(solution)/shard_map/rh,dh->rd/dot_general | solution.py:191
  350.7 28.8 %all-to-all-done.1 = bf16[8,432,512]{2,1,0:T(8,128)(2,1)S(1)} async-done(((bf16[8,432,512]{2,1,0:T(8,128)(2,1)}), bf16[8,432,512]{2,1,0:T(8,128)(2,1)S(1)}, u32[]{:S(2)}, u32[]{:S(2)}) %all-to-all-start.1) | async-done | bytes 3538976 | tf_op jit(solution)/shard_map/all_to_all | solution.py:152
  384.1 13.0 %fusion.7 = bf16[1,2048,512]{2,1,0:T(8,128)(2,1)} fusion(bf16[3456,2048]{1,0:T(8,128)(2,1)} %get-tuple-element.48, bf16[3456,512]{1,0:T(8,128)(2,1)} %bitcast.27), kind=kOutput, calls=%fused_computation.36 | convolution fusion | flops 7248805888 | bytes 19791872 | tf_op jit(solution)/shard_map/rh,rd->hd/dot_general | solution.py:184
  397.7 13.0 %fusion.8 = bf16[1,512,2048]{2,1,0:T(8,128)(2,1)} fusion(bf16[3456,512]{1,0:T(8,128)(2,1)} %bitcast.19, bf16[3456,2048]{1,0:T(8,128)(2,1)} %get-tuple-element.68), kind=kOutput, calls=%fused_computation.37 | convolution fusion | flops 7248805888 | bytes 19791872 | tf_op jit(solution)/shard_map/rd,rh->dh/dot_general | solution.py:188
  410.7 9.1 %gather_fusion = bf16[1970,512]{1,0:T(8,128)(2,1)} fusion(bf16[3456,512]{1,0:T(8,128)(2,1)S(1)} %bitcast.112, s32[2048]{0:T(1024)S(1)} %pad_clamp_fusion), kind=kCustom, calls=%fused_computation | custom fusion | bytes 4042440 | tf_op jit(solution)/shard_map/gather | solution.py:154
  419.9 5.6 reshape.306
  425.5 13.6 %multiply_reduce_fusion.3 = (f32[985,2]{1,0:T(8,128)S(1)}, f32[985,512]{1,0:T(8,128)}) fusion(f32[985,2,512]{2,1,0:T(2,128)} %reshape.306, f32[985,512]{1,0:T(8,128)S(1)} %copy-done.7, f32[985,2]{1,0:T(8,128)S(1)} %copy-done.23), kind=kLoop, calls=%fused_computation.31 | loop fusion | flops 3528270 | bytes 8084880 | tf_op jit(solution)/shard_map/reduce_sum | solution.py:164
  439.4 23.3 %all-to-all-done.3 = bf16[8,432,512]{2,1,0:T(8,128)(2,1)} async-done(((bf16[8,432,512]{2,1,0:T(8,128)(2,1)}), bf16[8,432,512]{2,1,0:T(8,128)(2,1)}, u32[]{:S(2)}, u32[]{:S(2)}) %all-to-all-start.3) | async-done | bytes 3538976 | tf_op jit(solution)/shard_map/all_to_all | solution.py:195
  462.7 10.4 %gather_fusion.1 = bf16[1970,512]{1,0:T(8,128)(2,1)S(1)} fusion(bf16[3456,512]{1,0:T(8,128)(2,1)} %bitcast.29, s32[2048]{0:T(1024)S(1)} %pad_clamp_fusion), kind=kCustom, calls=%fused_computation.1 | custom fusion | bytes 4042440 | tf_op jit(solution)/shard_map/gather | solution.py:197
  477.8 8.4 %reduce_sum.274 = f32[985,512]{1,0:T(8,128)} reduce(f32[985,2,512]{2,1,0:T(2,128)} %reshape.309, f32[]{:T(128)} %constant.40.clone.1), dimensions={1}, to_apply=%region_15.16 | reduce | flops 504320 | bytes 6051844 | tf_op jit(solution)/shard_map/reduce_sum | solution.py:203
  503.6 6.7 multiply_reduce_fusion.1
  563.9 38.0 %pmax.7 = f32[8]{0:T(128)S(1)} all-reduce(f32[8]{0:T(128)S(1)} %get-tuple-element.17), channel_id=1, replica_groups=mesh['expert'=8,'fsdp'=4] {'expert','fsdp'}, use_global_device_ids=true, to_apply=%region_58.59 | all-reduce | flops 8 | bytes 64 | tf_op jit(solution)/shard_map/pmax | solution.py:320
  604.4 6.5 multiply_reduce_fusion.7
  615.1 6.4 all-reduce.10
  632.5 21.7 %all-reduce.8 = (bf16[128]{0:T(256)(128)(2,1)S(1)}, bf16[128]{0:T(256)(128)(2,1)S(1)}, bf16[128]{0:T(256)(128)(2,1)S(1)}, bf16[128]{0:T(256)(128)(2,1)S(1)}, bf1...) all-reduce(bf16[128]{0:T(256)(128)(2,1)S(1)} %dynamic-slice.1, ...), channel_id=1, replica_groups=mesh['expert'=8,'fsdp'=4] {'expert'}, use_global_device_ids=true, to_apply=%region_26.27 | all-reduce | flops 1920 | bytes 7680 | tf_op jit(solution)/shard_map/psum | solution.py:295
  658.4 49.8 %all-reduce.13.cloned.1.call-done = (bf16[128,1536]{1,0:T(8,128)(2,1)}, bf16[128,512]{1,0:T(8,128)(2,1)}) async-done(((bf16[128,1536]{1,0:T(8,128)(2,1)}, bf16[128,512]{1,0:T(8,128)(2,1)}), (bf16[128,1536]{1,0:T(8,128)(2,1)}, bf16[128,512]{1,0:T(8,128)(2,1)})) %all-reduce.13.cloned.1.call-update) | async-done | bytes 524304 | tf_op jit(solution)/shard_map/psum | solution.py:297
  (326 shorter events, 202.0 us)
Async XLA Ops:
  7.3 31.0 %copy-start.71 = (bf16[128]{0:T(256)(128)(2,1)S(1)}, bf16[128]{0:T(256)(128)(2,1)}, u32[]{:S(2)}) copy-start(bf16[128]{0:T(256)(128)(2,1)} %param.26) | copy-start | bytes 772
  7.3 36.0 %copy-start.72 = (bf16[128]{0:T(256)(128)(2,1)S(1)}, bf16[128]{0:T(256)(128)(2,1)}, u32[]{:S(2)}) copy-start(bf16[128]{0:T(256)(128)(2,1)} %param.27) | copy-start | bytes 772
  7.3 41.0 %copy-start.44 = (s32[985,2]{0,1:T(2,128)S(1)}, s32[985,2]{0,1:T(2,128)}, u32[]{:S(2)}) copy-start(s32[985,2]{0,1:T(2,128)} %param.33) | copy-start | bytes 23644
  7.3 53.0 %all-gather.11.cloned.1.call-start = ((), (), s32[]{:S(2)}) async-start(), calls=%async_computation.11 | async-start | bytes 1966080 | tf_op jit(solution)/shard_map/all_gather | solution.py:57
  9.5 42.8 %copy-start.46 = (bf16[128,512]{1,0:T(8,128)(2,1)S(1)}, bf16[128,512]{1,0:T(8,128)(2,1)}, u32[]{:S(2)}) copy-start(bf16[128,512]{1,0:T(8,128)(2,1)} %param.24) | copy-start | bytes 393220
  11.0 52.5 %copy-start.4 = (f32[985,512]{1,0:T(8,128)}, f32[985,512]{1,0:T(8,128)S(1)}, u32[]{:S(2)}) copy-start(f32[985,512]{1,0:T(8,128)S(1)} %reshape.278) | copy-start | bytes 6051844
  11.1 52.4 %copy-start.40 = (f32[985]{0:T(1024)}, f32[985]{0:T(1024)S(1)}, u32[]{:S(2)}) copy-start(f32[985]{0:T(1024)S(1)} %div.38) | copy-start | bytes 11824
  11.8 51.7 %copy-start.42 = (f32[985]{0:T(1024)}, f32[985]{0:T(1024)S(1)}, u32[]{:S(2)}) copy-start(f32[985]{0:T(1024)S(1)} %rsqrt.20) | copy-start | bytes 11824
  17.8 45.7 %copy-start.47 = (f32[4,1,128]{2,1,0:T(1,128)}, f32[4,1,128]{2,1,0:T(1,128)S(1)}, u32[]{:S(2)}) copy-start(f32[4,1,128]{2,1,0:T(1,128)S(1)} %convert_element_type.334) | copy-start | bytes 6148
  23.1 40.4 %copy-start.55 = (f32[4,1,128]{2,1,0:T(1,128)}, f32[4,1,128]{2,1,0:T(1,128)S(1)}, u32[]{:S(2)}) copy-start(f32[4,1,128]{2,1,0:T(1,128)S(1)} %convert_element_type.335) | copy-start | bytes 6148
  43.3 114.8 %copy-start.51 = (f32[4,1,128]{2,1,0:T(1,128)}, f32[4,1,128]{2,1,0:T(1,128)S(1)}, u32[]{:S(2)}) copy-start(f32[4,1,128]{2,1,0:T(1,128)S(1)} %convert_element_type.339) | copy-start | bytes 6148
  48.3 109.7 %copy-start.61 = (f32[4,1,128]{2,1,0:T(1,128)}, f32[4,1,128]{2,1,0:T(1,128)S(1)}, u32[]{:S(2)}) copy-start(f32[4,1,128]{2,1,0:T(1,128)S(1)} %convert_element_type.340) | copy-start | bytes 6148
  60.2 101.0 %copy-start.59 = (s32[1970,1]{0,1:T(1,128)}, s32[1970,1]{0,1:T(1,128)S(1)}, u32[]{:S(2)}) copy-start(s32[1970,1]{0,1:T(1,128)S(1)} %compare_select_fusion) | copy-start | bytes 23644
  99.6 58.5 %copy-start.1 = (f32[985,512]{1,0:T(8,128)}, f32[985,512]{1,0:T(8,128)S(1)}, u32[]{:S(2)}) copy-start(f32[985,512]{1,0:T(8,128)S(1)} %get-tuple-element.56) | copy-start | bytes 6051844
  99.6 58.5 %copy-start.36 = (f32[985]{0:T(1024)}, f32[985]{0:T(1024)S(1)}, u32[]{:S(2)}) copy-start(f32[985]{0:T(1024)S(1)} %broadcast_multiply_fusion.6) | copy-start | bytes 11824
  100.0 58.0 %copy-start.38 = (f32[985]{0:T(1024)}, f32[985]{0:T(1024)S(1)}, u32[]{:S(2)}) copy-start(f32[985]{0:T(1024)S(1)} %add_rsqrt_fusion.1) | copy-start | bytes 11824
  121.6 85.7 %all-to-all-start = ((bf16[8,432,512]{2,1,0:T(8,128)(2,1)}), bf16[8,432,512]{2,1,0:T(8,128)(2,1)}, u32[]{:S(2)}, u32[]{:S(2)}) async-start(bf16[8,432,512]{2,1,0:T(8,128)(2,1)} %bitcast.113), calls=%async_computation | async-start | bytes 7077888 | tf_op jit(solution)/shard_map/all_to_all | solution.py:143
  127.6 84.4 %all-gather.13.cloned.1.call-start = ((), (), s32[]{:S(2)}) async-start(), calls=%async_computation.12 | async-start | bytes 2621440 | tf_op jit(solution)/shard_map/all_gather | solution.py:65
  128.3 154.5 %all-gather.15.cloned.1.call-start = ((), (), s32[]{:S(2)}) async-start(), calls=%async_computation.13 | async-start | bytes 2621440 | tf_op jit(solution)/shard_map/all_gather | solution.py:67
  207.3 88.1 %all-to-all-start.2 = ((bf16[8,432,512]{2,1,0:T(8,128)(2,1)}), bf16[8,432,512]{2,1,0:T(8,128)(2,1)}, u32[]{:S(2)}, u32[]{:S(2)}) async-start(bf16[8,432,512]{2,1,0:T(8,128)(2,1)} %bitcast.26), calls=%async_computation.2 | async-start | bytes 7077888 | tf_op jit(solution)/shard_map/all_to_all | solution.py:176
  212.0 70.8 %copy-start.65 = (f32[1,512]{1,0:T(1,128)S(1)}, f32[1,512]{1,0:T(1,128)}, u32[]{:S(2)}) copy-start(f32[1,512]{1,0:T(1,128)} %add.210) | copy-start | bytes 6148
  295.4 84.2 %all-to-all-start.1 = ((bf16[8,432,512]{2,1,0:T(8,128)(2,1)}), bf16[8,432,512]{2,1,0:T(8,128)(2,1)S(1)}, u32[]{:S(2)}, u32[]{:S(2)}) async-start(bf16[8,432,512]{2,1,0:T(8,128)(2,1)} %bitcast.115), calls=%async_computation.1 | async-start | bytes 7077888 | tf_op jit(solution)/shard_map/all_to_all | solution.py:152
  301.4 255.3 %reduce-scatter.26.cloned.1.call-start = ((), (), s32[]{:S(2)}) async-start(), calls=%async_computation.20 | async-start | bytes 163840
  304.8 253.3 %reduce-scatter.24.cloned.1.call-start = ((), (), s32[]{:S(2)}) async-start(), calls=%async_computation.19 | async-start | bytes 655360
  379.6 83.1 %all-to-all-start.3 = ((bf16[8,432,512]{2,1,0:T(8,128)(2,1)}), bf16[8,432,512]{2,1,0:T(8,128)(2,1)}, u32[]{:S(2)}, u32[]{:S(2)}) async-start(bf16[8,432,512]{2,1,0:T(8,128)(2,1)} %bitcast.114), calls=%async_computation.3 | async-start | bytes 7077888 | tf_op jit(solution)/shard_map/all_to_all | solution.py:195
  384.1 175.5 %reduce-scatter.20.cloned.1.call-start = ((), (), s32[]{:S(2)}) async-start(), calls=%async_computation.17 | async-start | bytes 2621440 | tf_op jit(solution)/shard_map/reduce_scatter | solution.py:313
  397.2 164.6 %reduce-scatter.18.cloned.1.call-start = ((), (), s32[]{:S(2)}) async-start(), calls=%async_computation.16 | async-start | bytes 2621440 | tf_op jit(solution)/shard_map/reduce_scatter | solution.py:307
  410.7 204.2 %reduce-scatter.16.cloned.1.call-start = ((), (), s32[]{:S(2)}) async-start(), calls=%async_computation.15 | async-start | bytes 655360 | tf_op jit(solution)/shard_map/reduce_scatter | solution.py:278
  520.5 94.3 %reduce-scatter.14.cloned.1.call-start = ((), (), s32[]{:S(2)}) async-start(), calls=%async_computation.14 | async-start | bytes 1966080 | tf_op jit(solution)/shard_map/reduce_scatter | solution.py:269
  555.3 46.7 %copy-start.62 = (f32[4,1,128]{2,1,0:T(1,128)S(1)}, f32[4,1,128]{2,1,0:T(1,128)}, u32[]{:S(2)}) copy-start(f32[4,1,128]{2,1,0:T(1,128)} %copy-done.61) | copy-start | bytes 6148
  555.3 76.4 %reduce-scatter.22.cloned.1.call-start = ((), (), s32[]{:S(2)}) async-start(), calls=%async_computation.18 | async-start | bytes 163840
  610.9 97.3 %all-reduce.13.cloned.1.call-start = ((), (), s32[]{:S(2)}) async-start(), calls=%async_computation.21 | async-start | bytes 1048576 | tf_op jit(solution)/shard_map/psum | solution.py:297
  (61 other events, 489.8 us)
Sparse Core Ops, SparseCore 0:
  9.7 22.3 all-gather.10
  130.0 24.0 all-gather.12
  155.6 22.5 all-gather.14
  304.9 21.0 reduce-scatter.25
  338.2 23.0 reduce-scatter.23
  397.3 32.7 reduce-scatter.19
  432.8 31.4 reduce-scatter.17
  520.6 20.7 reduce-scatter.15
  555.4 27.4 reduce-scatter.13
  611.0 20.5 reduce-scatter.21
  635.5 72.6 all-reduce.12
where the time goes:
time: 726 us; the launch traced here: 719 us
  matrix products  204 us (28%)
  local copies, waits for them, and re-layouts  138 us (19%)
  waiting for transfers between devices  136 us (19%)
  blocking collectives  126 us (17%)
  other arithmetic  76 us (10%)
  starting transfers between devices  22.2 us (3%)
  between operations  16.1 us (2%)
    dot_general x1, matrix products, shards(): jnp.dot(flat_in, first_weight, preferred_element_type=jnp.float32)  70.8 us
    psum x1, waiting for transfers between devices, shards(): lax.psum(shares[2].astype(jnp.bfloat16), 'expert').astype(jnp.float32)  49.8 us
    pmax x1, blocking collectives, shards(): peak_logit = lax.pmax(head_peak, ('expert', 'fsdp'))  38 us
    dot_general x1, matrix products, shards(): jnp.einsum('rd,hd->rh', flat_grad, second_weight, preferred_element_type=...  31.9 us
    all_to_all x1, waiting for transfers between devices, shards(): lax.all_to_all(produced, 'expert', split_axis=0, concat_axis=0, tiled=True)  28.8 us
    all_to_all x1, waiting for transfers between devices, shards(): lax.all_to_all(outgoing, 'expert', split_axis=0, concat_axis=0, tiled=True)  27.6 us
    all_to_all x1, waiting for transfers between devices, shards(): lax.all_to_all(row_grad, 'expert', split_axis=0, concat_axis=0, tiled=True)  23.3 us
    psum x1, blocking collectives, shards(): lax.psum(shares[0].astype(jnp.bfloat16), 'expert').astype(jnp.float32)  21.7 us
  transfers between devices with their start and end apart: 15, of which 5 were waited for; matrix products, arithmetic and copies ran while one was open for 49% of the time, Pallas kernels for 0%

commit v1 on v0

v1 whole, which is shorter than its diff:
```python
import functools

import jax
import jax.numpy as jnp
from jax import lax
from jax.experimental import pallas as pl
from jax.experimental.pallas import tpu as pltpu
from jax.sharding import Mesh
from jax.sharding import PartitionSpec as P

HEADS = 8
EPS = 1e-06
LANES = 128
VEC = 64
TAIL = 16
NEG = -1e30
f32 = jnp.float32
bf16 = jnp.bfloat16
i32 = jnp.int32
NN = (((1,), (0,)), ((), ()))
NT = (((1,), (1,)), ((), ()))
TN = (((0,), (0,)), ((), ()))
DEVICE = ("hi", "lo", "fy", "core")
GROUP = ("lo", "core")
VMEM_LIMIT = 58 << 20


def dot(a, b, dims):
    return lax.dot_general(a, b, dims, preferred_element_type=f32)


def pieces(value, count):
    parts = []
    for _ in range(count):
        part = value.astype(bf16)
        parts.append(part)
        value = value - part.astype(f32)
    return parts


def iota(shape, axis):
    return lax.broadcasted_iota(i32, shape, axis)


def relative_expert(place, shift, experts):
    other = jnp.bitwise_xor(place, shift)
    return (other & 1) * (experts // 2) + (other >> 1)


def router_order(place, experts):
    row, col = iota((LANES, LANES), 0), iota((LANES, LANES), 1)
    return jnp.where((row == relative_expert(place, col, experts)) & (col < experts), 1.0, 0.0).astype(bf16)


def norm_stats(matrix):
    centred = matrix - jnp.mean(matrix, axis=1, keepdims=True)
    inverse = lax.rsqrt(jnp.mean(centred * centred, axis=1, keepdims=True) + EPS)
    return centred * inverse, inverse


def norm_back(upstream, gain, hat, inverse):
    scaled = upstream * gain
    spread = (
        scaled
        - jnp.mean(scaled, axis=1, keepdims=True)
        - hat * jnp.mean(scaled * hat, axis=1, keepdims=True)
    )
    return spread * inverse


def softmax_lanes(logits, experts):
    logits = jnp.where(iota(logits.shape, 1) < experts, logits, NEG)
    top = jnp.max(logits, axis=1, keepdims=True)
    weight = jnp.exp(logits - top)
    return weight / jnp.sum(weight, axis=1, keepdims=True)


def gelu_pair(value):
    bell = jnp.exp(value * value * -0.5)
    t = 1.0 / (1.0 + jnp.abs(value) * (0.3275911 * 0.7071067811865476))
    poly = t * (
        0.127414796 + t * (-0.142248368 + t * (0.7107068705 + t * (-0.7265760135 + t * 0.5307027145)))
    )
    lower = poly * bell
    phi = jnp.where(value >= 0, 1.0 - lower, lower)
    return value * phi, phi + value * (bell * 0.3989422804014327)


def whole(shape):
    return pl.BlockSpec(shape, lambda *_: (0,) * len(shape))


def params(**extra):
    return pltpu.CompilerParams(vmem_limit_bytes=VMEM_LIMIT, **extra)


def cost(flops, moved, trans=0):
    return pl.CostEstimate(flops=int(flops), bytes_accessed=int(moved), transcendentals=int(trans))


def pack_kernel(spot_ref, wqkv, wout, router, *rest):
    vectors, (w2, b1, b2, pack_ref, w2_ref, spread, tail) = rest[:-7], rest[-7:]
    part, wide = wqkv.shape
    width, hidden = wout.shape[1], w2.shape[0]
    pack_ref[:, 0:wide] = wqkv[...]
    pack_ref[:, wide : wide + width] = wout[...]
    spread[...] = jnp.zeros_like(spread)
    for index, ref in enumerate(vectors):
        spread[VEC + index : VEC + index + 1, :] = ref[...].astype(f32)
    columns = spread[...].T
    pack_ref[:, wide + width :] = columns.astype(bf16)
    pack_ref[:, wide + width : wide + width + router.shape[1]] = router[...]
    w2_ref[0:hidden] = w2[...]
    tail[...] = jnp.zeros_like(tail)
    tail[0:1, 0 : b1.shape[1]] = b1[...].astype(f32)
    copies = jnp.concatenate([b2[...].astype(f32)] * (width // part), axis=1)
    tail[1:2] = jnp.where(iota((1, width), 1) // part == spot_ref[0], copies, 0.0)
    w2_ref[hidden : hidden + TAIL] = tail[...].astype(bf16)


def pack_parameters(spot, w_qkv, w_out, w_router, vectors, w2, b1, b2):
    part, width = w_out.shape
    hidden = w2.shape[0]
    operands = [w_qkv, w_out, w_router, *[v.reshape(1, part) for v in vectors], w2, b1, b2]
    return pl.pallas_call(
        pack_kernel,
        grid=(1,),
        in_specs=[pl.BlockSpec(memory_space=pltpu.SMEM)] + [whole(v.shape) for v in operands],
        out_specs=[whole((part, 4 * width + LANES)), whole((hidden + TAIL, width))],
        out_shape=[
            jax.ShapeDtypeStruct((part, 4 * width + LANES), bf16),
            jax.ShapeDtypeStruct((hidden + TAIL, width), bf16),
        ],
        scratch_shapes=[pltpu.VMEM((LANES, part), f32), pltpu.VMEM((TAIL, width), f32)],
        compiler_params=params(),
        cost_estimate=cost(1 << 20, 3 << 20),
        name="pack",
    )(spot, *operands)


def one_hot_rows(row, cap):
    slots = iota((cap, row.shape[1]), 0).astype(f32)
    return jnp.where(slots == row, 1.0, 0.0).astype(bf16)


def one_hot_cols(column, cap):
    slots = iota((column.shape[0], cap), 1).astype(f32)
    return jnp.where(slots == column, 1.0, 0.0).astype(bf16)


def route_kernel(place_ref, ids_ref, up_ref, post_ref, pos_ref, *rest, cap, stride):
    outs, gathered = rest[:-1], rest[-1]
    experts = len(outs)
    images, seq, width = up_ref.shape
    step = pl.program_id(0)

    @pl.when(step == 0)
    def _():
        expert = relative_expert(place_ref[0], iota((experts, stride), 0), experts)
        before = jnp.where(iota((stride, stride), 0) < iota((stride, stride), 1), 1.0, 0.0).astype(bf16)
        carry = jnp.zeros((experts, 1), f32)
        gathered[...] = jnp.zeros_like(gathered)
        for image in range(images):
            ids = ids_ref[:, image * stride : (image + 1) * stride]
            hit = jnp.zeros((experts, stride), jnp.bool_)
            for choice in range(ids_ref.shape[0]):
                hit = hit | (ids[choice : choice + 1] == expert)
            mask = jnp.where(hit, 1.0, 0.0)
            rank = carry + dot(mask.astype(bf16), before, NN)
            carry = carry + jnp.sum(mask, axis=1, keepdims=True)
            slot = jnp.where(hit, rank, -1.0)
            post_ref[:, image * stride : (image + 1) * stride] = slot
            padded = jnp.concatenate([slot, jnp.full((LANES - experts, stride), -1.0, f32)], axis=0)
            pos_ref[image] = padded.T
            gathered[image * stride : image * stride + seq] = up_ref[image]

    hot = one_hot_rows(post_ref[pl.ds(step, 1), :], cap)
    rows = dot(hot, gathered[...], NN).astype(bf16)
    for index in range(experts):

        @pl.when(step == index)
        def _():
            outs[index][...] = rows


def route(place, ids, grad_output, experts, cap, stride):
    images, seq, width = grad_output.shape
    total = images * stride
    return pl.pallas_call(
        functools.partial(route_kernel, cap=cap, stride=stride),
        grid=(experts,),
        in_specs=[
            pl.BlockSpec(memory_space=pltpu.SMEM),
            whole(ids.shape),
            whole(grad_output.shape),
        ],
        out_specs=[whole((experts, total)), whole((images, stride, LANES))] + [whole((cap, width))] * experts,
        out_shape=[
            jax.ShapeDtypeStruct((experts, total), f32),
            jax.ShapeDtypeStruct((images, stride, LANES), f32),
        ]
        + [jax.ShapeDtypeStruct((cap, width), bf16)] * experts,
        scratch_shapes=[pltpu.VMEM((total, width), bf16)],
        compiler_params=params(),
        cost_estimate=cost(2 * experts * cap * total * width, 8 << 20),
        name="route",
    )(place, ids, grad_output)


def forward_kernel(
    place_ref,
    tok_ref,
    wqkv_ref,
    wout_ref,
    misc_ref,
    post_ref,
    *rest,
    cap,
    stride,
    experts,
):
    qkv_ref, mixed_ref, hidden_ref, prob_ref, lse_ref, peak_ref = rest[-10 - experts : -4 - experts]
    outs, (tokens, vectors, router, gathered) = rest[-4 - experts : -4], rest[-4:]
    _, seq, width = tok_ref.shape
    rows = tokens.shape[0]
    head = width // HEADS
    step = pl.program_id(0)
    images = pl.num_programs(0) - experts

    @pl.when(step == 0)
    def _():
        vectors[...] = misc_ref[...].astype(f32).T
        router[...] = dot(misc_ref[...], router_order(place_ref[0], experts), NN).astype(bf16)
        gathered[...] = jnp.zeros_like(gathered)
        tokens[...] = jnp.zeros_like(tokens)
        peak_ref[...] = jnp.full_like(peak_ref, NEG)

    @pl.when(step < images)
    def _():
        def vector(index):
            return vectors[VEC + index : VEC + index + 1, :]

        tokens[0:seq] = tok_ref[0].astype(f32)
        residual = tokens[...]
        hat, _ = norm_stats(residual)
        normed = (hat * vector(0) + vector(1)).astype(bf16)
        projected = dot(normed, wqkv_ref[...], NN)
        qkv_ref[0, :, 0:width] = ((projected[:, 0:width] + vector(2)).astype(bf16).astype(f32) * head**-0.5).astype(
            bf16
        )
        qkv_ref[0, :, width : 2 * width] = projected[:, width : 2 * width].astype(bf16)
        qkv_ref[0, :, 2 * width :] = (projected[:, 2 * width :] + vector(3)).astype(bf16)
        lane = iota((1, LANES), 1)
        first = lane < head
        halves = (jnp.where(first, 1.0, 0.0).astype(bf16), jnp.where(first, 0.0, 1.0).astype(bf16))
        keys = jnp.where(iota((1, rows), 1) < seq, 0.0, NEG)
        valid = iota((rows, 1), 0) < seq

        def pair(index, carry):
            lse, peak = carry
            at = pl.multiple_of(index * LANES, LANES)
            query = qkv_ref[0, :, pl.ds(at, LANES)]
            key = qkv_ref[0, :, pl.ds(width + at, LANES)]
            value = qkv_ref[0, :, pl.ds(2 * width + at, LANES)]
            parts = []
            for half in range(2):
                scores = dot(query * halves[half], key, NT) + keys
                top = jnp.max(scores, axis=1, keepdims=True)
                weight = jnp.exp(scores - top)
                total = jnp.sum(weight, axis=1, keepdims=True)
                number = index * 2 + half
                lse = jnp.where(lane == number, top + jnp.log(total), lse)
                largest = jnp.max(jnp.where(valid, top, NEG), axis=0, keepdims=True)
                peak = jnp.where(lane == number, largest, peak)
                parts.append(dot(weight.astype(bf16), value, NN) * (1.0 / total))
            mixed_ref[0, :, pl.ds(at, LANES)] = jnp.where(first, parts[0], parts[1]).astype(bf16)
            return lse, peak

        lse, peak = lax.fori_loop(
            0, HEADS // 2, pair, (jnp.zeros((rows, LANES), f32), jnp.full((1, LANES), NEG, f32))
        )
        lse_ref[0] = lse
        peak_ref[...] = jnp.maximum(peak_ref[...], peak)
        hidden = residual + dot(mixed_ref[0], wout_ref[...], NN) + vector(4)
        hidden_ref[0] = hidden
        hat, _ = norm_stats(hidden)
        mid = hat * vector(5) + vector(6)
        logits = jnp.zeros((rows, LANES), f32)
        for part in pieces(mid, 3):
            logits = logits + dot(part, router[...], NN)
        prob_ref[0] = softmax_lanes(logits, experts)
        gathered[pl.ds(pl.multiple_of(step * stride, stride), rows)] = mid.astype(bf16)

    @pl.when(step >= images)
    def _():
        hot = one_hot_rows(post_ref[pl.ds(step - images, 1), :], cap)
        sent = dot(hot, gathered[...], NN).astype(bf16)
        for index in range(experts):

            @pl.when(step == images + index)
            def _():
                outs[index][...] = sent


def forward(place, tokens, pack, post, after, experts, cap, stride, rows):
    images, seq, width = tokens.shape
    total = images * stride

    def image(shape):
        return pl.BlockSpec((1,) + shape, lambda i: (jnp.minimum(i, images - 1), 0, 0))

    def struct(shape, kind):
        return jax.ShapeDtypeStruct((images,) + shape, kind)

    return pl.pallas_call(
        functools.partial(forward_kernel, cap=cap, stride=stride, experts=experts),
        grid=(images + experts,),
        in_specs=[
            pl.BlockSpec(memory_space=pltpu.SMEM),
            image((seq, width)),
            pl.BlockSpec((width, 3 * width), lambda i: (0, 0)),
            pl.BlockSpec((width, width), lambda i: (0, 3)),
            pl.BlockSpec((width, LANES), lambda i: (0, 4 * width // LANES)),
            whole(post.shape),
        ]
        + [pl.BlockSpec(memory_space=pl.ANY)] * len(after),
        out_specs=[
            image((rows, 3 * width)),
            image((rows, width)),
            image((rows, width)),
            image((rows, LANES)),
            image((rows, LANES)),
            whole((1, LANES)),
        ]
        + [whole((cap, width))] * experts,
        out_shape=[
            struct((rows, 3 * width), bf16),
            struct((rows, width), bf16),
            struct((rows, width), f32),
            struct((rows, LANES), f32),
            struct((rows, LANES), f32),
            jax.ShapeDtypeStruct((1, LANES), f32),
        ]
        + [jax.ShapeDtypeStruct((cap, width), bf16)] * experts,
        scratch_shapes=[
            pltpu.VMEM((rows, width), f32),
            pltpu.VMEM((LANES, width), f32),
            pltpu.VMEM((width, LANES), bf16),
            pltpu.VMEM((total, width), bf16),
        ],
        compiler_params=params(),
        cost_estimate=cost(2 * images * rows * width * 5 * width + 2 * experts * cap * total * width, 16 << 20),
        name="attend",
    )(place, tokens, pack, pack, pack, post, *after)


def expert_kernel(place_ref, *refs, cap, count, first, last, experts):
    taken = iter(refs)

    def take(number):
        return [next(taken) for _ in range(number)]

    rows_in, ups_in = take(count), take(count)
    w1, w2, b1, b2, misc = take(5)
    old = [] if first else take(2)
    row_back, gated = take(count), take(count)
    grad1, grad2 = take(2)
    rows, ups, gates, acc_row, acc_out, shift2, bias2 = take(7)
    step = pl.program_id(0)
    width = rows.shape[1]
    tile = w1.shape[1]

    @pl.when(step == 0)
    def _():
        for index in range(count):
            rows[index * cap : (index + 1) * cap] = rows_in[index][...]
        router = dot(misc[...], router_order(place_ref[0], experts), NN).astype(bf16)
        gate = softmax_lanes(dot(rows[...], router, NN), experts)[:, 0:1]
        gates[...] = jnp.broadcast_to(gate, gates.shape)
        for index in range(count):
            part = slice(index * cap, (index + 1) * cap)
            ups[part] = (ups_in[index][...].astype(f32) * gate[part]).astype(bf16)
        acc_row[...] = jnp.zeros_like(acc_row)
        acc_out[...] = jnp.zeros_like(acc_out)
        bias2[...] = jnp.zeros_like(bias2)
        shift2[...] = jnp.sum(ups[...].astype(f32), axis=0, keepdims=True)

    tail = b1[0].astype(f32)
    bias2[...] += tail[1:2]
    x, up = rows[...], ups[...]
    value, slope = gelu_pair(dot(x, w1[...], NN) + tail[0:1, 0:tile])
    act = value.astype(bf16)
    acc_out[...] += dot(act, w2[0], NN)
    raw = slope * dot(up, w2[0], NT)
    pre = raw.astype(bf16)
    acc_row[...] += dot(pre, w1[...], NT)
    part1 = dot(x, pre, TN)
    part2 = dot(act, up, TN)
    shift1 = jnp.sum(pre.astype(f32), axis=0, keepdims=True)
    if tile < width:
        shift1 = jnp.concatenate([shift1, jnp.zeros((1, width - tile), f32)], axis=1)
    place = iota((TAIL, width), 0)
    sums = jnp.where(place == 0, shift1, jnp.where(place == 1, shift2[...], 0.0))
    if not first:
        part1, part2, sums = old[0][...] + part1, old[1][0, 0:tile] + part2, old[1][0, tile:] + sums
    grad1[...] = part1.astype(grad1.dtype)
    grad2[0, 0:tile] = part2.astype(grad2.dtype)
    grad2[0, tile:] = sums.astype(grad2.dtype)

    @pl.when(step == pl.num_programs(0) - 1)
    def _():
        for index in range(count):
            part = slice(index * cap, (index + 1) * cap)
            made = acc_out[part] + bias2[...]
            gate = gates[part, 0:1]
            gated[index][...] = (made * gate).astype(bf16)
            row_back[index][0:cap] = acc_row[part].astype(bf16)
            effect = jnp.sum(made * ups_in[index][...].astype(f32), axis=1, keepdims=True) * gate
            effect = jnp.concatenate([effect, jnp.zeros((width - cap, 1), f32)], axis=0)
            line = jnp.broadcast_to(effect, (width, LANES)).T[0:1]
            end = jnp.zeros((TAIL, width), f32)
            for order, piece in enumerate(pieces(line, 3)):
                end = jnp.where(place == order, piece.astype(f32), end)
            row_back[index][cap : cap + TAIL] = end.astype(bf16)


def expert_call(place, rows, ups, weights, pack, old, cap, experts, last):
    count = len(rows)
    first = old is None
    w1, w2 = weights
    width, hidden = w1.shape
    shards_of, tall, _ = w2.shape
    tile = tall - TAIL
    total = count * cap
    kept = bf16 if last else f32
    column = pl.BlockSpec((width, tile), lambda h: (0, h))
    line = pl.BlockSpec((1, tall, width), lambda h: (h, 0, 0))
    unused = pl.BlockSpec((1, TAIL, width), lambda h: (h, tile // TAIL, 0))
    grads = [column, line]
    operands = [place, *rows, *ups, w1, w2, w2, w2, pack] + ([] if first else list(old))
    return pl.pallas_call(
        functools.partial(expert_kernel, cap=cap, count=count, first=first, last=last, experts=experts),
        grid=(shards_of,),
        in_specs=[pl.BlockSpec(memory_space=pltpu.SMEM)]
        + [whole((cap, width))] * (2 * count)
        + [
            column,
            pl.BlockSpec((1, tile, width), lambda h: (h, 0, 0)),
            unused,
            unused,
            pl.BlockSpec((width, LANES), lambda h: (0, 4 * width // LANES)),
        ]
        + ([] if first else grads),
        out_specs=[whole((cap + TAIL, width))] * count + [whole((cap, width))] * count + grads,
        out_shape=[jax.ShapeDtypeStruct((cap + TAIL, width), bf16)] * count
        + [jax.ShapeDtypeStruct((cap, width), bf16)] * count
        + [
            jax.ShapeDtypeStruct((width, hidden), kept),
            jax.ShapeDtypeStruct((shards_of, tall, width), kept),
        ],
        scratch_shapes=[pltpu.VMEM((total, width), bf16)] * 2
        + [pltpu.VMEM((total, LANES), f32)]
        + [pltpu.VMEM((total, width), f32)] * 2
        + [pltpu.VMEM((1, width), f32)] * 2,
        compiler_params=params(),
        cost_estimate=cost(12 * total * width * hidden, 24 << 20),
        name="expert",
    )(*operands)


def middle_kernel(
    place_ref, up_ref, wout_ref, misc_ref, pos_ref, mixed_ref, hidden_ref, prob_ref, *rest, cap, experts
):
    backs = rest[:experts]
    hidden_grad_ref, mixed_grad_ref, sums_ref, padded, vectors, router, shifts, acc_out, acc_router = rest[-9:]
    _, seq, width = up_ref.shape
    rows = padded.shape[0]
    step = pl.program_id(0)

    @pl.when(step == 0)
    def _():
        vectors[...] = misc_ref[...].astype(f32).T
        router[...] = dot(misc_ref[...], router_order(place_ref[0], experts), NN).astype(bf16)
        padded[...] = jnp.zeros_like(padded)
        shifts[...] = jnp.zeros_like(shifts)
        acc_out[...] = jnp.zeros_like(acc_out)
        acc_router[...] = jnp.zeros_like(acc_router)

    def vector(index):
        return vectors[VEC + index : VEC + index + 1, :]

    def shift(index, value):
        shifts[index : index + 1, :] += jnp.sum(value, axis=0, keepdims=True)

    lane = iota((1, LANES), 1)
    places = pos_ref[0, 0:rows, :]
    slot_sum = jnp.zeros((rows, width), f32)
    effect = jnp.zeros((rows, LANES), f32)
    for index in range(experts):
        hot = one_hot_cols(places[:, index : index + 1], cap)
        slot_sum = slot_sum + dot(hot, backs[index][0:cap], NN)
        parts = dot(hot, backs[index][cap : cap + TAIL, 0:cap], NT)
        effect = jnp.where(lane == index, jnp.sum(parts, axis=1, keepdims=True), effect)
    prob = prob_ref[0]
    logit_grad = effect - prob * jnp.sum(effect, axis=1, keepdims=True)
    logit_parts = pieces(logit_grad, 2)
    mid_grad = slot_sum
    for part in logit_parts:
        mid_grad = mid_grad + dot(part, router[...], NT)
    padded[0:seq] = up_ref[0].astype(f32)
    hat, inverse = norm_stats(hidden_ref[0])
    mid_parts = pieces(hat * vector(5) + vector(6), 2)
    acc_router[...] += (
        dot(logit_parts[0], mid_parts[0], TN)
        + dot(logit_parts[0], mid_parts[1], TN)
        + dot(logit_parts[1], mid_parts[0], TN)
    )
    shift(5, mid_grad * hat)
    shift(6, mid_grad)
    hidden_grad = padded[...] + norm_back(mid_grad, vector(5), hat, inverse)
    hidden_grad_ref[0] = hidden_grad
    branch = hidden_grad.astype(bf16)
    shift(4, branch.astype(f32))
    acc_out[...] += dot(mixed_ref[0], branch, TN)
    mixed_grad_ref[0] = dot(branch, wout_ref[...], NT).astype(bf16)

    @pl.when(step == pl.num_programs(0) - 1)
    def _():
        sums_ref[:, 0:width] = acc_out[...]
        ordered = dot(router_order(place_ref[0], experts), acc_router[...].astype(bf16), NN)
        spare = jnp.concatenate(
            [ordered[0:VEC], shifts[...], jnp.zeros((LANES - VEC - shifts.shape[0], width), f32)], axis=0
        )
        sums_ref[:, width:] = spare.T


def middle(place, grad_output, pack, pos, saved, backs, cap, experts):
    images, seq, width = grad_output.shape
    _, mixed, hidden, prob, _ = saved
    rows = mixed.shape[1]

    def image(shape):
        return pl.BlockSpec((1,) + shape, lambda i: (i, 0, 0))

    return pl.pallas_call(
        functools.partial(middle_kernel, cap=cap, experts=experts),
        grid=(images,),
        in_specs=[
            pl.BlockSpec(memory_space=pltpu.SMEM),
            image((seq, width)),
            pl.BlockSpec((width, width), lambda i: (0, 3)),
            pl.BlockSpec((width, LANES), lambda i: (0, 4 * width // LANES)),
            image((pos.shape[1], LANES)),
            image((rows, width)),
            image((rows, width)),
            image((rows, LANES)),
        ]
        + [whole((cap + TAIL, width))] * experts,
        out_specs=[image((rows, width)), image((rows, width)), whole((width, width + LANES))],
        out_shape=[
            jax.ShapeDtypeStruct((images, rows, width), f32),
            jax.ShapeDtypeStruct((images, rows, width), bf16),
            jax.ShapeDtypeStruct((width, width + LANES), f32),
        ],
        scratch_shapes=[
            pltpu.VMEM((rows, width), f32),
            pltpu.VMEM((LANES, width), f32),
            pltpu.VMEM((width, LANES), bf16),
            pltpu.VMEM((8, width), f32),
            pltpu.VMEM((width, width), f32),
            pltpu.VMEM((LANES, width), f32),
        ],
        compiler_params=params(),
        cost_estimate=cost(2 * images * rows * width * (2 * width + experts * cap), 16 << 20),
        name="middle",
    )(place, grad_output, pack, pack, pos, mixed, hidden, prob, *backs)


def backward_kernel(
    spots_ref, tok_ref, qkv_ref, lse_ref, mixed_grad_ref, sums_ref, peak_ref, *rest, head_rows, members
):
    qkv_grad_ref, keep_ref, give_ref, padded, acc_qkv, columns, spare, misc = rest[-8:]
    _, seq, width = tok_ref.shape
    rows = padded.shape[0]
    head = width // HEADS
    wide = 3 * width
    step = pl.program_id(0)
    part = keep_ref.shape[1]

    @pl.when(step == 0)
    def _():
        padded[...] = jnp.zeros_like(padded)
        acc_qkv[...] = jnp.zeros_like(acc_qkv)
        columns[...] = jnp.zeros_like(columns)

    lane = iota((1, LANES), 1)
    first = lane < head
    halves = (jnp.where(first, 1.0, 0.0).astype(bf16), jnp.where(first, 0.0, 1.0).astype(bf16))
    keys = jnp.where(iota((1, rows), 1) < seq, 0.0, NEG)
    lse = lse_ref[0]

    def pair(index, carry):
        at = pl.multiple_of(index * LANES, LANES)
        query = qkv_ref[0, :, pl.ds(at, LANES)]
        key = qkv_ref[0, :, pl.ds(width + at, LANES)]
        value = qkv_ref[0, :, pl.ds(2 * width + at, LANES)]
        up = mixed_grad_ref[0, :, pl.ds(at, LANES)]
        made = []
        for half in range(2):
            total = jnp.sum(jnp.where(lane == index * 2 + half, lse, 0.0), axis=1, keepdims=True)
            weight = jnp.exp(dot(query * halves[half], key, NT) + keys - total)
            value_grad = dot(weight.astype(bf16), up, TN)
            spread = weight * dot(up * halves[half], value, NT)
            score_grad = (spread - weight * jnp.sum(spread, axis=1, keepdims=True)).astype(bf16)
            made.append((dot(score_grad, key, NN) * head**-0.5, dot(score_grad, query, TN), value_grad))
        for index_of, (left, right) in enumerate(zip(*made)):
            qkv_grad_ref[0, :, pl.ds(index_of * width + at, LANES)] = jnp.where(first, left, right).astype(bf16)
        return carry

    lax.fori_loop(0, HEADS // 2, pair, 0)
    columns[...] += jnp.sum(qkv_grad_ref[0].astype(f32), axis=0, keepdims=True)
    padded[0:seq] = tok_ref[0].astype(f32)
    hat, _ = norm_stats(padded[...])
    acc_qkv[...] += dot(hat.astype(bf16), qkv_grad_ref[0], TN)

    @pl.when(step == pl.num_programs(0) - 1)
    def _():
        line = iota((LANES, width), 0)
        flat = columns[...]
        grown = jnp.where(line == VEC + 2, flat[:, 0:width], 0.0)
        grown = jnp.where(line == VEC + 3, flat[:, 2 * width :], grown)
        misc[...] = sums_ref[:, width:] + grown.T
        spare[...] = jnp.zeros_like(spare)
        number = wide // LANES
        for order, piece in enumerate(pieces(flat, 3)):
            value = piece.astype(f32)
            for index in range(number):
                at = order * number + index
                spare[at : at + 1, :] = value[:, index * LANES : (index + 1) * LANES]
        if members:
            top = jnp.where(lane < HEADS, peak_ref[...], 0.0)
            rows_of = jnp.zeros((TAIL, LANES), f32)
            for order, piece in enumerate(pieces(jnp.broadcast_to(top, (TAIL, LANES)), 3)):
                move = jnp.where(iota((LANES, LANES), 1) == iota((LANES, LANES), 0) + order * HEADS, 1.0, 0.0)
                rows_of = rows_of + dot(piece, move.astype(bf16), NN)
            spare[pl.ds(head_rows + spots_ref[1], 1), :] = rows_of[0:1]
        extra = spare[...].astype(bf16)
        for fy in range(keep_ref.shape[0]):
            for ref, core in ((keep_ref, spots_ref[0]), (give_ref, 1 - spots_ref[0])):
                at = pl.multiple_of((2 * fy + core) * part, part)
                ref[fy, :, 0:wide] = acc_qkv[pl.ds(at, part), :].astype(bf16)
                ref[fy, :, wide : wide + width] = sums_ref[pl.ds(at, part), 0:width].astype(bf16)
                ref[fy, :, wide + width : wide + width + LANES] = misc[pl.ds(at, part), :].astype(bf16)
                ref[fy, :, wide + width + LANES :] = extra


def backward(spots, tokens, saved, mixed_grad, sums, peak, after, ways, part, head_rows, members):
    images, seq, width = tokens.shape
    qkv, _, _, _, lse = saved
    rows = qkv.shape[1]
    wide = 4 * width + 2 * LANES

    def image(shape):
        return pl.BlockSpec((1,) + shape, lambda i: (i, 0, 0))

    return pl.pallas_call(
        functools.partial(backward_kernel, head_rows=head_rows, members=members),
        grid=(images,),
        in_specs=[
            pl.BlockSpec(memory_space=pltpu.SMEM),
            image((seq, width)),
            image((rows, 3 * width)),
            image((rows, LANES)),
            image((rows, width)),
            whole(sums.shape),
            whole(peak.shape),
        ]
        + [pl.BlockSpec(memory_space=pl.ANY)] * len(after),
        out_specs=[image((rows, 3 * width)), whole((ways, part, wide)), whole((ways, part, wide))],
        out_shape=[
            jax.ShapeDtypeStruct((images, rows, 3 * width), bf16),
            jax.ShapeDtypeStruct((ways, part, wide), bf16),
            jax.ShapeDtypeStruct((ways, part, wide), bf16),
        ],
        scratch_shapes=[
            pltpu.VMEM((rows, width), f32),
            pltpu.VMEM((width, 3 * width), f32),
            pltpu.VMEM((1, 3 * width), f32),
            pltpu.VMEM((part, LANES), f32),
            pltpu.VMEM((width, LANES), f32),
        ],
        compiler_params=params(),
        cost_estimate=cost(2 * images * rows * width * 8 * width, 24 << 20),
        name="attend_back",
    )(spots, tokens, qkv, lse, mixed_grad, sums, peak, *after)


def first_kernel(tok_ref, qkv_grad_ref, wqkv_ref, misc_ref, hidden_grad_ref, grad_ref, padded, gain):
    _, seq, width = tok_ref.shape

    @pl.when(pl.program_id(0) == 0)
    def _():
        gain[...] = misc_ref[...].astype(f32).T[VEC : VEC + 1]
        padded[...] = jnp.zeros_like(padded)

    in_grad = dot(qkv_grad_ref[0], wqkv_ref[...], NT)
    padded[0:seq] = tok_ref[0].astype(f32)
    hat, inverse = norm_stats(padded[...])
    grad_ref[0] = (hidden_grad_ref[0] + norm_back(in_grad, gain[...], hat, inverse))[0:seq]


def first_norm(tokens, qkv_grad, pack, hidden_grad):
    images, seq, width = tokens.shape
    rows = qkv_grad.shape[1]

    def image(shape):
        return pl.BlockSpec((1,) + shape, lambda i: (i, 0, 0))

    return pl.pallas_call(
        first_kernel,
        grid=(images,),
        in_specs=[
            image((seq, width)),
            image((rows, 3 * width)),
            pl.BlockSpec((width, 3 * width), lambda i: (0, 0)),
            pl.BlockSpec((width, LANES), lambda i: (0, 4 * width // LANES)),
            image((rows, width)),
        ],
        out_specs=image((seq, width)),
        out_shape=jax.ShapeDtypeStruct((images, seq, width), f32),
        scratch_shapes=[pltpu.VMEM((rows, width), f32), pltpu.VMEM((1, width), f32)],
        compiler_params=params(),
        cost_estimate=cost(2 * images * rows * width * 3 * width, 12 << 20),
        name="first_norm",
    )(tokens, qkv_grad, pack, pack, hidden_grad)


def output_kernel(pos_ref, hidden_ref, *rest, cap):
    made, out_ref = rest[:-1], rest[-1]
    seq = out_ref.shape[1]
    total = hidden_ref[0]
    places = pos_ref[0, 0 : total.shape[0], :]
    for index, ref in enumerate(made):
        total = total + dot(one_hot_cols(places[:, index : index + 1], cap), ref[...], NN)
    out_ref[0] = total[0:seq].astype(bf16)


def combine_output(pos, hidden, made, cap, seq):
    images, rows, width = hidden.shape

    def image(shape):
        return pl.BlockSpec((1,) + shape, lambda i: (i, 0, 0))

    return pl.pallas_call(
        functools.partial(output_kernel, cap=cap),
        grid=(images,),
        in_specs=[image((pos.shape[1], LANES)), image((rows, width))] + [whole((cap, width))] * len(made),
        out_specs=image((seq, width)),
        out_shape=jax.ShapeDtypeStruct((images, seq, width), bf16),
        compiler_params=params(),
        cost_estimate=cost(2 * images * rows * width * cap * len(made), 8 << 20),
        name="combine",
    )(pos, hidden, *made)


def finish_kernel(total_ref, own_ref, limit_ref, peak_ref, *rest, head_rows, members):
    qkv_ref, out_ref, misc_ref, vec_ref, clip_ref = rest
    part = own_ref.shape[0]
    width = out_ref.shape[1]
    wide = 3 * width
    number = wide // LANES
    base = total_ref[:, 0:wide].astype(f32)
    extra = total_ref[:, wide + width + LANES :].astype(f32)
    weight = own_ref[:, 0:wide].astype(f32)
    columns = [sum(extra[k * number + i : k * number + i + 1] for k in range(3)) for i in range(number)]
    columns = jnp.concatenate(columns, axis=1)
    own = own_ref[:, wide + width :].astype(f32)
    gain, bias = own[:, VEC : VEC + 1], own[:, VEC + 1 : VEC + 2]
    qkv_ref[...] = base * gain + bias * columns
    out_ref[...] = total_ref[:, wide : wide + width].astype(f32)
    misc = total_ref[:, wide + width : wide + width + LANES].astype(f32)
    misc_ref[...] = misc
    lane = iota((1, LANES), 1)
    misc = jnp.where(lane == VEC, jnp.sum(base * weight, axis=1, keepdims=True), misc)
    misc = jnp.where(lane == VEC + 1, jnp.sum(columns * weight, axis=1, keepdims=True), misc)
    vec_ref[...] = misc.T[VEC : VEC + 8]
    if members:
        move = jnp.where(
            (iota((LANES, LANES), 0) % HEADS == iota((LANES, LANES), 1)) & (iota((LANES, LANES), 0) < 3 * HEADS),
            1.0,
            0.0,
        )
        peaks = dot(total_ref[head_rows : head_rows + members, wide + width + LANES :], move.astype(bf16), NN)
        peak = jnp.max(peaks, axis=0, keepdims=True)
    else:
        peak = peak_ref[...]
    limit = limit_ref[...]
    root = jnp.sqrt(limit / jnp.maximum(peak, limit))
    place = iota((1, width), 1) // (width // HEADS)
    scale = jnp.zeros((1, width), f32)
    for index in range(HEADS):
        scale = jnp.where(place == index, root[:, index : index + 1], scale)
    clip_ref[:, 0:width] = (weight[:, 0:width] * scale).astype(bf16)
    clip_ref[:, width : 2 * width] = (weight[:, width : 2 * width] * scale).astype(bf16)
    clip_ref[:, 2 * width :] = own_ref[:, 2 * width : wide]


def finish(total, own, limit, peak, width, head_rows, members):
    part = own.shape[0]
    operands = [total, own, limit, peak]
    shapes = [(part, 3 * width), (part, width), (part, LANES), (8, part), (part, 3 * width)]
    return pl.pallas_call(
        functools.partial(finish_kernel, head_rows=head_rows, members=members),
        grid=(1,),
        in_specs=[whole(v.shape) for v in operands],
        out_specs=[whole(v) for v in shapes],
        out_shape=[jax.ShapeDtypeStruct(v, bf16 if i == 4 else f32) for i, v in enumerate(shapes)],
        compiler_params=params(),
        cost_estimate=cost(1 << 20, 4 << 20),
        name="finish",
    )(*operands)


def swap(value, axis):
    return lax.ppermute(value, axis, [(0, 1), (1, 0)])


def rotate(values, axis, size):
    if size != 2:
        return jnp.roll(jnp.stack(values), lax.axis_index(axis), axis=0)
    return jnp.where(lax.axis_index(axis) == 0, jnp.stack(values), jnp.stack(values[::-1]))


def around(value, axis, size):
    return [value] + [
        lax.ppermute(value, axis, [((k + step) % size, k) for k in range(size)]) for step in range(1, size)
    ]


def split_sum(value, axis, size):
    if size != 2:
        return lax.psum_scatter(value, axis, scatter_dimension=0, tiled=False)
    place = lax.axis_index(axis)
    sent = lax.dynamic_index_in_dim(value, 1 - place, 0, keepdims=False)
    kept = lax.dynamic_index_in_dim(value, place, 0, keepdims=False)
    return (kept.astype(f32) + swap(sent, axis).astype(f32)).astype(value.dtype)


def exchange(value, shift, experts):
    return lax.ppermute(value, GROUP, [(k, k ^ shift) for k in range(experts)])


def shift_order(experts):
    def key(shift):
        return (shift < 2, bin(shift >> 1).count("1"), shift & 1, shift)

    return sorted(range(experts), key=key)


STRAIGHT = [(0, 0), (1, 2), (2, 1), (3, 3)]
CROSSED = [(0, 2), (1, 0), (2, 3), (3, 1)]
BACK = [(b, a) for a, b in STRAIGHT]
BACK_CROSSED = [(b, a) for a, b in CROSSED]


def shards(
    tokens,
    ln1_gain,
    ln1_bias,
    w_qkv,
    q_bias,
    v_bias,
    w_out,
    out_bias,
    ln2_gain,
    ln2_bias,
    w_router,
    expert_w1,
    expert_b1,
    expert_w2,
    expert_b2,
    route_ids,
    clip_threshold,
    grad_output,
    *,
    experts,
    fsdp,
):
    images, seq, width = tokens.shape
    token_count = images * seq
    ways = fsdp // 2
    cap = (7 * token_count // (2 * experts) + 7) // 8 * 8
    stride = -(-seq // 256) * 256
    rows = -(-seq // 16) * 16
    part = w_qkv.shape[0]
    hidden_part = expert_w2.shape[1]
    high, low, fy, core = (lax.axis_index(name).astype(i32) for name in DEVICE)
    place_ref = (low * 2 + core).reshape(1)
    spot = fy * 2 + core

    vectors = (ln1_gain, ln1_bias, q_bias, v_bias, out_bias, ln2_gain, ln2_bias)
    own, w2_own = pack_parameters(
        spot.reshape(1), w_qkv, w_out, w_router, vectors, expert_w2[0], expert_b1, expert_b2
    )

    def to_places(shard):
        return (
            lax.ppermute(shard, ("hi", "core"), STRAIGHT),
            lax.ppermute(shard, ("hi", "core"), CROSSED),
        )

    def all_rows(pair):
        straight, crossed = (rotate(around(value, "fy", ways), "fy", ways) for value in pair)
        return jnp.where(
            high == 0, jnp.stack([straight, crossed], axis=1), jnp.stack([crossed, straight], axis=1)
        )

    pack = around(own, "fy", ways)
    w1_pair = to_places(expert_w1[0])
    pack = rotate(pack, "fy", ways)
    other = swap(pack, "core")
    pack = jnp.where(core == 0, jnp.stack([pack, other], axis=1), jnp.stack([other, pack], axis=1))
    pack = pack.reshape(width, pack.shape[-1])

    ids = jnp.pad(route_ids.reshape(images, seq, -1), ((0, 0), (0, stride - seq), (0, 0)), constant_values=-1)
    ids = ids.reshape(images * stride, -1).T
    post, pos, *ups = route(place_ref, ids, grad_output, experts, cap, stride)
    order = shift_order(experts)
    ups_in = {shift: ups[shift] if shift == 0 else exchange(ups[shift], shift, experts) for shift in order}

    w2_own, w1_pair = lax.optimization_barrier((w2_own, w1_pair))
    w2_pair = to_places(w2_own)
    outputs = forward(place_ref, tokens, pack, post, w1_pair, experts, cap, stride, rows)
    saved, peak, sent = outputs[:5], outputs[5], outputs[6:]
    w1 = all_rows(w1_pair).reshape(width, -1)
    w2 = all_rows(w2_pair).reshape(fsdp, hidden_part + TAIL, width)

    size = max(1, experts // 4)
    groups = [order[at : at + size] for at in range(0, experts, size)]
    arrived, before = {}, None
    for group in groups:
        pending = [sent[shift] for shift in group]
        if before is not None:
            pending, before = lax.optimization_barrier((pending, before))
        got = [value if shift == 0 else exchange(value, shift, experts) for shift, value in zip(group, pending)]
        before = got
        arrived.update(zip(group, got))

    old = None
    backs, made = {}, {}
    for number, group in enumerate(groups):
        result = expert_call(
            place_ref,
            [arrived[shift] for shift in group],
            [ups_in[shift] for shift in group],
            (w1, w2),
            pack,
            old,
            cap,
            experts,
            number == len(groups) - 1,
        )
        count = len(group)
        old = result[2 * count :]
        for at, shift in enumerate(group):
            backs[shift] = result[at] if shift == 0 else exchange(result[at], shift, experts)
            made[shift] = result[count + at]
    backs = [backs[shift] for shift in range(experts)]
    made = [made[shift] for shift in range(experts)]
    made, backs = lax.optimization_barrier((made, backs))
    made = [value if shift == 0 else exchange(value, shift, experts) for shift, value in enumerate(made)]

    hidden_grad, mixed_grad, sums = middle(place_ref, grad_output, pack, pos, saved, backs, cap, experts)
    head_rows = 3 * (3 * width // LANES) + 4
    devices = 2 * experts // 2 * fsdp
    members = devices if head_rows + devices <= part else 0
    device = ((high * (experts // 2) + low) * ways + fy) * 2 + core
    spots = jnp.stack([core, device])
    qkv_grad, keep, give = backward(
        spots, tokens, saved, mixed_grad, sums, peak, made[: experts // 2], ways, part, head_rows, members
    )

    def return_grad(grad):
        grad = split_sum(grad, "fy", ways)
        straight = lax.dynamic_index_in_dim(grad, high, 0, keepdims=False)
        crossed = lax.dynamic_index_in_dim(grad, 1 - high, 0, keepdims=False)
        straight = lax.ppermute(straight, ("hi", "core"), BACK)
        crossed = lax.ppermute(crossed, ("hi", "core"), BACK_CROSSED)
        return straight.astype(f32) + crossed.astype(f32)

    grad_w1 = return_grad(old[0].reshape(ways, 2, part, -1))[None]
    grad_w2 = return_grad(old[1].reshape(ways, 2, hidden_part + TAIL, width))
    grad_b1 = grad_w2[hidden_part : hidden_part + 1, :hidden_part]
    grad_b2 = lax.dynamic_slice_in_dim(grad_w2[hidden_part + 1 : hidden_part + 2], spot * part, part, axis=1)
    grad_w2 = grad_w2[None, :hidden_part]

    sums = (keep.astype(f32) + swap(give, "core").astype(f32)).astype(bf16)
    sums = split_sum(sums, "fy", ways)
    input_grad = first_norm(tokens, qkv_grad, pack, hidden_grad)
    output = combine_output(pos, saved[2], made, cap, seq)
    sums = sums.reshape(experts, part // experts, -1)
    sums = lax.all_to_all(sums, ("hi", "lo"), split_axis=0, concat_axis=0, tiled=True)
    total = jnp.sum(sums.astype(f32), axis=0, keepdims=True).astype(bf16)
    total = jnp.broadcast_to(total, (experts,) + total.shape[1:])
    total = lax.all_to_all(total, ("hi", "lo"), split_axis=0, concat_axis=0, tiled=True)
    total = total.reshape(part, -1)
    if not members:
        peak = jnp.max(lax.all_gather(peak, DEVICE, axis=0, tiled=True), axis=0, keepdims=True)
    limit = jnp.pad(clip_threshold.astype(f32).reshape(1, HEADS), ((0, 0), (0, LANES - HEADS)), constant_values=1.0)
    grad_qkv, grad_out, grad_misc, grads, clipped = finish(total, own, limit, peak, width, head_rows, members)
    return (
        output,
        input_grad,
        grads[0],
        grads[1],
        grad_qkv,
        grads[2],
        grads[3],
        grad_out,
        grads[4],
        grads[5],
        grads[6],
        grad_misc[:, :experts],
        grad_w1,
        grad_b1,
        grad_w2,
        grad_b2,
        clipped,
    )


def solution(mesh):
    experts, fsdp = mesh.shape["expert"], mesh.shape["fsdp"]
    inner = Mesh(mesh.devices.reshape(2, experts // 2, fsdp // 2, 2), DEVICE)
    token, row, expert = P(DEVICE, None, None), ("fy", "core"), ("hi", "lo")
    vector, matrix = P(row), P(row, None)
    return jax.shard_map(
        functools.partial(shards, experts=experts, fsdp=fsdp),
        mesh=inner,
        in_specs=(
            token,
            vector,
            vector,
            matrix,
            vector,
            vector,
            matrix,
            vector,
            vector,
            vector,
            matrix,
            P(expert, row, None),
            P(expert, row),
            P(expert, row, None),
            P(expert, row),
            P(DEVICE, None),
            P(),
            token,
        ),
        out_specs=(
            token,
            token,
            vector,
            vector,
            matrix,
            vector,
            vector,
            matrix,
            vector,
            vector,
            vector,
            matrix,
            P(expert, row, None),
            P(expert, row),
            P(expert, row, None),
            P(expert, row),
            matrix,
        ),
        check_vma=False,
    )
```

time: 726 us -> 447 us (0.62)
  Pallas kernels: 0 us -> 214 us
  matrix products: 204 us -> 0 us
  blocking collectives: 126 us -> 0 us
  local copies, waits for them, and re-layouts: 138 us -> 18.5 us
  starting transfers between devices: 22.2 us -> 87.9 us
  other arithmetic: 76 us -> 15.3 us
  waiting for transfers between devices: 136 us -> 106 us
  between operations: 16.1 us -> 1.34 us
    pallas_call x0 -> x12, Pallas kernels: none -> 214 us  [the longest x4 97.7 us: expert_call(): pl.pallas_call(functools.partial(expert_kernel, cap=cap, count=count, fir...]
    dot_general x21 -> x0, matrix products: 204 us -> none  [the longest x1 70.8 us: shards(): jnp.dot(flat_in, first_weight, preferred_element_type=jnp.float32)]
    ppermute x0 -> x46, waiting for transfers between devices: none -> 85.2 us  [the longest x28 58.4 us: exchange(): return lax.ppermute(value, GROUP, [(k, k ^ shift) for k in range(experts)])]
    ppermute x0 -> x46, starting transfers between devices: none -> 80.7 us  [the longest x28 45.7 us: exchange(): return lax.ppermute(value, GROUP, [(k, k ^ shift) for k in range(experts)])]
    all_gather x11 -> x0, blocking collectives: 60.2 us -> none  [the longest x1 7.87 us: shards(): lax.all_gather(w_out, 'fsdp', axis=0, tiled=True)]
    all_to_all x4 -> x2, waiting for transfers between devices: 79.7 us -> 20.7 us  [the longest x1 15.1 us: shards(): lax.all_to_all(sums, ('hi', 'lo'), split_axis=0, concat_axis=0, tiled=True)]
    psum x1 -> x0, waiting for transfers between devices: 49.8 us -> none  [shards(): lax.psum(shares[2].astype(jnp.bfloat16), 'expert').astype(jnp.float32)]
    reshape x18 -> x1, local copies, waits for them, and re-layouts: 49.3 us -> 0.77 us  [shards(): route_ids.reshape(images, seq, -1)]
  transfers between devices with their start and end apart: 15 -> 48, of which waited for: 5 -> 16; matrix products, arithmetic and copies ran while one was open for 49% -> 6% of each run, Pallas kernels for 0% -> 40%
where the time goes in v1:
time: 447 us; the launch traced here: 443 us
  Pallas kernels  214 us (48%)
  waiting for transfers between devices  106 us (24%)
  starting transfers between devices  87.9 us (20%)
  local copies, waits for them, and re-layouts  18.5 us (4%)
  other arithmetic  15.3 us (3%)
    pallas_call x4, Pallas kernels, expert_call(): pl.pallas_call(functools.partial(expert_kernel, cap=cap, count=count, fir...  97.7 us
    ppermute x28, waiting for transfers between devices, exchange(): return lax.ppermute(value, GROUP, [(k, k ^ shift) for k in range(experts)])  58.4 us
    ppermute x28, starting transfers between devices, exchange(): return lax.ppermute(value, GROUP, [(k, k ^ shift) for k in range(experts)])  45.7 us
    pallas_call x1, Pallas kernels, forward(): pl.pallas_call(functools.partial(forward_kernel, cap=cap, stride=stride,...  33.8 us
    pallas_call x1, Pallas kernels, backward(): pl.pallas_call(functools.partial(backward_kernel, head_rows=head_rows, me...  32.4 us
    ppermute x2, waiting for transfers between devices, return_grad(): crossed = lax.ppermute(crossed, ('hi', 'core'), BACK_CROSSED)  19.6 us
    pallas_call x1, Pallas kernels, middle(): pl.pallas_call(functools.partial(middle_kernel, cap=cap, experts=experts)...  18.1 us
    all_to_all x1, waiting for transfers between devices, shards(): lax.all_to_all(sums, ('hi', 'lo'), split_axis=0, concat_axis=0, tiled=True)  15.1 us
  transfers between devices with their start and end apart: 48, of which 16 were waited for; matrix products, arithmetic and copies ran while one was open for 6% of the time, Pallas kernels for 40%

profile of v1, /device:TPU:0, one launch (start us, length us, event | category | flops | bytes accessed | tf_op | source)
XLA Modules:
  0.0 442.8 jit_solution(14079370628616494308)
XLA Ops:
  2.1 2.4 pack.1
  4.5 3.0 collective-permute-start
  9.1 2.9 collective-permute-start.3
  13.4 10.4 %route.1 = (f32[8,1280]{1,0:T(8,128)}, f32[5,256,128]{2,1,0:T(8,128)}, bf16[432,512]{1,0:T(8,128)(2,1)}, bf16[432,512]{1,0:T(8,128)(2,1)}, bf16[432,512]{1,0:T(8...) custom-call(s32[1]{0:T(128)} %bitcast.place_ref, ...), custom_call_target="tpu_custom_call" | custom-call | flops 4529848320 | bytes 8388608 | tf_op jit(solution)/shard_map/route/pallas_call | solution.py:189
  27.4 9.2 %collective-permute-start.16 = (bf16[528,512]{1,0:T(8,128)(2,1)S(1)}, bf16[528,512]{1,0:T(8,128)(2,1)S(1)}, u32[]{:S(2)}, u32[]{:S(2)}) collective-permute-start(bf16[528,512]{1,0:T(8,128)(2,1)S(1)} %copy-done.7), channel_id=1, source_target_pairs={{0,16},{1,0},{16,17},{17,1},{2,18},{3,2},{18,19},{19,3},{4,20},{5,... | collective-permute-start | bytes 1622024 | tf_op jit(solution)/shard_map/ppermute | solution.py:909
  39.1 2.7 collective-permute-done.12
  41.8 20.0 %collective-permute-start.23 = (bf16[432,512]{1,0:T(8,128)(2,1)S(1)}, bf16[432,512]{1,0:T(8,128)(2,1)S(1)}, u32[]{:S(2)}, u32[]{:S(2)}) collective-permute-start(bf16[432,512]{1,0:T(8,128)(2,1)S(1)} %copy-done.26), channel_id=1, source_target_pairs={{0,8},{1,9},{4,12},{5,13},{8,0},{9,1},{12,4},{13,5},{2,10},{3,11},... | collective-permute-start | bytes 1327112 | tf_op jit(solution)/shard_map/ppermute | solution.py:850
  67.7 33.8 %attend.1 = (bf16[5,208,1536]{2,1,0:T(8,128)(2,1)}, bf16[5,208,512]{2,1,0:T(8,128)(2,1)}, f32[5,208,512]{2,1,0:T(8,128)}, f32[5,208,128]{2,1,0:T(8,128)}, f32[5,...) custom-call(s32[1]{0:T(128)} %bitcast.place_ref, ...), custom_call_target="tpu_custom_call" | custom-call | flops 7256145920 | bytes 16777216 | tf_op jit(solution)/shard_map/attend/pallas_call | solution.py:315
  105.3 7.0 %collective-permute-done.4.refs_0_ = bf16[432,512]{1,0:T(8,128)(2,1)S(1)} collective-permute-done((bf16[432,512]{1,0:T(8,128)(2,1)}, bf16[432,512]{1,0:T(8,128)(2,1)S(1)}, u32[]{:S(2)}, u32[]{:S(2)}) %collective-permute-start.4) | collective-permute-done | bytes 442400 | tf_op jit(solution)/shard_map/ppermute | solution.py:850
  116.1 23.8 %expert.4 = (bf16[448,512]{1,0:T(8,128)(2,1)}, bf16[448,512]{1,0:T(8,128)(2,1)}, bf16[432,512]{1,0:T(8,128)(2,1)}, bf16[432,512]{1,0:T(8,128)(2,1)}, f32[512,2048]{1,0:T(8,128)}, /*index=5*/f32[4,528,512]{2,1,0:T(8,128)}) custom-call(s32[1]{0:T(128)} %bitcast.place_ref, bf16[432,512]{1,0:T(8,128)(2,1)} %copy-done.37, bf16[432,512]{1,0:T(8,128)(2,1)} %copy-done.39, ...), custom_call_target="tpu_custom_call" | custom-call | flops 10871635968 | bytes 25165824 | tf_op jit(solution)/shard_map/expert/pallas_call | solution.py:441
  145.3 24.8 %expert.5 = (bf16[448,512]{1,0:T(8,128)(2,1)}, bf16[448,512]{1,0:T(8,128)(2,1)}, bf16[432,512]{1,0:T(8,128)(2,1)}, bf16[432,512]{1,0:T(8,128)(2,1)}, f32[512,2048]{1,0:T(8,128)}, /*index=5*/f32[4,528,512]{2,1,0:T(8,128)}) custom-call(s32[1]{0:T(128)} %bitcast.place_ref, bf16[432,512]{1,0:T(8,128)(2,1)} %collective-permute-done.6.refs_0_, ...), custom_call_target="tpu_custom_call" | custom-call | flops 10871635968 | bytes 25165824 | tf_op jit(solution)/shard_map/expert/pallas_call | solution.py:441
  170.1 2.8 collective-permute-done.8.refs_0_
  175.2 5.5 %collective-permute-done.9.refs_1_ = bf16[432,512]{1,0:T(8,128)(2,1)S(1)} collective-permute-done((bf16[432,512]{1,0:T(8,128)(2,1)S(1)}, bf16[432,512]{1,0:T(8,128)(2,1)S(1)}, u32[]{:S(2)}, u32[]{:S(2)}) %collective-permute-start.9) | collective-permute-done | bytes 442400 | tf_op jit(solution)/shard_map/ppermute | solution.py:850
  184.8 24.4 %expert.6 = (bf16[448,512]{1,0:T(8,128)(2,1)}, bf16[448,512]{1,0:T(8,128)(2,1)}, bf16[432,512]{1,0:T(8,128)(2,1)}, bf16[432,512]{1,0:T(8,128)(2,1)}, f32[512,2048]{1,0:T(8,128)}, /*index=5*/f32[4,528,512]{2,1,0:T(8,128)}) custom-call(s32[1]{0:T(128)} %bitcast.place_ref, bf16[432,512]{1,0:T(8,128)(2,1)} %copy-done.38, bf16[432,512]{1,0:T(8,128)(2,1)} %copy-done.41, ...), custom_call_target="tpu_custom_call" | custom-call | flops 10871635968 | bytes 25165824 | tf_op jit(solution)/shard_map/expert/pallas_call | solution.py:441
  211.5 24.6 %expert.7 = (bf16[448,512]{1,0:T(8,128)(2,1)}, bf16[448,512]{1,0:T(8,128)(2,1)}, bf16[432,512]{1,0:T(8,128)(2,1)}, bf16[432,512]{1,0:T(8,128)(2,1)}, bf16[512,20...) custom-call(s32[1]{0:T(128)} %bitcast.place_ref, bf16[432,512]{1,0:T(8,128)(2,1)} %get-tuple-element.122.refs_0_, ...), custom_call_target="tpu_custom_call" | custom-call | flops 10871635968 | bytes 25165824 | tf_op jit(solution)/shard_map/expert/pallas_call | solution.py:441
  238.5 11.6 %collective-permute-done.30.rest_7_ = bf16[448,512]{1,0:T(8,128)(2,1)} collective-permute-done((bf16[448,512]{1,0:T(8,128)(2,1)S(1)}, bf16[448,512]{1,0:T(8,128)(2,1)}, u32[]{:S(2)}, u32[]{:S(2)}) %collective-permute-start.30) | collective-permute-done | bytes 458784 | tf_op jit(solution)/shard_map/ppermute | solution.py:850
  251.9 18.1 %middle.1 = (f32[5,208,512]{2,1,0:T(8,128)}, bf16[5,208,512]{2,1,0:T(8,128)(2,1)}, f32[512,640]{1,0:T(8,128)}) custom-call(s32[1]{0:T(128)} %bitcast.place_ref, bf16[5,197,512]{2,1,0:T(8,128)(2,1)} %up_ref.3, bf16[512,2176]{1,0:T(8,128)(2,1)} %bitcast.93, bf16[512,2176]{1,0:T(8,128)(2,1)} %bitcast.94, f32[5,256,128]{2,1,0:T(8,128)} %get-tuple-element.103.pos_ref, ...), custom_call_target="tpu_custom_call" | custom-call | flops 4771020800 | bytes 16777216 | tf_op jit(solution)/shard_map/middle/pallas_call | solution.py:545
  272.6 32.4 %attend_back.1 = (bf16[5,208,1536]{2,1,0:T(8,128)(2,1)}, bf16[2,128,2304]{2,1,0:T(8,128)(2,1)}, bf16[2,128,2304]{2,1,0:T(8,128)(2,1)}) custom-call(s32[2]{0:T(128)} %pad_add_fusion.spots_ref, bf16[5,197,512]{2,1,0:T(8,128)(2,1)} %tok_ref.5, bf16[5,208,1536]{2,1,0:T(8,128)(2,1)} %get-tuple-element.163.qkv_ref, f32[5,208,128]{2,1,0:T(8,128)} %get-tuple-element.164.lse_ref, ...), custom_call_target="tpu_custom_call" | custom-call | flops 4362076160 | bytes 25165824 | tf_op jit(solution)/shard_map/attend_back/pallas_call | solution.py:666
  315.8 4.2 collective-permute-done.34.rest_4_
  321.5 6.6 %collective-permute-done.35.rest_5_ = bf16[432,512]{1,0:T(8,128)(2,1)S(1)} collective-permute-done((bf16[432,512]{1,0:T(8,128)(2,1)S(1)}, bf16[432,512]{1,0:T(8,128)(2,1)S(1)}, u32[]{:S(2)}, u32[]{:S(2)}) %collective-permute-start.35) | collective-permute-done | bytes 442400 | tf_op jit(solution)/shard_map/ppermute | solution.py:850
  329.7 10.2 %collective-permute-done.36.rest_6_ = bf16[432,512]{1,0:T(8,128)(2,1)S(1)} collective-permute-done((bf16[432,512]{1,0:T(8,128)(2,1)}, bf16[432,512]{1,0:T(8,128)(2,1)S(1)}, u32[]{:S(2)}, u32[]{:S(2)}) %collective-permute-start.36) | collective-permute-done | bytes 442400 | tf_op jit(solution)/shard_map/ppermute | solution.py:850
  340.6 7.6 %collective-permute-done.37.rest_7_ = bf16[432,512]{1,0:T(8,128)(2,1)} collective-permute-done((bf16[432,512]{1,0:T(8,128)(2,1)}, bf16[432,512]{1,0:T(8,128)(2,1)}, u32[]{:S(2)}, u32[]{:S(2)}) %collective-permute-start.37) | collective-permute-done | bytes 442400 | tf_op jit(solution)/shard_map/ppermute | solution.py:850
  348.2 8.4 %combine.1 = bf16[5,197,512]{2,1,0:T(8,128)(2,1)} custom-call(f32[5,256,128]{2,1,0:T(8,128)} %get-tuple-element.103.pos_ref, f32[5,208,512]{2,1,0:T(8,128)} %get-tuple-element.109.hidden_ref, bf16[432,512]{1,0:T(8,128)(2,1)} %get-tuple-element.155.rest_0_, bf16[432,512]{1,0:T(8,128)(2,1)} %copy-done.27, bf16[432,512]{1,0:T(8,128)(2,1)} %copy-done.28, ...), custom_call_target="tpu_custom_call" | custom-call | flops 3680501760 | bytes 8388608 | tf_op jit(solution)/shard_map/combine/pallas_call | solution.py:754
  357.6 3.5 all-to-all-start
  364.6 5.4 %collective-permute-start.41 = (bf16[128,2048]{1,0:T(8,128)(2,1)}, bf16[128,2048]{1,0:T(8,128)(2,1)}, u32[]{:S(2)}, u32[]{:S(2)}) collective-permute-start(bf16[128,2048]{1,0:T(8,128)(2,1)} %get-tuple-element.227), channel_id=1, source_target_pairs={{0,0},{16,1},{1,16},{17,17},{2,2},{18,3},{3,18},{19,19},{4,4},{20,... | collective-permute-start | bytes 1572872 | tf_op jit(solution)/shard_map/ppermute | solution.py:987
  369.9 4.5 %collective-permute-done.43 = bf16[2,528,512]{2,1,0:T(8,128)(2,1)} collective-permute-done((bf16[2,528,512]{2,1,0:T(8,128)(2,1)}, bf16[2,528,512]{2,1,0:T(8,128)(2,1)}, u32[]{:S(2)}, u32[]{:S(2)}) %collective-permute-start.43) | collective-permute-done | bytes 1081376 | tf_op jit(solution)/shard_map/ppermute | solution.py:825
  377.6 8.0 %first_norm.1 = f32[5,197,512]{2,1,0:T(8,128)} custom-call(bf16[5,197,512]{2,1,0:T(8,128)(2,1)} %tok_ref.5, bf16[5,208,1536]{2,1,0:T(8,128)(2,1)} %get-tuple-element.178.qkv_grad_ref, bf16[512,2176]{1,0:T(8,128)(2,1)} %bitcast.95, bf16[512,2176]{1,0:T(8,128)(2,1)} %bitcast.96, f32[5,208,512]{2,1,0:T(8,128)} %get-tuple-element.179.hidden_grad_ref), custom_call_target="tpu_custom_call" | custom-call | flops 1635778560 | bytes 12582912 | tf_op jit(solution)/shard_map/first_norm/pallas_call | solution.py:719
  385.6 15.1 %all-to-all-done = bf16[8,16,2304]{2,1,0:T(8,128)(2,1)S(1)} async-done(((bf16[8,16,2304]{2,1,0:T(8,128)(2,1)}), bf16[8,16,2304]{2,1,0:T(8,128)(2,1)S(1)}, u32[]{:S(2)}, u32[]{:S(2)}) %all-to-all-start) | async-done | bytes 589856 | tf_op jit(solution)/shard_map/all_to_all | solution.py:1002
  401.6 3.7 all-to-all-start.1
  408.7 18.5 %collective-permute-done.45 = bf16[528,512]{1,0:T(8,128)(2,1)S(1)} collective-permute-done((bf16[528,512]{1,0:T(8,128)(2,1)S(1)}, bf16[528,512]{1,0:T(8,128)(2,1)S(1)}, u32[]{:S(2)}, u32[]{:S(2)}) %collective-permute-start.45) | collective-permute-done | bytes 540704 | tf_op jit(solution)/shard_map/ppermute | solution.py:988
  430.6 5.6 %all-to-all-done.1 = bf16[8,16,2304]{2,1,0:T(8,128)(2,1)S(1)} async-done(((bf16[8,16,2304]{2,1,0:T(8,128)(2,1)}), bf16[8,16,2304]{2,1,0:T(8,128)(2,1)S(1)}, u32[]{:S(2)}, u32[]{:S(2)}) %all-to-all-start.1) | async-done | bytes 589856 | tf_op jit(solution)/shard_map/all_to_all | solution.py:1005
  437.0 2.6 finish.1
  (203 shorter events, 78.2 us)
Async XLA Ops:
  4.5 32.2 %collective-permute-start = (bf16[128,2176]{1,0:T(8,128)(2,1)}, bf16[128,2176]{1,0:T(8,128)(2,1)S(1)}, u32[]{:S(2)}, u32[]{:S(2)}) collective-permute-start(bf16[128,2176]{1,0:T(8,128)(2,1)} %get-tuple-element.104.own_ref), channel_id=1, source_target_pairs={{2,0},{0,2},{3,1},{1,3},{6,4},{4,6},{7,5},{5,7},{10,8},{8,10},{11,... | collective-permute-start | bytes 1671176 | tf_op jit(solution)/shard_map/ppermute | solution.py:836
  23.8 90.0 %collective-permute-start.22 = (bf16[432,512]{1,0:T(8,128)(2,1)}, bf16[432,512]{1,0:T(8,128)(2,1)S(1)}, u32[]{:S(2)}, u32[]{:S(2)}) collective-permute-start(bf16[432,512]{1,0:T(8,128)(2,1)} %get-tuple-element.131), channel_id=1, source_target_pairs={{0,4},{1,5},{4,0},{5,1},{8,12},{9,13},{12,8},{13,9},{2,6},{3,7},{6... | collective-permute-start | bytes 1327112 | tf_op jit(solution)/shard_map/ppermute | solution.py:850
  27.4 36.3 %collective-permute-start.16 = (bf16[528,512]{1,0:T(8,128)(2,1)S(1)}, bf16[528,512]{1,0:T(8,128)(2,1)S(1)}, u32[]{:S(2)}, u32[]{:S(2)}) collective-permute-start(bf16[528,512]{1,0:T(8,128)(2,1)S(1)} %copy-done.7), channel_id=1, source_target_pairs={{0,16},{1,0},{16,17},{17,1},{2,18},{3,2},{18,19},{19,3},{4,20},{5,... | collective-permute-start | bytes 1622024 | tf_op jit(solution)/shard_map/ppermute | solution.py:909
  36.8 28.9 %collective-permute-start.1 = (bf16[2,128,2176]{2,1,0:T(8,128)(2,1)S(1)}, bf16[2,128,2176]{2,1,0:T(8,128)(2,1)S(1)}, u32[]{:S(2)}, u32[]{:S(2)}) collective-permute-start(bf16[2,128,2176]{2,1,0:T(8,128)(2,1)S(1)} %maximum_select_fusion.4), channel_id=1, source_target_pairs={{0,1},{1,0},{2,3},{3,2},{4,5},{5,4},{6,7},{7,6},{8,9},{9,8},{10,11... | collective-permute-start | bytes 3342344 | tf_op jit(solution)/shard_map/ppermute | solution.py:825
  37.9 26.3 %collective-permute-start.14 = (bf16[528,512]{1,0:T(8,128)(2,1)S(1)}, bf16[528,512]{1,0:T(8,128)(2,1)S(1)}, u32[]{:S(2)}, u32[]{:S(2)}) collective-permute-start(bf16[528,512]{1,0:T(8,128)(2,1)S(1)} %copy-done.7), channel_id=1, source_target_pairs={{0,0},{1,16},{16,1},{17,17},{2,2},{3,18},{18,3},{19,19},{4,4},{5,2... | collective-permute-start | bytes 1622024 | tf_op jit(solution)/shard_map/ppermute | solution.py:908
  41.8 72.5 %collective-permute-start.23 = (bf16[432,512]{1,0:T(8,128)(2,1)S(1)}, bf16[432,512]{1,0:T(8,128)(2,1)S(1)}, u32[]{:S(2)}, u32[]{:S(2)}) collective-permute-start(bf16[432,512]{1,0:T(8,128)(2,1)S(1)} %copy-done.26), channel_id=1, source_target_pairs={{0,8},{1,9},{4,12},{5,13},{8,0},{9,1},{12,4},{13,5},{2,10},{3,11},... | collective-permute-start | bytes 1327112 | tf_op jit(solution)/shard_map/ppermute | solution.py:850
  63.7 39.3 %collective-permute-start.17 = (bf16[528,512]{1,0:T(8,128)(2,1)S(1)}, bf16[528,512]{1,0:T(8,128)(2,1)S(1)}, u32[]{:S(2)}, u32[]{:S(2)}) collective-permute-start(bf16[528,512]{1,0:T(8,128)(2,1)S(1)} %collective-permute-done.16), channel_id=1, source_target_pairs={{2,0},{0,2},{3,1},{1,3},{6,4},{4,6},{7,5},{5,7},{10,8},{8,10},{11,... | collective-permute-start | bytes 1622024 | tf_op jit(solution)/shard_map/ppermute | solution.py:836
  64.3 39.0 %collective-permute-start.15 = (bf16[528,512]{1,0:T(8,128)(2,1)S(1)}, bf16[528,512]{1,0:T(8,128)(2,1)S(1)}, u32[]{:S(2)}, u32[]{:S(2)}) collective-permute-start(bf16[528,512]{1,0:T(8,128)(2,1)S(1)} %collective-permute-done.14), channel_id=1, source_target_pairs={{2,0},{0,2},{3,1},{1,3},{6,4},{4,6},{7,5},{5,7},{10,8},{8,10},{11,... | collective-permute-start | bytes 1622024 | tf_op jit(solution)/shard_map/ppermute | solution.py:836
  103.3 106.0 %collective-permute-start.11 = (bf16[432,512]{1,0:T(8,128)(2,1)S(1)}, bf16[432,512]{1,0:T(8,128)(2,1)}, u32[]{:S(2)}, u32[]{:S(2)}) collective-permute-start(bf16[432,512]{1,0:T(8,128)(2,1)S(1)} %copy-done.19), channel_id=1, source_target_pairs={{0,1},{1,0},{4,5},{5,4},{8,9},{9,8},{12,13},{13,12},{2,3},{3,2},{6... | collective-permute-start | bytes 1327112 | tf_op jit(solution)/shard_map/ppermute | solution.py:850
  112.3 30.0 %collective-permute-start.20 = (bf16[432,512]{1,0:T(8,128)(2,1)S(1)}, bf16[432,512]{1,0:T(8,128)(2,1)}, u32[]{:S(2)}, u32[]{:S(2)}) collective-permute-start(bf16[432,512]{1,0:T(8,128)(2,1)S(1)} %copy-done.23), channel_id=1, source_target_pairs={{0,5},{1,4},{4,1},{5,0},{8,13},{9,12},{12,9},{13,8},{2,7},{3,6},{6... | collective-permute-start | bytes 1327112 | tf_op jit(solution)/shard_map/ppermute | solution.py:850
  113.6 30.7 %collective-permute-start.21 = (bf16[432,512]{1,0:T(8,128)(2,1)S(1)}, bf16[432,512]{1,0:T(8,128)(2,1)}, u32[]{:S(2)}, u32[]{:S(2)}) collective-permute-start(bf16[432,512]{1,0:T(8,128)(2,1)S(1)} %copy-done.22), channel_id=1, source_target_pairs={{0,9},{1,8},{4,13},{5,12},{8,1},{9,0},{12,5},{13,4},{2,11},{3,10},... | collective-permute-start | bytes 1327112 | tf_op jit(solution)/shard_map/ppermute | solution.py:850
  114.3 27.3 %collective-permute-start.7 = (bf16[432,512]{1,0:T(8,128)(2,1)S(1)}, bf16[432,512]{1,0:T(8,128)(2,1)}, u32[]{:S(2)}, u32[]{:S(2)}) collective-permute-start(bf16[432,512]{1,0:T(8,128)(2,1)S(1)} %copy-done.33), channel_id=1, source_target_pairs={{0,9},{1,8},{4,13},{5,12},{8,1},{9,0},{12,5},{13,4},{2,11},{3,10},... | collective-permute-start | bytes 1327112 | tf_op jit(solution)/shard_map/ppermute | solution.py:850
  139.9 43.0 %collective-permute-start.18 = (bf16[432,512]{1,0:T(8,128)(2,1)S(1)}, bf16[432,512]{1,0:T(8,128)(2,1)S(1)}, u32[]{:S(2)}, u32[]{:S(2)}) collective-permute-start(bf16[432,512]{1,0:T(8,128)(2,1)S(1)} %copy-done.21), channel_id=1, source_target_pairs={{0,12},{1,13},{4,8},{5,9},{8,4},{9,5},{12,0},{13,1},{2,14},{3,15},... | collective-permute-start | bytes 1327112 | tf_op jit(solution)/shard_map/ppermute | solution.py:850
  141.5 42.5 %collective-permute-start.19 = (bf16[432,512]{1,0:T(8,128)(2,1)S(1)}, bf16[432,512]{1,0:T(8,128)(2,1)S(1)}, u32[]{:S(2)}, u32[]{:S(2)}) collective-permute-start(bf16[432,512]{1,0:T(8,128)(2,1)S(1)} %copy-done.20), channel_id=1, source_target_pairs={{0,13},{1,12},{4,9},{5,8},{8,5},{9,4},{12,1},{13,0},{2,15},{3,14},... | collective-permute-start | bytes 1327112 | tf_op jit(solution)/shard_map/ppermute | solution.py:850
  142.3 30.6 %collective-permute-start.8 = (bf16[432,512]{1,0:T(8,128)(2,1)S(1)}, bf16[432,512]{1,0:T(8,128)(2,1)S(1)}, u32[]{:S(2)}, u32[]{:S(2)}) collective-permute-start(bf16[432,512]{1,0:T(8,128)(2,1)S(1)} %copy-done.31), channel_id=1, source_target_pairs={{0,12},{1,13},{4,8},{5,9},{8,4},{9,5},{12,0},{13,1},{2,14},{3,15},... | collective-permute-start | bytes 1327112 | tf_op jit(solution)/shard_map/ppermute | solution.py:850
  144.3 36.4 %collective-permute-start.9 = (bf16[432,512]{1,0:T(8,128)(2,1)S(1)}, bf16[432,512]{1,0:T(8,128)(2,1)S(1)}, u32[]{:S(2)}, u32[]{:S(2)}) collective-permute-start(bf16[432,512]{1,0:T(8,128)(2,1)S(1)} %copy-done.30), channel_id=1, source_target_pairs={{0,13},{1,12},{4,9},{5,8},{8,5},{9,4},{12,1},{13,0},{2,15},{3,14},... | collective-permute-start | bytes 1327112 | tf_op jit(solution)/shard_map/ppermute | solution.py:850
  173.7 62.5 %collective-permute-start.25 = (bf16[448,512]{1,0:T(8,128)(2,1)S(1)}, bf16[448,512]{1,0:T(8,128)(2,1)S(1)}, u32[]{:S(2)}, u32[]{:S(2)}) collective-permute-start(bf16[448,512]{1,0:T(8,128)(2,1)S(1)} %copy-done.11), channel_id=1, source_target_pairs={{0,4},{1,5},{4,0},{5,1},{8,12},{9,13},{12,8},{13,9},{2,6},{3,7},{6... | collective-permute-start | bytes 1376264 | tf_op jit(solution)/shard_map/ppermute | solution.py:850
  181.4 56.1 %collective-permute-start.27 = (bf16[448,512]{1,0:T(8,128)(2,1)S(1)}, bf16[448,512]{1,0:T(8,128)(2,1)S(1)}, u32[]{:S(2)}, u32[]{:S(2)}) collective-permute-start(bf16[448,512]{1,0:T(8,128)(2,1)S(1)} %copy-done.9), channel_id=1, source_target_pairs={{0,8},{1,9},{4,12},{5,13},{8,0},{9,1},{12,4},{13,5},{2,10},{3,11},... | collective-permute-start | bytes 1376264 | tf_op jit(solution)/shard_map/ppermute | solution.py:850
  182.9 55.5 %collective-permute-start.26 = (bf16[448,512]{1,0:T(8,128)(2,1)}, bf16[448,512]{1,0:T(8,128)(2,1)S(1)}, u32[]{:S(2)}, u32[]{:S(2)}) collective-permute-start(bf16[448,512]{1,0:T(8,128)(2,1)} %get-tuple-element.150), channel_id=1, source_target_pairs={{0,5},{1,4},{4,1},{5,0},{8,13},{9,12},{12,9},{13,8},{2,7},{3,6},{6... | collective-permute-start | bytes 1376264 | tf_op jit(solution)/shard_map/ppermute | solution.py:850
  209.3 29.1 %collective-permute-start.28 = (bf16[448,512]{1,0:T(8,128)(2,1)S(1)}, bf16[448,512]{1,0:T(8,128)(2,1)S(1)}, u32[]{:S(2)}, u32[]{:S(2)}) collective-permute-start(bf16[448,512]{1,0:T(8,128)(2,1)S(1)} %copy-done.13), channel_id=1, source_target_pairs={{0,9},{1,8},{4,13},{5,12},{8,1},{9,0},{12,5},{13,4},{2,11},{3,10},... | collective-permute-start | bytes 1376264 | tf_op jit(solution)/shard_map/ppermute | solution.py:850
  210.0 28.4 %collective-permute-start.29 = (bf16[448,512]{1,0:T(8,128)(2,1)}, bf16[448,512]{1,0:T(8,128)(2,1)S(1)}, u32[]{:S(2)}, u32[]{:S(2)}) collective-permute-start(bf16[448,512]{1,0:T(8,128)(2,1)} %get-tuple-element.153), channel_id=1, source_target_pairs={{0,12},{1,13},{4,8},{5,9},{8,4},{9,5},{12,0},{13,1},{2,14},{3,15},... | collective-permute-start | bytes 1376264 | tf_op jit(solution)/shard_map/ppermute | solution.py:850
  308.6 31.2 %collective-permute-start.36 = (bf16[432,512]{1,0:T(8,128)(2,1)}, bf16[432,512]{1,0:T(8,128)(2,1)S(1)}, u32[]{:S(2)}, u32[]{:S(2)}) collective-permute-start(bf16[432,512]{1,0:T(8,128)(2,1)} %get-tuple-element.161), channel_id=1, source_target_pairs={{0,12},{1,13},{4,8},{5,9},{8,4},{9,5},{12,0},{13,1},{2,14},{3,15},... | collective-permute-start | bytes 1327112 | tf_op jit(solution)/shard_map/ppermute | solution.py:850
  310.3 37.9 %collective-permute-start.37 = (bf16[432,512]{1,0:T(8,128)(2,1)}, bf16[432,512]{1,0:T(8,128)(2,1)}, u32[]{:S(2)}, u32[]{:S(2)}) collective-permute-start(bf16[432,512]{1,0:T(8,128)(2,1)} %get-tuple-element.162), channel_id=1, source_target_pairs={{0,13},{1,12},{4,9},{5,8},{8,5},{9,4},{12,1},{13,0},{2,15},{3,14},... | collective-permute-start | bytes 1327112 | tf_op jit(solution)/shard_map/ppermute | solution.py:850
  313.2 43.5 %collective-permute-start.39 = (bf16[128,2304]{1,0:T(8,128)(2,1)S(1)}, bf16[128,2304]{1,0:T(8,128)(2,1)S(1)}, u32[]{:S(2)}, u32[]{:S(2)}) collective-permute-start(bf16[128,2304]{1,0:T(8,128)(2,1)S(1)} %dynamic-slice_bitcast_fusion.2), channel_id=1, source_target_pairs={{0,2},{2,0},{1,3},{3,1},{4,6},{6,4},{5,7},{7,5},{8,10},{10,8},{9,1... | collective-permute-start | bytes 1769480 | tf_op jit(solution)/shard_map/ppermute | solution.py:825
  320.0 41.1 %collective-permute-start.40 = (bf16[2,128,2048]{2,1,0:T(8,128)(2,1)}, bf16[2,128,2048]{2,1,0:T(8,128)(2,1)}, u32[]{:S(2)}, u32[]{:S(2)}) collective-permute-start(bf16[2,128,2048]{2,1,0:T(8,128)(2,1)} %dynamic-slice_bitcast_fusion.1), channel_id=1, source_target_pairs={{0,2},{2,0},{1,3},{3,1},{4,6},{6,4},{5,7},{7,5},{8,10},{10,8},{9,1... | collective-permute-start | bytes 3145736 | tf_op jit(solution)/shard_map/ppermute | solution.py:825
  328.1 46.3 %collective-permute-start.43 = (bf16[2,528,512]{2,1,0:T(8,128)(2,1)}, bf16[2,528,512]{2,1,0:T(8,128)(2,1)}, u32[]{:S(2)}, u32[]{:S(2)}) collective-permute-start(bf16[2,528,512]{2,1,0:T(8,128)(2,1)} %dynamic-slice_bitcast_fusion), channel_id=1, source_target_pairs={{0,2},{2,0},{1,3},{3,1},{4,6},{6,4},{5,7},{7,5},{8,10},{10,8},{9,1... | collective-permute-start | bytes 3244040 | tf_op jit(solution)/shard_map/ppermute | solution.py:825
  357.6 43.1 %all-to-all-start = ((bf16[8,16,2304]{2,1,0:T(8,128)(2,1)}), bf16[8,16,2304]{2,1,0:T(8,128)(2,1)S(1)}, u32[]{:S(2)}, u32[]{:S(2)}) async-start(bf16[8,16,2304]{2,1,0:T(8,128)(2,1)} %bitcast.32), calls=%async_computation | async-start | bytes 1179648 | tf_op jit(solution)/shard_map/all_to_all | solution.py:1002
  364.1 42.3 %collective-permute-start.42 = (bf16[128,2048]{1,0:T(8,128)(2,1)}, bf16[128,2048]{1,0:T(8,128)(2,1)}, u32[]{:S(2)}, u32[]{:S(2)}) collective-permute-start(bf16[128,2048]{1,0:T(8,128)(2,1)} %get-tuple-element.228), channel_id=1, source_target_pairs={{16,0},{0,1},{17,16},{1,17},{18,2},{2,3},{19,18},{3,19},{20,4},{4,... | collective-permute-start | bytes 1572872 | tf_op jit(solution)/shard_map/ppermute | solution.py:988
  364.6 41.9 %collective-permute-start.41 = (bf16[128,2048]{1,0:T(8,128)(2,1)}, bf16[128,2048]{1,0:T(8,128)(2,1)}, u32[]{:S(2)}, u32[]{:S(2)}) collective-permute-start(bf16[128,2048]{1,0:T(8,128)(2,1)} %get-tuple-element.227), channel_id=1, source_target_pairs={{0,0},{16,1},{1,16},{17,17},{2,2},{18,3},{3,18},{19,19},{4,4},{20,... | collective-permute-start | bytes 1572872 | tf_op jit(solution)/shard_map/ppermute | solution.py:987
  376.1 51.1 %collective-permute-start.45 = (bf16[528,512]{1,0:T(8,128)(2,1)S(1)}, bf16[528,512]{1,0:T(8,128)(2,1)S(1)}, u32[]{:S(2)}, u32[]{:S(2)}) collective-permute-start(bf16[528,512]{1,0:T(8,128)(2,1)S(1)} %get-tuple-element.226), channel_id=1, source_target_pairs={{16,0},{0,1},{17,16},{1,17},{18,2},{2,3},{19,18},{3,19},{20,4},{4,... | collective-permute-start | bytes 1622024 | tf_op jit(solution)/shard_map/ppermute | solution.py:988
  376.2 51.1 %collective-permute-start.44 = (bf16[528,512]{1,0:T(8,128)(2,1)S(1)}, bf16[528,512]{1,0:T(8,128)(2,1)}, u32[]{:S(2)}, u32[]{:S(2)}) collective-permute-start(bf16[528,512]{1,0:T(8,128)(2,1)S(1)} %get-tuple-element.225), channel_id=1, source_target_pairs={{0,0},{16,1},{1,16},{17,17},{2,2},{18,3},{3,18},{19,19},{4,4},{20,... | collective-permute-start | bytes 1622024 | tf_op jit(solution)/shard_map/ppermute | solution.py:987
  401.6 34.5 %all-to-all-start.1 = ((bf16[8,16,2304]{2,1,0:T(8,128)(2,1)}), bf16[8,16,2304]{2,1,0:T(8,128)(2,1)S(1)}, u32[]{:S(2)}, u32[]{:S(2)}) async-start(bf16[8,16,2304]{2,1,0:T(8,128)(2,1)} %broadcast_in_dim.12), calls=%async_computation.1 | async-start | bytes 1179648 | tf_op jit(solution)/shard_map/all_to_all | solution.py:1005
  (62 other events, 831.9 us)

commit v2 on v1

v2 whole, which is shorter than its diff:
```python
import functools

import jax
import jax.numpy as jnp
from jax import lax
from jax.experimental import pallas as pl
from jax.experimental.pallas import tpu as pltpu
from jax.sharding import Mesh
from jax.sharding import PartitionSpec as P

HEADS = 8
EPS = 1e-06
LANES = 128
VEC = 64
TAIL = 16
NEG = -1e30
f32 = jnp.float32
bf16 = jnp.bfloat16
i32 = jnp.int32
NN = (((1,), (0,)), ((), ()))
NT = (((1,), (1,)), ((), ()))
TN = (((0,), (0,)), ((), ()))
DEVICE = ("hi", "lo", "fy", "core")
GROUP = ("lo", "core")
VMEM_LIMIT = 58 << 20


def dot(a, b, dims):
    return lax.dot_general(a, b, dims, preferred_element_type=f32)


def pieces(value, count):
    parts = []
    for _ in range(count):
        part = value.astype(bf16)
        parts.append(part)
        value = value - part.astype(f32)
    return parts


def iota(shape, axis):
    return lax.broadcasted_iota(i32, shape, axis)


def relative_expert(place, shift, experts):
    other = jnp.bitwise_xor(place, shift)
    return (other & 1) * (experts // 2) + (other >> 1)


def router_order(place, experts):
    row, col = iota((LANES, LANES), 0), iota((LANES, LANES), 1)
    return jnp.where((row == relative_expert(place, col, experts)) & (col < experts), 1.0, 0.0).astype(bf16)


def norm_stats(matrix):
    centred = matrix - jnp.mean(matrix, axis=1, keepdims=True)
    inverse = lax.rsqrt(jnp.mean(centred * centred, axis=1, keepdims=True) + EPS)
    return centred * inverse, inverse


def norm_back(upstream, gain, hat, inverse):
    scaled = upstream * gain
    spread = (
        scaled
        - jnp.mean(scaled, axis=1, keepdims=True)
        - hat * jnp.mean(scaled * hat, axis=1, keepdims=True)
    )
    return spread * inverse


def softmax_lanes(logits, experts):
    logits = jnp.where(iota(logits.shape, 1) < experts, logits, NEG)
    top = jnp.max(logits, axis=1, keepdims=True)
    weight = jnp.exp(logits - top)
    return weight / jnp.sum(weight, axis=1, keepdims=True)


def gelu_pair(value):
    bell = jnp.exp(value * value * -0.5)
    t = 1.0 / (1.0 + jnp.abs(value) * (0.3275911 * 0.7071067811865476))
    poly = t * (
        0.127414796 + t * (-0.142248368 + t * (0.7107068705 + t * (-0.7265760135 + t * 0.5307027145)))
    )
    lower = poly * bell
    phi = jnp.where(value >= 0, 1.0 - lower, lower)
    return value * phi, phi + value * (bell * 0.3989422804014327)


def whole(shape):
    return pl.BlockSpec(shape, lambda *_: (0,) * len(shape))


def params(**extra):
    return pltpu.CompilerParams(vmem_limit_bytes=VMEM_LIMIT, **extra)


def cost(micros):
    return pl.CostEstimate(flops=int(micros * 1e9), bytes_accessed=0, transcendentals=0)


def pack_kernel(spot_ref, wqkv, wout, router, *rest):
    vectors, (w1, w2, b1, b2, pack_ref, pay_ref, spread, tail) = rest[:-8], rest[-8:]
    part, wide = wqkv.shape
    width, hidden = wout.shape[1], w2.shape[0]
    pack_ref[:, 0:wide] = wqkv[...]
    pack_ref[:, wide : wide + width] = wout[...]
    spread[...] = jnp.zeros_like(spread)
    spread[0 : router.shape[0], :] = router[...].astype(f32)
    for index, ref in enumerate(vectors):
        spread[VEC + index : VEC + index + 1, :] = ref[...].astype(f32)
    columns = spread[...].T
    pack_ref[:, wide + width :] = columns.astype(bf16)
    pay_ref[0:hidden] = w2[...]
    tail[...] = jnp.zeros_like(tail)
    tail[0:1, 0 : b1.shape[1]] = b1[...].astype(f32)
    copies = jnp.concatenate([b2[...].astype(f32)] * (width // part), axis=1)
    tail[1:2] = jnp.where(iota((1, width), 1) // part == spot_ref[0], copies, 0.0)
    tall = hidden + TAIL
    pay_ref[hidden:tall] = tail[...].astype(bf16)
    for index in range(width // part):
        block = w1[:, index * hidden : (index + 1) * hidden]
        if hidden < width:
            block = jnp.concatenate([block, jnp.zeros((part, width - hidden), bf16)], axis=1)
        pay_ref[tall + index * part : tall + (index + 1) * part] = block


def pack_parameters(spot, w_qkv, w_out, w_router, vectors, w1, w2, b1, b2):
    part, width = w_out.shape
    hidden = w2.shape[0]
    operands = [w_qkv, w_out, w_router.T, *[v.reshape(1, part) for v in vectors], w1, w2, b1, b2]
    return pl.pallas_call(
        pack_kernel,
        grid=(1,),
        in_specs=[pl.BlockSpec(memory_space=pltpu.SMEM)] + [whole(v.shape) for v in operands],
        out_specs=[whole((part, 4 * width + LANES)), whole((hidden + TAIL + width, width))],
        out_shape=[
            jax.ShapeDtypeStruct((part, 4 * width + LANES), bf16),
            jax.ShapeDtypeStruct((hidden + TAIL + width, width), bf16),
        ],
        scratch_shapes=[pltpu.VMEM((LANES, part), f32), pltpu.VMEM((TAIL, width), f32)],
        compiler_params=params(),
        cost_estimate=cost(0.02),
        name="pack",
    )(spot, *operands)


def one_hot_rows(row, cap):
    slots = iota((cap, row.shape[1]), 0).astype(f32)
    return jnp.where(slots == row, 1.0, 0.0).astype(bf16)


def one_hot_cols(column, cap):
    slots = iota((column.shape[0], cap), 1).astype(f32)
    return jnp.where(slots == column, 1.0, 0.0).astype(bf16)


def route_kernel(place_ref, ids_ref, up_ref, post_ref, pos_ref, *rest, cap, stride):
    outs, gathered = rest[:-1], rest[-1]
    experts = post_ref.shape[0]
    images, seq, width = up_ref.shape
    step = pl.program_id(0)

    @pl.when(step == 0)
    def _():
        expert = relative_expert(place_ref[0], iota((experts, stride), 0), experts)
        before = jnp.where(iota((stride, stride), 0) < iota((stride, stride), 1), 1.0, 0.0).astype(bf16)
        carry = jnp.zeros((experts, 1), f32)
        gathered[...] = jnp.zeros_like(gathered)
        for image in range(images):
            ids = ids_ref[:, image * stride : (image + 1) * stride]
            hit = jnp.zeros((experts, stride), jnp.bool_)
            for choice in range(ids_ref.shape[0]):
                hit = hit | (ids[choice : choice + 1] == expert)
            mask = jnp.where(hit, 1.0, 0.0)
            rank = carry + dot(mask.astype(bf16), before, NN)
            carry = carry + jnp.sum(mask, axis=1, keepdims=True)
            slot = jnp.where(hit, rank, -1.0)
            post_ref[:, image * stride : (image + 1) * stride] = slot
            padded = jnp.concatenate([slot, jnp.full((LANES - experts, stride), -1.0, f32)], axis=0)
            pos_ref[image] = padded.T
            gathered[image * stride : image * stride + seq] = up_ref[image]

    hot = one_hot_rows(post_ref[pl.ds(step, 1), :], cap)
    made = dot(hot, gathered[...], NN).astype(bf16)
    for index in range(experts):

        @pl.when(step == index)
        def _():
            outs[index][...] = made


def route(place, ids, grad_output, experts, cap, stride):
    images, seq, width = grad_output.shape
    total = images * stride
    return pl.pallas_call(
        functools.partial(route_kernel, cap=cap, stride=stride),
        grid=(experts,),
        in_specs=[pl.BlockSpec(memory_space=pltpu.SMEM), whole(ids.shape), whole(grad_output.shape)],
        out_specs=[whole((experts, total)), whole((images, stride, LANES))] + [whole((cap, width))] * experts,
        out_shape=[
            jax.ShapeDtypeStruct((experts, total), f32),
            jax.ShapeDtypeStruct((images, stride, LANES), f32),
        ]
        + [jax.ShapeDtypeStruct((cap, width), bf16)] * experts,
        scratch_shapes=[pltpu.VMEM((total, width), bf16)],
        compiler_params=params(),
        cost_estimate=cost(0.02),
        name="route",
    )(place, ids, grad_output)


def dispatch_kernel(post_ref, rows_ref, *outs, cap):
    step = pl.program_id(0)
    hot = one_hot_rows(post_ref[pl.ds(step, 1), :], cap)
    sent = dot(hot, rows_ref[...], NN).astype(bf16)
    for index in range(len(outs)):

        @pl.when(step == index)
        def _():
            outs[index][...] = sent


def dispatch_after_kernel(post_ref, rows_ref, *rest, cap, skip):
    dispatch_kernel(post_ref, rows_ref, *rest[skip:], cap=cap)


def dispatch(post, rows, after, experts, cap):
    width = rows.shape[1]
    return pl.pallas_call(
        functools.partial(dispatch_after_kernel, cap=cap, skip=len(after)),
        grid=(experts,),
        in_specs=[whole(post.shape), whole(rows.shape)] + [pl.BlockSpec(memory_space=pl.ANY)] * len(after),
        out_specs=[whole((cap, width))] * experts,
        out_shape=[jax.ShapeDtypeStruct((cap, width), bf16)] * experts,
        compiler_params=params(),
        cost_estimate=cost(32),
        name="dispatch",
    )(post, rows, *after)


def forward_kernel(spots_ref, tok_ref, *rest, experts, fsdp, later):
    if later:
        pack_ref, old_peak_ref = rest[:2]
        rest = rest[-10:]
    else:
        shards_of, pack_ref = rest[:fsdp], rest[-4]
        rest = rest[-11:-4] + rest[-3:]
    qkv_ref, mixed_ref, hidden_ref, prob_ref, attn_ref, mid_ref, peak_ref, tokens, vectors, router = rest
    _, seq, width = tok_ref.shape
    rows = tokens.shape[0]
    head = width // HEADS
    step = pl.program_id(0)
    wide = 3 * width

    @pl.when(step == 0)
    def _():
        if not later:
            part = shards_of[0].shape[0]
            for index, ref in enumerate(shards_of):
                pack_ref[pl.ds(pl.multiple_of(spots_ref[1 + index] * part, part), part), :] = ref[...]
        misc = pack_ref[:, wide + width :]
        vectors[...] = misc.astype(f32).T
        router[...] = dot(misc, router_order(spots_ref[0], experts), NN).astype(bf16)
        tokens[...] = jnp.zeros_like(tokens)
        peak_ref[...] = old_peak_ref[...] if later else jnp.full_like(peak_ref, NEG)

    def vector(index):
        return vectors[VEC + index : VEC + index + 1, :]

    tokens[0:seq] = tok_ref[0].astype(f32)
    residual = tokens[...]
    hat, _ = norm_stats(residual)
    normed = (hat * vector(0) + vector(1)).astype(bf16)
    projected = dot(normed, pack_ref[:, 0:wide], NN)
    qkv_ref[0, :, 0:width] = ((projected[:, 0:width] + vector(2)).astype(bf16).astype(f32) * head**-0.5).astype(
        bf16
    )
    qkv_ref[0, :, width : 2 * width] = projected[:, width : 2 * width].astype(bf16)
    qkv_ref[0, :, 2 * width :] = (projected[:, 2 * width :] + vector(3)).astype(bf16)
    lane = iota((1, LANES), 1)
    first = lane < head
    halves = (jnp.where(first, 1.0, 0.0).astype(bf16), jnp.where(first, 0.0, 1.0).astype(bf16))
    keys = jnp.where(iota((1, rows), 1) < seq, 0.0, NEG)
    valid = iota((rows, 1), 0) < seq

    def pair(index, peak):
        at = pl.multiple_of(index * LANES, LANES)
        query = qkv_ref[0, :, pl.ds(at, LANES)]
        key = qkv_ref[0, :, pl.ds(width + at, LANES)]
        value = qkv_ref[0, :, pl.ds(2 * width + at, LANES)]
        parts = []
        for half in range(2):
            scores = dot(query * halves[half], key, NT) + keys
            top = jnp.max(scores, axis=1, keepdims=True)
            weight = jnp.exp(scores - top)
            total = jnp.sum(weight, axis=1, keepdims=True)
            number = index * 2 + half
            largest = jnp.max(jnp.where(valid, top, NEG), axis=0, keepdims=True)
            peak = jnp.where(lane == number, largest, peak)
            low = (weight * (1.0 / total)).astype(bf16)
            attn_ref[0, number] = low
            parts.append(dot(low, value, NN))
        mixed_ref[0, :, pl.ds(at, LANES)] = jnp.where(first, parts[0], parts[1]).astype(bf16)
        return peak

    peak = lax.fori_loop(0, HEADS // 2, pair, jnp.full((1, LANES), NEG, f32))
    peak_ref[...] = jnp.maximum(peak_ref[...], peak)
    hidden = residual + dot(mixed_ref[0], pack_ref[:, wide : wide + width], NN) + vector(4)
    hidden_ref[0] = hidden
    hat, _ = norm_stats(hidden)
    mid = hat * vector(5) + vector(6)
    logits = jnp.zeros((rows, LANES), f32)
    for part in pieces(mid, 3):
        logits = logits + dot(part, router[...], NN)
    prob_ref[0] = softmax_lanes(logits, experts)
    mid_ref[0, 0:rows] = mid.astype(bf16)
    mid_ref[0, rows:] = jnp.zeros((mid_ref.shape[1] - rows, width), bf16)


def forward(spots, tokens, shards_of, old, after, at, count, experts, stride, rows):
    images, seq, width = tokens.shape
    later = old is not None
    far = pl.BlockSpec(memory_space=pl.ANY)
    shapes = [
        ((1, rows, 3 * width), bf16),
        ((1, rows, width), bf16),
        ((1, rows, width), f32),
        ((1, rows, LANES), f32),
        ((1, HEADS, rows, rows), bf16),
        ((1, stride, width), bf16),
    ]

    def image(shape):
        return pl.BlockSpec(shape, lambda i: (at + i,) + (0,) * (len(shape) - 1))

    out_specs = [image(shape) for shape, _ in shapes] + [whole((1, LANES))]
    out_shape = [jax.ShapeDtypeStruct((images,) + shape[1:], kind) for shape, kind in shapes]
    out_shape.append(jax.ShapeDtypeStruct((1, LANES), f32))
    operands = [spots, tokens]
    in_specs = [pl.BlockSpec(memory_space=pltpu.SMEM), image((1, seq, width))]
    if later:
        *arrays, peak, pack = old
        aliases = {len(operands) + 2 + index: index for index in range(len(arrays))}
        operands += [pack, peak, *arrays]
        in_specs += [whole(pack.shape), whole(peak.shape)] + [far] * len(arrays)
    else:
        aliases = {}
        packed = (width, shards_of[0].shape[1])
        operands += shards_of
        in_specs += [whole(v.shape) for v in shards_of]
        out_specs.append(whole(packed))
        out_shape.append(jax.ShapeDtypeStruct(packed, bf16))
    outputs = pl.pallas_call(
        functools.partial(forward_kernel, experts=experts, fsdp=len(shards_of), later=later),
        grid=(count,),
        in_specs=in_specs + [far] * len(after),
        out_specs=out_specs,
        out_shape=out_shape,
        scratch_shapes=[
            pltpu.VMEM((rows, width), f32),
            pltpu.VMEM((LANES, width), f32),
            pltpu.VMEM((width, LANES), bf16),
        ],
        input_output_aliases=aliases,
        compiler_params=params(),
        cost_estimate=cost(20 * count if later else 0.02),
        name="attend",
    )(*operands, *after)
    return [*outputs, pack] if later else outputs


def expert_kernel(place_ref, *refs, cap, group, first, last, experts, fsdp, split, skip):
    taken = iter(refs)

    def take(number):
        return [next(taken) for _ in range(number)]

    count = len(group)
    rows_in, ups_in = take(count), take(count)
    pays, misc = take(fsdp), next(taken)
    old = [] if first else take(3)
    take(skip)
    row_back, made_ref = take(count), next(taken)
    out1, out2, *out3 = take(4 if split else 2) if split or not last else (None, next(taken))
    rows, ups, gates, acc_row, acc_out, shift2, bias2, gated, sems, w1s, w2s, sems_w = take(12)
    step = pl.program_id(0)
    width = rows.shape[1]
    tile = w1s.shape[2]
    tall = tile + TAIL
    chunk = width // fsdp

    @pl.when(step == 0)
    def _():
        loads = []
        for index, ref in enumerate(pays):
            at = place_ref[2 + index]
            loads.append(pltpu.make_async_copy(ref.at[0:tall], w2s.at[at], sems_w.at[index, fsdp]))
            for block in range(fsdp):
                start = tall + block * chunk
                loads.append(
                    pltpu.make_async_copy(
                        ref.at[start : start + chunk, 0:tile],
                        w1s.at[block, pl.ds(pl.multiple_of(at * chunk, chunk), chunk)],
                        sems_w.at[index, block],
                    )
                )
        for load in loads:
            load.start()
        for index in range(count):
            rows[index * cap : (index + 1) * cap] = rows_in[index][...]
        router = dot(misc[...], router_order(place_ref[0], experts), NN).astype(bf16)
        gate = softmax_lanes(dot(rows[...], router, NN), experts)[:, 0:1]
        gates[...] = jnp.broadcast_to(gate, gates.shape)
        for index in range(count):
            part = slice(index * cap, (index + 1) * cap)
            ups[part] = (ups_in[index][...].astype(f32) * gate[part]).astype(bf16)
        acc_row[...] = jnp.zeros_like(acc_row)
        acc_out[...] = jnp.zeros_like(acc_out)
        bias2[...] = jnp.zeros_like(bias2)
        shift2[...] = jnp.sum(ups[...].astype(f32), axis=0, keepdims=True)
        for load in loads:
            load.wait()

    w1, w2 = w1s.at[step], w2s.at[step]
    tail = w2[tile:tall].astype(f32)
    bias2[...] += tail[1:2]
    x, up = rows[...], ups[...]
    value, slope = gelu_pair(dot(x, w1[...], NN) + tail[0:1, 0:tile])
    act = value.astype(bf16)
    acc_out[...] += dot(act, w2[0:tile], NN)
    raw = slope * dot(up, w2[0:tile], NT)
    pre = raw.astype(bf16)
    acc_row[...] += dot(pre, w1[...], NT)
    part1 = dot(x, pre, TN)
    part2 = dot(act, up, TN)
    shift1 = jnp.sum(pre.astype(f32), axis=0, keepdims=True)
    if tile < width:
        shift1 = jnp.concatenate([shift1, jnp.zeros((1, width - tile), f32)], axis=1)
    place = iota((TAIL, width), 0)
    sums = jnp.where(place == 0, shift1, jnp.where(place == 1, shift2[...], 0.0))
    if not first:
        part1, part2, sums = old[1][...] + part1, old[2][0, 0:tile] + part2, old[2][0, tile:] + sums
    if last:
        if tile < width:
            part1 = jnp.concatenate([part1, jnp.zeros((width, width - tile), f32)], axis=1)
        if split:
            for ref, fy in ((out1, place_ref[1]), (out2, 1 - place_ref[1])):

                @pl.when((step >> 1) == fy)
                def _():
                    ref[step & 1, 0:tile] = part2.astype(bf16)
                    ref[step & 1, tile:tall] = sums.astype(bf16)

            at = pl.multiple_of(step * chunk, TAIL)
            for index in range(fsdp):
                block = part1[index * chunk : (index + 1) * chunk].astype(bf16)
                for ref, fy in ((out3[0], place_ref[1]), (out3[1], 1 - place_ref[1])):

                    @pl.when(index // 2 == fy)
                    def _():
                        ref[index % 2, pl.ds(at, chunk), :] = block

        else:
            at = pl.multiple_of(tall + step * chunk, TAIL)
            out2[step, 0:tile] = part2.astype(bf16)
            out2[step, tile:tall] = sums.astype(bf16)
            for index in range(fsdp):
                out2[index, pl.ds(at, chunk), :] = part1[index * chunk : (index + 1) * chunk].astype(bf16)
    else:
        out1[...] = part1
        out2[0, 0:tile] = part2
        out2[0, tile:] = sums

    @pl.when(step == pl.num_programs(0) - 1)
    def _():
        copies = []
        for index, shift in enumerate(group):
            part = slice(index * cap, (index + 1) * cap)
            made = acc_out[part] + bias2[...]
            gate = gates[part, 0:1]
            gated[index] = (made * gate).astype(bf16)
            copies.append(
                pltpu.make_async_copy(gated.at[index], made_ref.at[place_ref[0] ^ shift], sems.at[index])
            )
            copies[-1].start()
            row_back[index][0:cap] = acc_row[part].astype(bf16)
            effect = jnp.sum(made * ups_in[index][...].astype(f32), axis=1, keepdims=True) * gate
            effect = jnp.concatenate([effect, jnp.zeros((width - cap, 1), f32)], axis=0)
            line = jnp.broadcast_to(effect, (width, LANES)).T[0:1]
            end = jnp.zeros((TAIL, width), f32)
            for order, piece in enumerate(pieces(line, 3)):
                end = jnp.where(place == order, piece.astype(f32), end)
            row_back[index][cap : cap + TAIL] = end.astype(bf16)
        for copy in copies:
            copy.wait()


def expert_call(spots, rows, ups, pays, pack, old, after, group, cap, experts, last):
    count = len(group)
    first = old is None
    fsdp = len(pays)
    high, width = pays[0].shape
    tall = high - width
    tile = tall - TAIL
    total = count * cap
    split = last and fsdp == 4
    column = pl.BlockSpec((width, tile), lambda h, _: (0, h))
    line = pl.BlockSpec((1, tall, width), lambda h, _: (h, 0, 0))
    far = pl.BlockSpec(memory_space=pl.ANY)
    if split:
        grads = [(2, tall, width)] * 2 + [(2, width, width)] * 2
    else:
        grads = [(fsdp, high, width)]

    operands = [spots, *rows, *ups, *pays, pack]
    aliases = {}
    if not first:
        aliases = {len(operands): count}
        operands += list(old)
    return pl.pallas_call(
        functools.partial(
            expert_kernel,
            cap=cap,
            group=group,
            first=first,
            last=last,
            experts=experts,
            fsdp=fsdp,
            split=split,
            skip=len(after),
        ),
        grid_spec=pltpu.PrefetchScalarGridSpec(
            num_scalar_prefetch=1,
            grid=(fsdp,),
            in_specs=[whole((cap, width))] * (2 * count)
            + [far] * fsdp
            + [pl.BlockSpec((width, LANES), lambda h, _: (0, 4 * width // LANES))]
            + ([] if first else [far, column, line])
            + [far] * len(after),
            out_specs=[whole((cap + TAIL, width))] * count
            + [far]
            + ([whole(v) for v in grads] if last else [column, line]),
            scratch_shapes=[pltpu.VMEM((total, width), bf16)] * 2
            + [pltpu.VMEM((total, LANES), f32)]
            + [pltpu.VMEM((total, width), f32)] * 2
            + [pltpu.VMEM((1, width), f32)] * 2
            + [pltpu.VMEM((count, cap, width), bf16), pltpu.SemaphoreType.DMA((count,))]
            + [pltpu.VMEM((fsdp, width, tile), bf16), pltpu.VMEM((fsdp, tall, width), bf16)]
            + [pltpu.SemaphoreType.DMA((fsdp, fsdp + 1))],
        ),
        out_shape=[jax.ShapeDtypeStruct((cap + TAIL, width), bf16)] * count
        + [jax.ShapeDtypeStruct((experts, cap, width), bf16)]
        + (
            [jax.ShapeDtypeStruct(v, bf16) for v in grads]
            if last
            else [
                jax.ShapeDtypeStruct((width, tile * fsdp), f32),
                jax.ShapeDtypeStruct((fsdp, tall, width), f32),
            ]
        ),
        input_output_aliases=aliases,
        compiler_params=params(),
        cost_estimate=cost(96),
        name="expert",
    )(*operands, *after)


def middle_kernel(
    place_ref, up_ref, wout_ref, misc_ref, pos_ref, mixed_ref, hidden_ref, prob_ref, *rest, cap, experts
):
    backs = rest[:experts]
    hidden_grad_ref, mixed_grad_ref, sums_ref, padded, vectors, router, shifts, acc_out, acc_router = rest[-9:]
    _, seq, width = up_ref.shape
    rows = padded.shape[0]
    step = pl.program_id(0)

    @pl.when(step == 0)
    def _():
        vectors[...] = misc_ref[...].astype(f32).T
        router[...] = dot(misc_ref[...], router_order(place_ref[0], experts), NN).astype(bf16)
        padded[...] = jnp.zeros_like(padded)
        shifts[...] = jnp.zeros_like(shifts)
        acc_out[...] = jnp.zeros_like(acc_out)
        acc_router[...] = jnp.zeros_like(acc_router)

    def vector(index):
        return vectors[VEC + index : VEC + index + 1, :]

    def shift(index, value):
        shifts[index : index + 1, :] += jnp.sum(value, axis=0, keepdims=True)

    lane = iota((1, LANES), 1)
    places = pos_ref[0, 0:rows, :]
    slot_sum = jnp.zeros((rows, width), f32)
    effect = jnp.zeros((rows, LANES), f32)
    for index in range(experts):
        hot = one_hot_cols(places[:, index : index + 1], cap)
        slot_sum = slot_sum + dot(hot, backs[index][0:cap], NN)
        parts = dot(hot, backs[index][cap : cap + TAIL, 0:cap], NT)
        effect = jnp.where(lane == index, jnp.sum(parts, axis=1, keepdims=True), effect)
    prob = prob_ref[0]
    logit_grad = effect - prob * jnp.sum(effect, axis=1, keepdims=True)
    logit_parts = pieces(logit_grad, 2)
    mid_grad = slot_sum
    for part in logit_parts:
        mid_grad = mid_grad + dot(part, router[...], NT)
    padded[0:seq] = up_ref[0].astype(f32)
    hat, inverse = norm_stats(hidden_ref[0])
    mid_parts = pieces(hat * vector(5) + vector(6), 2)
    acc_router[...] += (
        dot(logit_parts[0], mid_parts[0], TN)
        + dot(logit_parts[0], mid_parts[1], TN)
        + dot(logit_parts[1], mid_parts[0], TN)
    )
    shift(5, mid_grad * hat)
    shift(6, mid_grad)
    hidden_grad = padded[...] + norm_back(mid_grad, vector(5), hat, inverse)
    hidden_grad_ref[0] = hidden_grad
    branch = hidden_grad.astype(bf16)
    shift(4, branch.astype(f32))
    acc_out[...] += dot(mixed_ref[0], branch, TN)
    mixed_grad_ref[0] = dot(branch, wout_ref[...], NT).astype(bf16)

    @pl.when(step == pl.num_programs(0) - 1)
    def _():
        sums_ref[:, 0:width] = acc_out[...]
        ordered = dot(router_order(place_ref[0], experts), acc_router[...].astype(bf16), NN)
        spare = jnp.concatenate(
            [ordered[0:VEC], shifts[...], jnp.zeros((LANES - VEC - shifts.shape[0], width), f32)], axis=0
        )
        sums_ref[:, width:] = spare.T


def middle(place, grad_output, pack, pos, saved, backs, after, cap, experts):
    images, seq, width = grad_output.shape
    _, mixed, hidden, prob, _ = saved
    rows = mixed.shape[1]

    def image(shape):
        return pl.BlockSpec((1,) + shape, lambda i: (i, 0, 0))

    return pl.pallas_call(
        functools.partial(middle_kernel, cap=cap, experts=experts),
        grid=(images,),
        in_specs=[
            pl.BlockSpec(memory_space=pltpu.SMEM),
            image((seq, width)),
            pl.BlockSpec((width, width), lambda i: (0, 3)),
            pl.BlockSpec((width, LANES), lambda i: (0, 4 * width // LANES)),
            image((pos.shape[1], LANES)),
            image((rows, width)),
            image((rows, width)),
            image((rows, LANES)),
        ]
        + [whole((cap + TAIL, width))] * experts
        + [pl.BlockSpec(memory_space=pl.ANY)] * len(after),
        out_specs=[image((rows, width)), image((rows, width)), whole((width, width + LANES))],
        out_shape=[
            jax.ShapeDtypeStruct((images, rows, width), f32),
            jax.ShapeDtypeStruct((images, rows, width), bf16),
            jax.ShapeDtypeStruct((width, width + LANES), f32),
        ],
        scratch_shapes=[
            pltpu.VMEM((rows, width), f32),
            pltpu.VMEM((LANES, width), f32),
            pltpu.VMEM((width, LANES), bf16),
            pltpu.VMEM((8, width), f32),
            pltpu.VMEM((width, width), f32),
            pltpu.VMEM((LANES, width), f32),
        ],
        compiler_params=params(),
        cost_estimate=cost(0.02),
        name="middle",
    )(place, grad_output, pack, pack, pos, mixed, hidden, prob, *backs, *after)


def backward_kernel(
    spots_ref, tok_ref, qkv_ref, attn_ref, mixed_grad_ref, *rest, head_rows, members
):
    sums_ref, peak_ref = rest[:2]
    qkv_grad_ref, keep_ref, give_ref, padded, acc_qkv, columns, spare, misc = rest[-8:]
    _, seq, width = tok_ref.shape
    rows = padded.shape[0]
    head = width // HEADS
    wide = 3 * width
    step = pl.program_id(0)

    @pl.when(step == 0)
    def _():
        padded[...] = jnp.zeros_like(padded)
        acc_qkv[...] = jnp.zeros_like(acc_qkv)
        columns[...] = jnp.zeros_like(columns)

    lane = iota((1, LANES), 1)
    first = lane < head
    halves = (jnp.where(first, 1.0, 0.0).astype(bf16), jnp.where(first, 0.0, 1.0).astype(bf16))

    def pair(index, carry):
        at = pl.multiple_of(index * LANES, LANES)
        query = qkv_ref[0, :, pl.ds(at, LANES)]
        key = qkv_ref[0, :, pl.ds(width + at, LANES)]
        value = qkv_ref[0, :, pl.ds(2 * width + at, LANES)]
        up = mixed_grad_ref[0, :, pl.ds(at, LANES)]
        made = []
        for half in range(2):
            low = attn_ref[0, index * 2 + half]
            weight = low.astype(f32)
            value_grad = dot(low, up, TN)
            spread = weight * dot(up * halves[half], value, NT)
            score_grad = (spread - weight * jnp.sum(spread, axis=1, keepdims=True)).astype(bf16)
            made.append((dot(score_grad, key, NN) * head**-0.5, dot(score_grad, query, TN), value_grad))
        for index_of, (left, right) in enumerate(zip(*made)):
            qkv_grad_ref[0, :, pl.ds(index_of * width + at, LANES)] = jnp.where(first, left, right).astype(bf16)
        return carry

    lax.fori_loop(0, HEADS // 2, pair, 0)
    columns[...] += jnp.sum(qkv_grad_ref[0].astype(f32), axis=0, keepdims=True)
    padded[0:seq] = tok_ref[0].astype(f32)
    hat, _ = norm_stats(padded[...])
    acc_qkv[...] += dot(hat.astype(bf16), qkv_grad_ref[0], TN)
    part = keep_ref.shape[1]

    @pl.when(step == pl.num_programs(0) - 1)
    def _():
        line = iota((LANES, width), 0)
        flat = columns[...]
        grown = jnp.where(line == VEC + 2, flat[:, 0:width], 0.0)
        grown = jnp.where(line == VEC + 3, flat[:, 2 * width :], grown)
        misc[...] = sums_ref[:, width:] + grown.T
        spare[...] = jnp.zeros_like(spare)
        number = wide // LANES
        for order, piece in enumerate(pieces(flat, 3)):
            value = piece.astype(f32)
            for index in range(number):
                at = order * number + index
                spare[at : at + 1, :] = value[:, index * LANES : (index + 1) * LANES]
        if members:
            top = jnp.where(lane < HEADS, peak_ref[...], 0.0)
            rows_of = jnp.zeros((TAIL, LANES), f32)
            for order, piece in enumerate(pieces(jnp.broadcast_to(top, (TAIL, LANES)), 3)):
                move = jnp.where(iota((LANES, LANES), 1) == iota((LANES, LANES), 0) + order * HEADS, 1.0, 0.0)
                rows_of = rows_of + dot(piece, move.astype(bf16), NN)
            spare[pl.ds(head_rows + spots_ref[1], 1), :] = rows_of[0:1]
        extra = spare[...].astype(bf16)
        for fy in range(keep_ref.shape[0]):
            for ref, core in ((keep_ref, spots_ref[0]), (give_ref, 1 - spots_ref[0])):
                at = pl.multiple_of((2 * fy + core) * part, part)
                ref[fy, :, 0:wide] = acc_qkv[pl.ds(at, part), :].astype(bf16)
                ref[fy, :, wide : wide + width] = sums_ref[pl.ds(at, part), 0:width].astype(bf16)
                ref[fy, :, wide + width : wide + width + LANES] = misc[pl.ds(at, part), :].astype(bf16)
                ref[fy, :, wide + width + LANES :] = extra


def backward(spots, tokens, saved, mixed_grad, sums, peak, after, ways, part, head_rows, members):
    images, seq, width = tokens.shape
    qkv, attn = saved[0], saved[-1]
    rows = qkv.shape[1]
    wide = 4 * width + 2 * LANES

    def image(shape):
        return pl.BlockSpec((1,) + shape, lambda i: (i,) + (0,) * len(shape))

    return pl.pallas_call(
        functools.partial(backward_kernel, head_rows=head_rows, members=members),
        grid=(images,),
        in_specs=[
            pl.BlockSpec(memory_space=pltpu.SMEM),
            image((seq, width)),
            image((rows, 3 * width)),
            image((HEADS, rows, rows)),
            image((rows, width)),
            whole(sums.shape),
            whole(peak.shape),
        ]
        + [pl.BlockSpec(memory_space=pl.ANY)] * len(after),
        out_specs=[image((rows, 3 * width)), whole((ways, part, wide)), whole((ways, part, wide))],
        out_shape=[
            jax.ShapeDtypeStruct((images, rows, 3 * width), bf16),
            jax.ShapeDtypeStruct((ways, part, wide), bf16),
            jax.ShapeDtypeStruct((ways, part, wide), bf16),
        ],
        scratch_shapes=[
            pltpu.VMEM((rows, width), f32),
            pltpu.VMEM((width, 3 * width), f32),
            pltpu.VMEM((1, 3 * width), f32),
            pltpu.VMEM((part, LANES), f32),
            pltpu.VMEM((width, LANES), f32),
        ],
        compiler_params=params(),
        cost_estimate=cost(0.05),
        name="attend_back",
    )(spots, tokens, qkv, attn, mixed_grad, sums, peak, *after)


def first_kernel(tok_ref, qkv_grad_ref, wqkv_ref, misc_ref, hidden_grad_ref, grad_ref, padded, gain):
    _, seq, width = tok_ref.shape

    @pl.when(pl.program_id(0) == 0)
    def _():
        gain[...] = misc_ref[...].astype(f32).T[VEC : VEC + 1]
        padded[...] = jnp.zeros_like(padded)

    in_grad = dot(qkv_grad_ref[0], wqkv_ref[...], NT)
    padded[0:seq] = tok_ref[0].astype(f32)
    hat, inverse = norm_stats(padded[...])
    grad_ref[0] = (hidden_grad_ref[0] + norm_back(in_grad, gain[...], hat, inverse))[0:seq]


def first_norm(tokens, qkv_grad, pack, hidden_grad):
    images, seq, width = tokens.shape
    rows = qkv_grad.shape[1]

    def image(shape):
        return pl.BlockSpec((1,) + shape, lambda i: (i, 0, 0))

    return pl.pallas_call(
        first_kernel,
        grid=(images,),
        in_specs=[
            image((seq, width)),
            image((rows, 3 * width)),
            pl.BlockSpec((width, 3 * width), lambda i: (0, 0)),
            pl.BlockSpec((width, LANES), lambda i: (0, 4 * width // LANES)),
            image((rows, width)),
        ],
        out_specs=image((seq, width)),
        out_shape=jax.ShapeDtypeStruct((images, seq, width), f32),
        scratch_shapes=[pltpu.VMEM((rows, width), f32), pltpu.VMEM((1, width), f32)],
        compiler_params=params(),
        cost_estimate=cost(0.02),
        name="first_norm",
    )(tokens, qkv_grad, pack, pack, hidden_grad)


def output_kernel(place_ref, pos_ref, hidden_ref, made_ref, out_ref):
    experts, cap, _ = made_ref.shape
    seq = out_ref.shape[1]
    total = hidden_ref[0]
    places = pos_ref[0, 0 : total.shape[0], :]
    for index in range(experts):
        total = total + dot(one_hot_cols(places[:, index : index + 1], cap), made_ref[place_ref[0] ^ index], NN)
    out_ref[0] = total[0:seq].astype(bf16)


def combine_output(place, pos, hidden, made, seq):
    images, rows, width = hidden.shape

    def image(shape):
        return pl.BlockSpec((1,) + shape, lambda i: (i, 0, 0))

    return pl.pallas_call(
        output_kernel,
        grid=(images,),
        in_specs=[
            pl.BlockSpec(memory_space=pltpu.SMEM),
            image((pos.shape[1], LANES)),
            image((rows, width)),
            whole(made.shape),
        ],
        out_specs=image((seq, width)),
        out_shape=jax.ShapeDtypeStruct((images, seq, width), bf16),
        compiler_params=params(),
        cost_estimate=cost(0.02),
        name="combine",
    )(place, pos, hidden, made)


def finish_kernel(slot_ref, *refs, number, head_rows, members):
    parts, (own_ref, limit_ref, peak_ref) = refs[:number], refs[number : number + 3]
    qkv_ref, out_ref, misc_ref, vec_ref, clip_ref, total_ref = refs[number + 3 :]
    part = own_ref.shape[0]
    for shift, ref in enumerate(parts):
        size = part // number
        total_ref[pl.ds(pl.multiple_of((slot_ref[0] ^ shift) * size, size), size), :] = ref[...]
    width = out_ref.shape[1]
    wide = 3 * width
    number = wide // LANES
    base = total_ref[:, 0:wide].astype(f32)
    extra = total_ref[:, wide + width + LANES :].astype(f32)
    weight = own_ref[:, 0:wide].astype(f32)
    columns = [sum(extra[k * number + i : k * number + i + 1] for k in range(3)) for i in range(number)]
    columns = jnp.concatenate(columns, axis=1)
    own = own_ref[:, wide + width :].astype(f32)
    gain, bias = own[:, VEC : VEC + 1], own[:, VEC + 1 : VEC + 2]
    qkv_ref[...] = base * gain + bias * columns
    out_ref[...] = total_ref[:, wide : wide + width].astype(f32)
    misc = total_ref[:, wide + width : wide + width + LANES].astype(f32)
    lane = iota((1, LANES), 1)
    misc = jnp.where(lane == VEC, jnp.sum(base * weight, axis=1, keepdims=True), misc)
    misc = jnp.where(lane == VEC + 1, jnp.sum(columns * weight, axis=1, keepdims=True), misc)
    misc = misc.T
    vec_ref[...] = misc[VEC : VEC + 8]
    misc_ref[...] = misc[0 : misc_ref.shape[0]]
    if members:
        move = jnp.where(
            (iota((LANES, LANES), 0) % HEADS == iota((LANES, LANES), 1)) & (iota((LANES, LANES), 0) < 3 * HEADS),
            1.0,
            0.0,
        )
        peaks = dot(total_ref[head_rows : head_rows + members, wide + width + LANES :], move.astype(bf16), NN)
        peak = jnp.max(peaks, axis=0, keepdims=True)
    else:
        peak = peak_ref[...]
    limit = limit_ref[...]
    root = jnp.sqrt(limit / jnp.maximum(peak, limit))
    place = iota((1, width), 1) // (width // HEADS)
    scale = jnp.zeros((1, width), f32)
    for index in range(HEADS):
        scale = jnp.where(place == index, root[:, index : index + 1], scale)
    clip_ref[:, 0:width] = (weight[:, 0:width] * scale).astype(bf16)
    clip_ref[:, width : 2 * width] = (weight[:, width : 2 * width] * scale).astype(bf16)
    clip_ref[:, 2 * width :] = own_ref[:, 2 * width : wide]


def finish(slot, total, own, limit, peak, width, experts, head_rows, members):
    part = own.shape[0]
    operands = [*total, own, limit, peak]
    shapes = [(part, 3 * width), (part, width), (experts, part), (8, part), (part, 3 * width)]
    return pl.pallas_call(
        functools.partial(finish_kernel, number=len(total), head_rows=head_rows, members=members),
        grid=(1,),
        in_specs=[pl.BlockSpec(memory_space=pltpu.SMEM)] + [whole(v.shape) for v in operands],
        out_specs=[whole(v) for v in shapes],
        out_shape=[jax.ShapeDtypeStruct(v, bf16 if i == 4 else f32) for i, v in enumerate(shapes)],
        scratch_shapes=[pltpu.VMEM((part, total[0].shape[1]), bf16)],
        compiler_params=params(),
        cost_estimate=cost(0.02),
        name="finish",
    )(slot, *operands)


def half_sums_kernel(high_ref, keep_ref, got_ref, *rest):
    straight_ref, crossed_ref = rest[-2:]
    for ref, core in ((straight_ref, high_ref[0]), (crossed_ref, 1 - high_ref[0])):
        ref[...] = (keep_ref[core].astype(f32) + got_ref[core].astype(f32)).astype(bf16)


def half_sums(high, keep, got, after, micros):
    shape = keep.shape[1:]
    return pl.pallas_call(
        half_sums_kernel,
        grid=(1,),
        in_specs=[pl.BlockSpec(memory_space=pltpu.SMEM), whole(keep.shape), whole(got.shape)]
        + [pl.BlockSpec(memory_space=pl.ANY)] * len(after),
        out_specs=[whole(shape)] * 2,
        out_shape=[jax.ShapeDtypeStruct(shape, bf16)] * 2,
        compiler_params=params(),
        cost_estimate=cost(micros),
        name="half_sums",
    )(high, keep, got, *after)


def home_sums_kernel(spot_ref, one, two, three, four, _, w1_ref, w2_ref, b1_ref, b2_ref):
    tile, width = w2_ref.shape
    part = w1_ref.shape[0]
    w2_ref[...] = one[0:tile].astype(f32) + two[0:tile].astype(f32)
    edge = one[tile:].astype(f32) + two[tile:].astype(f32)
    b1_ref[...] = edge[0:1, 0:tile]
    b2_ref[...] = sum(
        jnp.where(spot_ref[0] == index, edge[1:2, index * part : (index + 1) * part], 0.0)
        for index in range(width // part)
    )
    for index in range(w1_ref.shape[1] // tile):
        rows = slice(index * part, (index + 1) * part)
        total = three[rows].astype(f32) + four[rows].astype(f32)
        w1_ref[:, index * tile : (index + 1) * tile] = total[:, 0:tile]


def home_sums(spot, second, first, after, tile, part, fsdp):
    width = second[0].shape[1]
    shapes = [(part, tile * fsdp), (tile, width), (1, tile), (1, part)]
    operands = [*second, *first]
    return pl.pallas_call(
        home_sums_kernel,
        grid=(1,),
        in_specs=[pl.BlockSpec(memory_space=pltpu.SMEM)]
        + [whole(v.shape) for v in operands]
        + [pl.BlockSpec(memory_space=pl.ANY)],
        out_specs=[whole(v) for v in shapes],
        out_shape=[jax.ShapeDtypeStruct(v, f32) for v in shapes],
        compiler_params=params(),
        cost_estimate=cost(0.02),
        name="home_sums",
    )(spot, *operands, after)


def add_halves_kernel(fy_ref, keep_ref, got_ref, *rest):
    mine_ref, theirs_ref = rest[-2:]
    for ref, half in ((mine_ref, fy_ref[0]), (theirs_ref, 1 - fy_ref[0])):
        ref[...] = (keep_ref[half].astype(f32) + got_ref[half].astype(f32)).astype(bf16)


def add_halves(fy, keep, got, after):
    shape = keep.shape[1:]
    return pl.pallas_call(
        add_halves_kernel,
        grid=(1,),
        in_specs=[pl.BlockSpec(memory_space=pltpu.SMEM), whole(keep.shape), whole(got.shape)]
        + [pl.BlockSpec(memory_space=pl.ANY)] * len(after),
        out_specs=[whole(shape)] * 2,
        out_shape=[jax.ShapeDtypeStruct(shape, bf16)] * 2,
        compiler_params=params(),
        cost_estimate=cost(0.02),
        name="add_halves",
    )(fy, keep, got, *after)


def split_rows_kernel(slot_ref, mine_ref, got_ref, *refs, skip):
    outs, total = refs[skip:-1], refs[-1]
    total[...] = (mine_ref[...].astype(f32) + got_ref[...].astype(f32)).astype(bf16)
    size = outs[0].shape[0]
    for shift, ref in enumerate(outs):
        ref[...] = total[pl.ds(pl.multiple_of((slot_ref[0] ^ shift) * size, size), size), :]


def split_rows(slot, mine, got, after, number):
    part, wide = mine.shape
    shape = (part // number, wide)
    return pl.pallas_call(
        functools.partial(split_rows_kernel, skip=len(after)),
        grid=(1,),
        in_specs=[pl.BlockSpec(memory_space=pltpu.SMEM), whole(mine.shape), whole(got.shape)]
        + [pl.BlockSpec(memory_space=pl.ANY)] * len(after),
        out_specs=[whole(shape)] * number,
        out_shape=[jax.ShapeDtypeStruct(shape, bf16)] * number,
        scratch_shapes=[pltpu.VMEM((part, wide), bf16)],
        compiler_params=params(),
        cost_estimate=cost(0.02),
        name="split_rows",
    )(slot, mine, got, *after)


def add_parts_kernel(*refs):
    parts, out_ref = refs[:-1], refs[-1]
    out_ref[...] = sum(ref[...].astype(f32) for ref in parts).astype(bf16)


def add_parts(parts):
    shape = parts[0].shape
    return pl.pallas_call(
        add_parts_kernel,
        grid=(1,),
        in_specs=[whole(shape)] * len(parts),
        out_specs=whole(shape),
        out_shape=jax.ShapeDtypeStruct(shape, bf16),
        compiler_params=params(),
        cost_estimate=cost(0.02),
        name="add_parts",
    )(*parts)


def swap(value, axis):
    return lax.ppermute(value, axis, [(0, 1), (1, 0)])


def around(value, axis, size):
    return [value] + [
        lax.ppermute(value, axis, [((k + step) % size, k) for k in range(size)]) for step in range(1, size)
    ]


def split_sum(value, axis, size):
    if size != 2:
        return lax.psum_scatter(value, axis, scatter_dimension=0, tiled=False)
    place = lax.axis_index(axis)
    sent = lax.dynamic_index_in_dim(value, 1 - place, 0, keepdims=False)
    kept = lax.dynamic_index_in_dim(value, place, 0, keepdims=False)
    return (kept.astype(f32) + swap(sent, axis).astype(f32)).astype(value.dtype)


def exchange(value, shift, experts):
    return lax.ppermute(value, GROUP, [(k, k ^ shift) for k in range(experts)])


def shift_order(experts):
    def key(shift):
        distance = bin(shift >> 1).count("1")
        return (distance == 0, distance == 1 and shift & 1, distance, shift)

    return sorted(range(experts), key=key)


STRAIGHT = [(0, 0), (1, 2), (2, 1), (3, 3)]
CROSSED = [(0, 2), (1, 0), (2, 3), (3, 1)]
BACK = [(b, a) for a, b in STRAIGHT]
BACK_CROSSED = [(b, a) for a, b in CROSSED]


def shards(
    tokens,
    ln1_gain,
    ln1_bias,
    w_qkv,
    q_bias,
    v_bias,
    w_out,
    out_bias,
    ln2_gain,
    ln2_bias,
    w_router,
    expert_w1,
    expert_b1,
    expert_w2,
    expert_b2,
    route_ids,
    clip_threshold,
    grad_output,
    *,
    experts,
    fsdp,
):
    images, seq, width = tokens.shape
    token_count = images * seq
    ways = fsdp // 2
    cap = (7 * token_count // (2 * experts) + 7) // 8 * 8
    stride = -(-seq // 256) * 256
    rows = -(-seq // 16) * 16
    part = w_qkv.shape[0]
    hidden_part = expert_w2.shape[1]
    high, low, fy, core = (lax.axis_index(name).astype(i32) for name in DEVICE)
    place_ref = (low * 2 + core).reshape(1)
    spot = fy * 2 + core

    vectors = (ln1_gain, ln1_bias, q_bias, v_bias, out_bias, ln2_gain, ln2_bias)
    own, pay = pack_parameters(
        spot.reshape(1), w_qkv, w_out, w_router, vectors, expert_w1[0], expert_w2[0], expert_b1, expert_b2
    )

    near = around(own, "fy", ways)
    far = [swap(own, "core")]
    straight = lax.ppermute(pay, ("hi", "core"), STRAIGHT)

    ids = jnp.pad(route_ids.reshape(images, seq, -1), ((0, 0), (0, stride - seq), (0, 0)), constant_values=-1)
    ids = ids.reshape(images * stride, -1).T
    post, pos, *ups = route(place_ref, ids, grad_output, experts, cap, stride)
    order = shift_order(experts)
    near[1:], post, ups[0] = lax.optimization_barrier((near[1:], post, ups[0]))
    ups = [value if shift == 0 else exchange(value, shift, experts) for shift, value in enumerate(ups)]
    far += [swap(value, "core") for value in near[1:]]
    homes = [((fy + step) % ways) * 2 for step in range(ways)]
    homes = [home + core for home in homes] + [home + 1 - core for home in homes]

    early = max(1, images * 2 // 5)
    spots = jnp.stack([place_ref[0], *homes])
    size = max(1, experts // 4)
    firsts = [ups[shift] for shift in order[:size]]
    begun = list(forward(spots, tokens, near + far, None, [], 0, early, experts, stride, rows))
    pay, straight, begun[0] = lax.optimization_barrier((pay, straight, begun[0]))
    crossed = lax.ppermute(pay, ("hi", "core"), CROSSED)
    pays = around(straight, "fy", ways)
    pay_homes = [((fy + step) % ways) * 2 + high for step in range(ways)]
    *saved, mid, peak, pack = forward(
        spots, tokens, [], begun, [straight, *firsts], early, images - early, experts, stride, rows
    )
    mid = mid.reshape(images * stride, width)
    crossed, mid = lax.optimization_barrier((crossed, mid))
    seconds = [ups[shift] for shift in order[size : 2 * size]]
    sent = dispatch(post, mid, [crossed, *pays[1:], *seconds], experts, cap)
    pays += around(crossed, "fy", ways)
    pay_homes += [((fy + step) % ways) * 2 + 1 - high for step in range(ways)]
    expert_spots = jnp.stack([place_ref[0], fy, *pay_homes])

    groups = [order[at : at + size] for at in range(0, experts, size)]
    arrived = {}

    def send(number, after):
        pending, after = lax.optimization_barrier(([sent[shift] for shift in groups[number]], after))
        for shift, value in zip(groups[number], pending):
            arrived[shift] = value if shift == 0 else exchange(value, shift, experts)
        return after

    send(0, ())
    send(1, [arrived[shift] for shift in groups[0]])
    old, after = None, []
    backs = {}
    for number, group in enumerate(groups):
        result = expert_call(
            expert_spots,
            [arrived[shift] for shift in group],
            [ups[shift] for shift in group],
            pays,
            pack,
            old,
            after,
            group,
            cap,
            experts,
            number == len(groups) - 1,
        )
        old = result[len(group) :]
        after = [backs[shift] for shift in groups[number - 1]] if number else []
        out = result[: len(group)]
        if number + 2 < len(groups):
            out = send(number + 2, out)
        for at, shift in enumerate(group):
            backs[shift] = out[at] if shift == 0 else exchange(out[at], shift, experts)
    backs = [backs[shift] for shift in range(experts)]
    made, *grad = old
    made, backs = lax.optimization_barrier((made, backs))
    made = lax.all_to_all(made, GROUP, split_axis=0, concat_axis=0, tiled=True)

    hidden_grad, mixed_grad, sums = middle(
        place_ref, grad_output, pack, pos, saved, backs, [], cap, experts
    )
    head_rows = 3 * (3 * width // LANES) + 4
    devices = 2 * experts // 2 * fsdp
    members = devices if head_rows + devices <= part else 0
    device = ((high * (experts // 2) + low) * ways + fy) * 2 + core
    spots = jnp.stack([core, device])
    def homeward(straight, crossed):
        return [
            lax.ppermute(straight, ("hi", "core"), BACK),
            lax.ppermute(crossed, ("hi", "core"), BACK_CROSSED),
        ]

    which = high.reshape(1)
    if len(grad) == 4:
        sums_two = list(half_sums(which, grad[0], swap(grad[1], "fy"), [sums], 0.02))
        home_two = homeward(*sums_two)
        grad[3], sums_two[0] = lax.optimization_barrier((grad[3], sums_two[0]))
        got_one = swap(grad[3], "fy")
    else:
        half = split_sum(grad[0].reshape((ways, 2) + grad[0].shape[1:]), "fy", ways)
        home = homeward(*(lax.dynamic_index_in_dim(half, k, 0, keepdims=False) for k in (high, 1 - high)))
        tall = hidden_part + TAIL
        home_two, home_one = [v[:tall] for v in home], [v[tall:] for v in home]
    qkv_grad, keep, give = backward(
        spots, tokens, saved, mixed_grad, sums, peak, [], ways, part, head_rows, members
    )

    got = swap(give, "core")
    after = []
    if len(grad) == 4:
        after = half_sums(which, grad[2], got_one, home_two, 40)
        home_one = homeward(*after)
    output = combine_output(place_ref, pos, saved[2], made, seq)
    near_by = experts // 2
    if ways == 2 and part % (TAIL * near_by) == 0:

        def spread(values):
            return [
                value if k == 0 else lax.ppermute(value, "lo", [(j, j ^ k) for j in range(near_by)])
                for k, value in enumerate(values)
            ]

        mine, theirs = add_halves(fy.reshape(1), keep, got, after)
        theirs, qkv_grad = lax.optimization_barrier((theirs, qkv_grad))
        input_grad = first_norm(tokens, qkv_grad, pack, hidden_grad)
        parts = split_rows(low.reshape(1), mine, swap(theirs, "fy"), [output, input_grad], near_by)
        total = add_parts(spread(parts))
        total = add_parts([total, swap(total, "hi")])
        total = spread([total] * near_by)
    else:
        sums = split_sum((keep.astype(f32) + got.astype(f32)).astype(bf16), "fy", ways)
        total = [lax.psum(sums, ("hi", "lo"))]
        input_grad = first_norm(tokens, qkv_grad, pack, hidden_grad)
    if not members:
        peak = jnp.max(lax.all_gather(peak, DEVICE, axis=0, tiled=True), axis=0, keepdims=True)
    limit = jnp.pad(clip_threshold.astype(f32).reshape(1, HEADS), ((0, 0), (0, LANES - HEADS)), constant_values=1.0)
    grad_qkv, grad_out, grad_router, grads, clipped = finish(
        low.reshape(1), total, own, limit, peak, width, experts, head_rows, members
    )
    grad_w1, grad_w2, grad_b1, grad_b2 = home_sums(
        spot.reshape(1), home_two, home_one, total[0], hidden_part, part, fsdp
    )
    return (
        output,
        input_grad,
        grads[0],
        grads[1],
        grad_qkv,
        grads[2],
        grads[3],
        grad_out,
        grads[4],
        grads[5],
        grads[6],
        grad_router.T,
        grad_w1[None],
        grad_b1,
        grad_w2[None],
        grad_b2,
        clipped,
    )


def solution(mesh):
    experts, fsdp = mesh.shape["expert"], mesh.shape["fsdp"]
    inner = Mesh(mesh.devices.reshape(2, experts // 2, fsdp // 2, 2), DEVICE)
    token, row, expert = P(DEVICE, None, None), ("fy", "core"), ("hi", "lo")
    vector, matrix = P(row), P(row, None)
    return jax.shard_map(
        functools.partial(shards, experts=experts, fsdp=fsdp),
        mesh=inner,
        in_specs=(
            token,
            vector,
            vector,
            matrix,
            vector,
            vector,
            matrix,
            vector,
            vector,
            vector,
            matrix,
            P(expert, row, None),
            P(expert, row),
            P(expert, row, None),
            P(expert, row),
            P(DEVICE, None),
            P(),
            token,
        ),
        out_specs=(
            token,
            token,
            vector,
            vector,
            matrix,
            vector,
            vector,
            matrix,
            vector,
            vector,
            vector,
            matrix,
            P(expert, row, None),
            P(expert, row),
            P(expert, row, None),
            P(expert, row),
            matrix,
        ),
        check_vma=False,
    )
```

time: 447 us -> 371 us (0.83)
  waiting for transfers between devices: 106 us -> 52.8 us
  starting transfers between devices: 87.9 us -> 58.2 us
  Pallas kernels: 214 us -> 241 us
  other arithmetic: 15.3 us -> 0.59 us
  local copies, waits for them, and re-layouts: 18.5 us -> 12.4 us
    pallas_call x7 -> x16, Pallas kernels: 143 us -> 174 us  [the longest x4 104 us: expert_call(): pl.pallas_call(functools.partial(expert_kernel, cap=cap, group=group, fir...]
    ppermute x28 -> x21, waiting for transfers between devices: 58.4 us -> 31.6 us  [exchange(): return lax.ppermute(value, GROUP, [(k, k ^ shift) for k in range(experts)])]
    ppermute x28 -> x21, starting transfers between devices: 45.7 us -> 20.7 us  [exchange(): return lax.ppermute(value, GROUP, [(k, k ^ shift) for k in range(experts)])]
    all_to_all x2 -> x1, waiting for transfers between devices: 20.7 us -> 0.01 us  [shards(): made = lax.all_to_all(made, GROUP, split_axis=0, concat_axis=0, tiled=True)]
    ppermute x8 -> x12, waiting for transfers between devices: 19.6 us -> 12.8 us  [the longest x6 10.1 us: spread(): lax.ppermute(value, 'lo', [(j, j ^ k) for j in range(near_by)])]
    convert_element_type x4 -> x0, other arithmetic: 6.11 us -> none  [the longest x3 4.42 us: split_sum(): return (kept.astype(f32) + swap(sent, axis).astype(f32)).astype(value.dtype)]
    pallas_call x1, Pallas kernels: 32.4 us -> 27 us  [backward(): pl.pallas_call(functools.partial(backward_kernel, head_rows=head_rows, me...]
    select_n x9 -> x0, other arithmetic: 4.98 us -> none  [the longest x2 3.53 us: all_rows(): jnp.where(high == 0, jnp.stack([straight, crossed], axis=1), jnp.stack([c...]
  transfers between devices with their start and end apart: 48 -> 44, of which waited for: 16 -> 13; matrix products, arithmetic and copies ran while one was open for 6% -> 1% of each run, Pallas kernels for 40% -> 57%
where the time goes in v2:
time: 371 us; the launch traced here: 366 us
  Pallas kernels  241 us (65%)
  starting transfers between devices  58.2 us (16%)
  waiting for transfers between devices  52.8 us (14%)
  local copies, waits for them, and re-layouts  12.4 us (3%)
    pallas_call x4, Pallas kernels, expert_call(): pl.pallas_call(functools.partial(expert_kernel, cap=cap, group=group, fir...  104 us
    pallas_call x2, Pallas kernels, forward(): pl.pallas_call(functools.partial(forward_kernel, experts=experts, fsdp=le...  32.5 us
    ppermute x21, waiting for transfers between devices, exchange(): return lax.ppermute(value, GROUP, [(k, k ^ shift) for k in range(experts)])  31.6 us
    pallas_call x1, Pallas kernels, backward(): pl.pallas_call(functools.partial(backward_kernel, head_rows=head_rows, me...  27 us
    ppermute x21, starting transfers between devices, exchange(): return lax.ppermute(value, GROUP, [(k, k ^ shift) for k in range(experts)])  20.7 us
    pallas_call x1, Pallas kernels, middle(): pl.pallas_call(functools.partial(middle_kernel, cap=cap, experts=experts)...  18.1 us
    ppermute x2, starting transfers between devices, homeward(): lax.ppermute(straight, ('hi', 'core'), BACK)  11.2 us
    pallas_call x1, Pallas kernels, route(): pl.pallas_call(functools.partial(route_kernel, cap=cap, stride=stride), g...  10.3 us
  transfers between devices with their start and end apart: 44, of which 13 were waited for; matrix products, arithmetic and copies ran while one was open for 1% of the time, Pallas kernels for 57%

profile of v2, /device:TPU:0, one launch (start us, length us, event | category | flops | bytes accessed | tf_op | source)
XLA Modules:
  0.0 366.0 jit_solution(12195175595006702255)
XLA Ops:
  0.7 2.8 pack.1
  3.4 3.0 collective-permute-start
  8.3 2.8 collective-permute-start.1
  12.5 10.3 %route.1 = (f32[8,1280]{1,0:T(8,128)}, f32[5,256,128]{2,1,0:T(8,128)}, bf16[432,512]{1,0:T(8,128)(2,1)}, bf16[432,512]{1,0:T(8,128)(2,1)}, bf16[432,512]{1,0:T(8...) custom-call(s32[1]{0:T(128)} %bitcast.place_ref, ...), custom_call_target="tpu_custom_call" | custom-call | flops 20000000 | tf_op jit(solution)/shard_map/route/pallas_call | solution.py:195
  28.8 13.8 %attend.2 = (bf16[5,208,1536]{2,1,0:T(8,128)(2,1)}, bf16[5,208,512]{2,1,0:T(8,128)(2,1)}, f32[5,208,512]{2,1,0:T(8,128)}, f32[5,208,128]{2,1,0:T(8,128)}, bf16[5...) custom-call(s32[5]{0:T(128)} %stack.46.spots_ref, ...), custom_call_target="tpu_custom_call" | custom-call | flops 20000000 | tf_op jit(solution)/shard_map/attend/pallas_call | solution.py:353
  45.1 18.6 %attend.3 = (bf16[5,208,1536]{2,1,0:T(8,128)(2,1)}, bf16[5,208,512]{2,1,0:T(8,128)(2,1)}, f32[5,208,512]{2,1,0:T(8,128)}, f32[5,208,128]{2,1,0:T(8,128)}, bf16[5...) custom-call(s32[5]{0:T(128)} %stack.46.spots_ref, ...), custom_call_target="tpu_custom_call", output_to_operand_aliasing={{0}: (4, {}), {1}: (5, {}), {2}: (6, {}), {3}: (7, {}), {4}... | custom-call | flops 60000002048 | tf_op jit(solution)/shard_map/attend/pallas_call | solution.py:353
  63.8 2.7 collective-permute-done.6.rest_0_.refs_6_
  67.0 9.3 %collective-permute-done.9.rest_3_.refs_3_ = bf16[432,512]{1,0:T(8,128)(2,1)} collective-permute-done((bf16[432,512]{1,0:T(8,128)(2,1)}, bf16[432,512]{1,0:T(8,128)(2,1)}, u32[]{:S(2)}, u32[]{:S(2)}) %collective-permute-start.9) | collective-permute-done | bytes 442400 | tf_op jit(solution)/shard_map/ppermute | solution.py:1072
  77.3 9.7 %dispatch.1 = (bf16[432,512]{1,0:T(8,128)(2,1)}, bf16[432,512]{1,0:T(8,128)(2,1)}, bf16[432,512]{1,0:T(8,128)(2,1)}, bf16[432,512]{1,0:T(8,128)(2,1)}, bf16[432,...) custom-call(f32[8,1280]{1,0:T(8,128)} %get-tuple-element.150.post_ref, ...), custom_call_target="tpu_custom_call" | custom-call | flops 32000000000 | tf_op jit(solution)/shard_map/dispatch/pallas_call | solution.py:229
  91.4 8.9 %collective-permute-done.10.refs_0_ = bf16[432,512]{1,0:T(8,128)(2,1)S(1)} collective-permute-done((bf16[432,512]{1,0:T(8,128)(2,1)}, bf16[432,512]{1,0:T(8,128)(2,1)S(1)}, u32[]{:S(2)}, u32[]{:S(2)}) %collective-permute-start.10) | collective-permute-done | bytes 442400 | tf_op jit(solution)/shard_map/ppermute | solution.py:1072
  101.7 24.9 %expert.4 = (bf16[448,512]{1,0:T(8,128)(2,1)}, bf16[448,512]{1,0:T(8,128)(2,1)}, bf16[8,432,512]{2,1,0:T(8,128)(2,1)}, f32[512,2048]{1,0:T(8,128)}, f32[4,528,512]{2,1,0:T(8,128)}) custom-call(s32[6]{0:T(128)} %stack.52.place_ref, bf16[432,512]{1,0:T(8,128)(2,1)} %copy-done.33, bf16[432,512]{1,0:T(8,128)(2,1)} %copy-done.34, bf16[432,512]{1,0:T(8,128)(2,1)} %copy-done.24, ...), custom_call_target="tpu_custom_call" | custom-call | flops 96000000000 | tf_op jit(solution)/shard_map/expert/pallas_call | solution.py:520
  131.6 26.1 %expert.5 = (bf16[448,512]{1,0:T(8,128)(2,1)}, bf16[448,512]{1,0:T(8,128)(2,1)}, bf16[8,432,512]{2,1,0:T(8,128)(2,1)}, f32[512,2048]{1,0:T(8,128)}, f32[4,528,512]{2,1,0:T(8,128)}) custom-call(s32[6]{0:T(128)} %stack.52.place_ref, bf16[432,512]{1,0:T(8,128)(2,1)} %copy-done.35, bf16[432,512]{1,0:T(8,128)(2,1)} %copy-done.36, ...), custom_call_target="tpu_custom_call", output_to_operand_aliasing={{2}: (10, {})} | custom-call | flops 96000000000 | tf_op jit(solution)/shard_map/expert/pallas_call | solution.py:520
  162.3 25.7 %expert.6 = (bf16[448,512]{1,0:T(8,128)(2,1)}, bf16[448,512]{1,0:T(8,128)(2,1)}, bf16[8,432,512]{2,1,0:T(8,128)(2,1)}, f32[512,2048]{1,0:T(8,128)}, f32[4,528,512]{2,1,0:T(8,128)}) custom-call(s32[6]{0:T(128)} %stack.52.place_ref, bf16[432,512]{1,0:T(8,128)(2,1)} %copy-done.31, bf16[432,512]{1,0:T(8,128)(2,1)} %copy-done.32, ...), custom_call_target="tpu_custom_call", output_to_operand_aliasing={{2}: (10, {})} | custom-call | flops 96000000000 | tf_op jit(solution)/shard_map/expert/pallas_call | solution.py:520
  189.3 27.3 %expert.7 = (bf16[448,512]{1,0:T(8,128)(2,1)}, bf16[448,512]{1,0:T(8,128)(2,1)}, bf16[8,432,512]{2,1,0:T(8,128)(2,1)}, bf16[2,528,512]{2,1,0:T(8,128)(2,1)}, bf1...) custom-call(s32[6]{0:T(128)} %stack.52.place_ref, ...), custom_call_target="tpu_custom_call", output_to_operand_aliasing={{2}: (10, {})} | custom-call | flops 96000000000 | tf_op jit(solution)/shard_map/expert/pallas_call | solution.py:520
  219.2 9.9 %collective-permute-done.26.rest_3_ = bf16[448,512]{1,0:T(8,128)(2,1)} collective-permute-done((bf16[448,512]{1,0:T(8,128)(2,1)S(1)}, bf16[448,512]{1,0:T(8,128)(2,1)}, u32[]{:S(2)}, u32[]{:S(2)}) %collective-permute-start.26) | collective-permute-done | bytes 458784 | tf_op jit(solution)/shard_map/ppermute | solution.py:1072
  230.9 3.7 %all-to-all-start = ((bf16[8,432,512]{2,1,0:T(8,128)(2,1)}), bf16[8,432,512]{2,1,0:T(8,128)(2,1)S(1)}, u32[]{:S(2)}, u32[]{:S(2)}) async-start(bf16[8,432,512]{2,1,0:T(8,128)(2,1)} %get-tuple-element.199), calls=%async_computation | async-start | bytes 7077888 | tf_op jit(solution)/shard_map/all_to_all | solution.py:1200
  234.5 18.1 %middle.1 = (f32[5,208,512]{2,1,0:T(8,128)}, bf16[5,208,512]{2,1,0:T(8,128)(2,1)}, f32[512,640]{1,0:T(8,128)}) custom-call(s32[1]{0:T(128)} %bitcast.place_ref, bf16[5,197,512]{2,1,0:T(8,128)(2,1)} %up_ref.3, bf16[512,2176]{1,0:T(8,128)(2,1)} %get-tuple-element.136.rest_0_.refs_8_.wout_ref.misc_ref.wqkv_ref, ...), custom_call_target="tpu_custom_call" | custom-call | flops 20000000 | tf_op jit(solution)/shard_map/middle/pallas_call | solution.py:642
  252.6 2.7 half_sums.2
  255.8 5.8 %collective-permute-start.31 = (bf16[528,512]{1,0:T(8,128)(2,1)}, bf16[528,512]{1,0:T(8,128)(2,1)}, u32[]{:S(2)}, u32[]{:S(2)}) collective-permute-start(bf16[528,512]{1,0:T(8,128)(2,1)} %get-tuple-element.221), channel_id=1, source_target_pairs={{0,0},{16,1},{1,16},{17,17},{2,2},{18,3},{3,18},{19,19},{4,4},{20,... | collective-permute-start | bytes 1622024 | tf_op jit(solution)/shard_map/ppermute | solution.py:1212
  262.2 27.0 %attend_back.1 = (bf16[5,208,1536]{2,1,0:T(8,128)(2,1)}, bf16[2,128,2304]{2,1,0:T(8,128)(2,1)}, bf16[2,128,2304]{2,1,0:T(8,128)(2,1)}) custom-call(s32[2]{0:T(128)} %pad_add_fusion.spots_ref, bf16[5,197,512]{2,1,0:T(8,128)(2,1)} %tok_ref.7, bf16[5,208,1536]{2,1,0:T(8,128)(2,1)} %get-tuple-element.200.qkv_ref, ...), custom_call_target="tpu_custom_call" | custom-call | flops 50000000 | tf_op jit(solution)/shard_map/attend_back/pallas_call | solution.py:763
  289.3 3.5 collective-permute-start.28
  292.8 2.7 half_sums.3
  296.5 2.8 add_halves.1
  299.7 5.4 %collective-permute-start.41 = (bf16[512,512]{1,0:T(8,128)(2,1)}, bf16[512,512]{1,0:T(8,128)(2,1)}, u32[]{:S(2)}, u32[]{:S(2)}) collective-permute-start(bf16[512,512]{1,0:T(8,128)(2,1)} %get-tuple-element.224.rest_0_), channel_id=1, source_target_pairs={{0,0},{16,1},{1,16},{17,17},{2,2},{18,3},{3,18},{19,19},{4,4},{20,... | collective-permute-start | bytes 1572872 | tf_op jit(solution)/shard_map/ppermute | solution.py:1212
  305.1 8.0 %first_norm.1.refs_1_ = f32[5,197,512]{2,1,0:T(8,128)} custom-call(bf16[5,197,512]{2,1,0:T(8,128)(2,1)} %tok_ref.7, bf16[5,208,1536]{2,1,0:T(8,128)(2,1)} %get-tuple-element.228.qkv_grad_ref, bf16[512,2176]{1,0:T(8,128)(2,1)} %get-tuple-element.136.rest_0_.refs_8_.wout_ref.misc_ref.wqkv_ref, ...), custom_call_target="tpu_custom_call" | custom-call | flops 20000000 | tf_op jit(solution)/shard_map/first_norm/pallas_call | solution.py:816
  314.9 8.5 %combine.1.refs_0_ = bf16[5,197,512]{2,1,0:T(8,128)(2,1)} custom-call(s32[1]{0:T(128)} %bitcast.place_ref, f32[5,256,128]{2,1,0:T(8,128)} %get-tuple-element.131.pos_ref, f32[5,208,512]{2,1,0:T(8,128)} %get-tuple-element.149.hidden_ref, bf16[8,432,512]{2,1,0:T(8,128)(2,1)} %copy-done), custom_call_target="tpu_custom_call" | custom-call | flops 20000000 | tf_op jit(solution)/shard_map/combine/pallas_call | solution.py:851
  323.4 2.4 split_rows.1
  329.2 3.2 collective-permute-done.34.refs_1_
  334.3 2.5 collective-permute-done.36.refs_3_
  340.6 8.4 %collective-permute-done.37.refs_1_ = bf16[32,2304]{1,0:T(8,128)(2,1)S(1)} collective-permute-done((bf16[32,2304]{1,0:T(8,128)(2,1)}, bf16[32,2304]{1,0:T(8,128)(2,1)S(1)}, u32[]{:S(2)}, u32[]{:S(2)}) %collective-permute-start.37) | collective-permute-done | bytes 147488 | tf_op jit(solution)/shard_map/ppermute | solution.py:1053
  355.3 3.0 home_sums.1
  361.5 2.8 finish.1
  (164 shorter events, 58.6 us)
Async XLA Ops:
  3.4 19.4 %collective-permute-start = (bf16[128,2176]{1,0:T(8,128)(2,1)}, bf16[128,2176]{1,0:T(8,128)(2,1)S(1)}, u32[]{:S(2)}, u32[]{:S(2)}) collective-permute-start(bf16[128,2176]{1,0:T(8,128)(2,1)} %get-tuple-element.132.rest_0_.refs_4_), channel_id=1, source_target_pairs={{2,0},{0,2},{3,1},{1,3},{6,4},{4,6},{7,5},{5,7},{10,8},{8,10},{11,... | collective-permute-start | bytes 1671176 | tf_op jit(solution)/shard_map/ppermute | solution.py:1058
  6.4 36.2 %collective-permute-start.3 = (bf16[1040,512]{1,0:T(8,128)(2,1)}, bf16[1040,512]{1,0:T(8,128)(2,1)S(1)}, u32[]{:S(2)}, u32[]{:S(2)}) collective-permute-start(bf16[1040,512]{1,0:T(8,128)(2,1)} %get-tuple-element.151), channel_id=1, source_target_pairs={{0,0},{1,16},{16,1},{17,17},{2,2},{3,18},{18,3},{19,19},{4,4},{5,2... | collective-permute-start | bytes 3194888 | tf_op jit(solution)/shard_map/ppermute | solution.py:1131
  8.3 18.4 %collective-permute-start.1 = (bf16[128,2176]{1,0:T(8,128)(2,1)}, bf16[128,2176]{1,0:T(8,128)(2,1)S(1)}, u32[]{:S(2)}, u32[]{:S(2)}) collective-permute-start(bf16[128,2176]{1,0:T(8,128)(2,1)} %get-tuple-element.132.rest_0_.refs_4_), channel_id=1, source_target_pairs={{0,1},{1,0},{2,3},{3,2},{4,5},{5,4},{6,7},{7,6},{8,9},{9,8},{10,11... | collective-permute-start | bytes 1671176 | tf_op jit(solution)/shard_map/ppermute | solution.py:1053
  22.9 20.4 %collective-permute-start.4 = (bf16[432,512]{1,0:T(8,128)(2,1)}, bf16[432,512]{1,0:T(8,128)(2,1)S(1)}, u32[]{:S(2)}, u32[]{:S(2)}) collective-permute-start(bf16[432,512]{1,0:T(8,128)(2,1)} %get-tuple-element.147), channel_id=1, source_target_pairs={{0,4},{1,5},{4,0},{5,1},{8,12},{9,13},{12,8},{13,9},{2,6},{3,7},{6... | collective-permute-start | bytes 1327112 | tf_op jit(solution)/shard_map/ppermute | solution.py:1072
  24.5 20.7 %collective-permute-start.5 = (bf16[432,512]{1,0:T(8,128)(2,1)}, bf16[432,512]{1,0:T(8,128)(2,1)}, u32[]{:S(2)}, u32[]{:S(2)}) collective-permute-start(bf16[432,512]{1,0:T(8,128)(2,1)} %get-tuple-element.148), channel_id=1, source_target_pairs={{0,8},{1,9},{4,12},{5,13},{8,0},{9,1},{12,4},{13,5},{2,10},{3,11},... | collective-permute-start | bytes 1327112 | tf_op jit(solution)/shard_map/ppermute | solution.py:1072
  26.7 40.3 %collective-permute-start.8 = (bf16[432,512]{1,0:T(8,128)(2,1)}, bf16[432,512]{1,0:T(8,128)(2,1)S(1)}, u32[]{:S(2)}, u32[]{:S(2)}) collective-permute-start(bf16[432,512]{1,0:T(8,128)(2,1)} %get-tuple-element.155), channel_id=1, source_target_pairs={{0,12},{1,13},{4,8},{5,9},{8,4},{9,5},{12,0},{13,1},{2,14},{3,15},... | collective-permute-start | bytes 1327112 | tf_op jit(solution)/shard_map/ppermute | solution.py:1072
  27.1 49.2 %collective-permute-start.9 = (bf16[432,512]{1,0:T(8,128)(2,1)}, bf16[432,512]{1,0:T(8,128)(2,1)}, u32[]{:S(2)}, u32[]{:S(2)}) collective-permute-start(bf16[432,512]{1,0:T(8,128)(2,1)} %get-tuple-element.156), channel_id=1, source_target_pairs={{0,13},{1,12},{4,9},{5,8},{8,5},{9,4},{12,1},{13,0},{2,15},{3,14},... | collective-permute-start | bytes 1327112 | tf_op jit(solution)/shard_map/ppermute | solution.py:1072
  42.7 23.8 %collective-permute-start.6 = (bf16[1040,512]{1,0:T(8,128)(2,1)S(1)}, bf16[1040,512]{1,0:T(8,128)(2,1)S(1)}, u32[]{:S(2)}, u32[]{:S(2)}) collective-permute-start(bf16[1040,512]{1,0:T(8,128)(2,1)S(1)} %copy-done.19), channel_id=1, source_target_pairs={{0,16},{1,0},{16,17},{17,1},{2,18},{3,2},{18,19},{19,3},{4,20},{5,... | collective-permute-start | bytes 3194888 | tf_op jit(solution)/shard_map/ppermute | solution.py:1149
  43.3 33.0 %collective-permute-start.7 = (bf16[1040,512]{1,0:T(8,128)(2,1)S(1)}, bf16[1040,512]{1,0:T(8,128)(2,1)S(1)}, u32[]{:S(2)}, u32[]{:S(2)}) collective-permute-start(bf16[1040,512]{1,0:T(8,128)(2,1)S(1)} %collective-permute-done.3.rest_8_.refs_4_), channel_id=1, source_target_pairs={{2,0},{0,2},{3,1},{1,3},{6,4},{4,6},{7,5},{5,7},{10,8},{8,10},{11,... | collective-permute-start | bytes 3194888 | tf_op jit(solution)/shard_map/ppermute | solution.py:1058
  66.4 35.3 %collective-permute-start.14 = (bf16[1040,512]{1,0:T(8,128)(2,1)S(1)}, bf16[1040,512]{1,0:T(8,128)(2,1)}, u32[]{:S(2)}, u32[]{:S(2)}) collective-permute-start(bf16[1040,512]{1,0:T(8,128)(2,1)S(1)} %collective-permute-done.6.rest_0_.refs_6_), channel_id=1, source_target_pairs={{2,0},{0,2},{3,1},{1,3},{6,4},{4,6},{7,5},{5,7},{10,8},{8,10},{11,... | collective-permute-start | bytes 3194888 | tf_op jit(solution)/shard_map/ppermute | solution.py:1058
  87.0 13.2 %collective-permute-start.10 = (bf16[432,512]{1,0:T(8,128)(2,1)}, bf16[432,512]{1,0:T(8,128)(2,1)S(1)}, u32[]{:S(2)}, u32[]{:S(2)}) collective-permute-start(bf16[432,512]{1,0:T(8,128)(2,1)} %get-tuple-element.163), channel_id=1, source_target_pairs={{0,4},{1,5},{4,0},{5,1},{8,12},{9,13},{12,8},{13,9},{2,6},{3,7},{6... | collective-permute-start | bytes 1327112 | tf_op jit(solution)/shard_map/ppermute | solution.py:1072
  87.5 13.3 %collective-permute-start.11 = (bf16[432,512]{1,0:T(8,128)(2,1)}, bf16[432,512]{1,0:T(8,128)(2,1)S(1)}, u32[]{:S(2)}, u32[]{:S(2)}) collective-permute-start(bf16[432,512]{1,0:T(8,128)(2,1)} %get-tuple-element.164), channel_id=1, source_target_pairs={{0,8},{1,9},{4,12},{5,13},{8,0},{9,1},{12,4},{13,5},{2,10},{3,11},... | collective-permute-start | bytes 1327112 | tf_op jit(solution)/shard_map/ppermute | solution.py:1072
  87.5 40.6 %collective-permute-start.19 = (bf16[432,512]{1,0:T(8,128)(2,1)S(1)}, bf16[432,512]{1,0:T(8,128)(2,1)S(1)}, u32[]{:S(2)}, u32[]{:S(2)}) collective-permute-start(bf16[432,512]{1,0:T(8,128)(2,1)S(1)} %copy-done.23), channel_id=1, source_target_pairs={{0,5},{1,4},{4,1},{5,0},{8,13},{9,12},{12,9},{13,8},{2,7},{3,6},{6... | collective-permute-start | bytes 1327112 | tf_op jit(solution)/shard_map/ppermute | solution.py:1072
  88.5 69.2 %collective-permute-start.20 = (bf16[432,512]{1,0:T(8,128)(2,1)}, bf16[432,512]{1,0:T(8,128)(2,1)}, u32[]{:S(2)}, u32[]{:S(2)}) collective-permute-start(bf16[432,512]{1,0:T(8,128)(2,1)} %get-tuple-element.183), channel_id=1, source_target_pairs={{0,9},{1,8},{4,13},{5,12},{8,1},{9,0},{12,5},{13,4},{2,11},{3,10},... | collective-permute-start | bytes 1327112 | tf_op jit(solution)/shard_map/ppermute | solution.py:1072
  100.8 28.5 %collective-permute-start.12 = (bf16[432,512]{1,0:T(8,128)(2,1)}, bf16[432,512]{1,0:T(8,128)(2,1)S(1)}, u32[]{:S(2)}, u32[]{:S(2)}) collective-permute-start(bf16[432,512]{1,0:T(8,128)(2,1)} %get-tuple-element.165), channel_id=1, source_target_pairs={{0,12},{1,13},{4,8},{5,9},{8,4},{9,5},{12,0},{13,1},{2,14},{3,15},... | collective-permute-start | bytes 1327112 | tf_op jit(solution)/shard_map/ppermute | solution.py:1072
  101.7 28.6 %collective-permute-start.13 = (bf16[432,512]{1,0:T(8,128)(2,1)}, bf16[432,512]{1,0:T(8,128)(2,1)S(1)}, u32[]{:S(2)}, u32[]{:S(2)}) collective-permute-start(bf16[432,512]{1,0:T(8,128)(2,1)} %get-tuple-element.166), channel_id=1, source_target_pairs={{0,13},{1,12},{4,9},{5,8},{8,5},{9,4},{12,1},{13,0},{2,15},{3,14},... | collective-permute-start | bytes 1327112 | tf_op jit(solution)/shard_map/ppermute | solution.py:1072
  126.7 34.1 %collective-permute-start.21 = (bf16[448,512]{1,0:T(8,128)(2,1)}, bf16[448,512]{1,0:T(8,128)(2,1)S(1)}, u32[]{:S(2)}, u32[]{:S(2)}) collective-permute-start(bf16[448,512]{1,0:T(8,128)(2,1)} %get-tuple-element.187), channel_id=1, source_target_pairs={{0,4},{1,5},{4,0},{5,1},{8,12},{9,13},{12,8},{13,9},{2,6},{3,7},{6... | collective-permute-start | bytes 1376264 | tf_op jit(solution)/shard_map/ppermute | solution.py:1072
  128.1 33.4 %collective-permute-start.22 = (bf16[448,512]{1,0:T(8,128)(2,1)}, bf16[448,512]{1,0:T(8,128)(2,1)S(1)}, u32[]{:S(2)}, u32[]{:S(2)}) collective-permute-start(bf16[448,512]{1,0:T(8,128)(2,1)} %get-tuple-element.188), channel_id=1, source_target_pairs={{0,8},{1,9},{4,12},{5,13},{8,0},{9,1},{12,4},{13,5},{2,10},{3,11},... | collective-permute-start | bytes 1376264 | tf_op jit(solution)/shard_map/ppermute | solution.py:1072
  129.3 29.1 %collective-permute-start.17 = (bf16[432,512]{1,0:T(8,128)(2,1)S(1)}, bf16[432,512]{1,0:T(8,128)(2,1)S(1)}, u32[]{:S(2)}, u32[]{:S(2)}) collective-permute-start(bf16[432,512]{1,0:T(8,128)(2,1)S(1)} %copy-done.29), channel_id=1, source_target_pairs={{0,5},{1,4},{4,1},{5,0},{8,13},{9,12},{12,9},{13,8},{2,7},{3,6},{6... | collective-permute-start | bytes 1327112 | tf_op jit(solution)/shard_map/ppermute | solution.py:1072
  130.3 29.6 %collective-permute-start.18 = (bf16[432,512]{1,0:T(8,128)(2,1)S(1)}, bf16[432,512]{1,0:T(8,128)(2,1)S(1)}, u32[]{:S(2)}, u32[]{:S(2)}) collective-permute-start(bf16[432,512]{1,0:T(8,128)(2,1)S(1)} %copy-done.28), channel_id=1, source_target_pairs={{0,9},{1,8},{4,13},{5,12},{8,1},{9,0},{12,5},{13,4},{2,11},{3,10},... | collective-permute-start | bytes 1327112 | tf_op jit(solution)/shard_map/ppermute | solution.py:1072
  157.7 30.3 %collective-permute-start.16 = (bf16[432,512]{1,0:T(8,128)(2,1)S(1)}, bf16[432,512]{1,0:T(8,128)(2,1)S(1)}, u32[]{:S(2)}, u32[]{:S(2)}) collective-permute-start(bf16[432,512]{1,0:T(8,128)(2,1)S(1)} %copy-done.22), channel_id=1, source_target_pairs={{0,1},{1,0},{4,5},{5,4},{8,9},{9,8},{12,13},{13,12},{2,3},{3,2},{6... | collective-permute-start | bytes 1327112 | tf_op jit(solution)/shard_map/ppermute | solution.py:1072
  158.4 29.7 %collective-permute-start.23 = (bf16[448,512]{1,0:T(8,128)(2,1)}, bf16[448,512]{1,0:T(8,128)(2,1)S(1)}, u32[]{:S(2)}, u32[]{:S(2)}) collective-permute-start(bf16[448,512]{1,0:T(8,128)(2,1)} %get-tuple-element.192), channel_id=1, source_target_pairs={{0,12},{1,13},{4,8},{5,9},{8,4},{9,5},{12,0},{13,1},{2,14},{3,15},... | collective-permute-start | bytes 1376264 | tf_op jit(solution)/shard_map/ppermute | solution.py:1072
  159.9 28.2 %collective-permute-start.24 = (bf16[448,512]{1,0:T(8,128)(2,1)}, bf16[448,512]{1,0:T(8,128)(2,1)S(1)}, u32[]{:S(2)}, u32[]{:S(2)}) collective-permute-start(bf16[448,512]{1,0:T(8,128)(2,1)} %get-tuple-element.193), channel_id=1, source_target_pairs={{0,13},{1,12},{4,9},{5,8},{8,5},{9,4},{12,1},{13,0},{2,15},{3,14},... | collective-permute-start | bytes 1376264 | tf_op jit(solution)/shard_map/ppermute | solution.py:1072
  160.8 27.3 %collective-permute-start.15 = (bf16[432,512]{1,0:T(8,128)(2,1)S(1)}, bf16[432,512]{1,0:T(8,128)(2,1)S(1)}, u32[]{:S(2)}, u32[]{:S(2)}) collective-permute-start(bf16[432,512]{1,0:T(8,128)(2,1)S(1)} %copy-done.26), channel_id=1, source_target_pairs={{0,1},{1,0},{4,5},{5,4},{8,9},{9,8},{12,13},{13,12},{2,3},{3,2},{6... | collective-permute-start | bytes 1327112 | tf_op jit(solution)/shard_map/ppermute | solution.py:1072
  218.6 34.0 %collective-permute-start.29 = (bf16[2,528,512]{2,1,0:T(8,128)(2,1)}, bf16[2,528,512]{2,1,0:T(8,128)(2,1)}, u32[]{:S(2)}, u32[]{:S(2)}) collective-permute-start(bf16[2,528,512]{2,1,0:T(8,128)(2,1)} %get-tuple-element.220), channel_id=1, source_target_pairs={{0,2},{2,0},{1,3},{3,1},{4,6},{6,4},{5,7},{7,5},{8,10},{10,8},{9,1... | collective-permute-start | bytes 3244040 | tf_op jit(solution)/shard_map/ppermute | solution.py:1053
  230.9 82.3 %all-to-all-start = ((bf16[8,432,512]{2,1,0:T(8,128)(2,1)}), bf16[8,432,512]{2,1,0:T(8,128)(2,1)S(1)}, u32[]{:S(2)}, u32[]{:S(2)}) async-start(bf16[8,432,512]{2,1,0:T(8,128)(2,1)} %get-tuple-element.199), calls=%async_computation | async-start | bytes 7077888 | tf_op jit(solution)/shard_map/all_to_all | solution.py:1200
  255.3 37.4 %collective-permute-start.30 = (bf16[2,512,512]{2,1,0:T(8,128)(2,1)}, bf16[2,512,512]{2,1,0:T(8,128)(2,1)}, u32[]{:S(2)}, u32[]{:S(2)}) collective-permute-start(bf16[2,512,512]{2,1,0:T(8,128)(2,1)} %get-tuple-element.222), channel_id=1, source_target_pairs={{0,2},{2,0},{1,3},{3,1},{4,6},{6,4},{5,7},{7,5},{8,10},{10,8},{9,1... | collective-permute-start | bytes 3145736 | tf_op jit(solution)/shard_map/ppermute | solution.py:1053
  255.8 36.9 %collective-permute-start.31 = (bf16[528,512]{1,0:T(8,128)(2,1)}, bf16[528,512]{1,0:T(8,128)(2,1)}, u32[]{:S(2)}, u32[]{:S(2)}) collective-permute-start(bf16[528,512]{1,0:T(8,128)(2,1)} %get-tuple-element.221), channel_id=1, source_target_pairs={{0,0},{16,1},{1,16},{17,17},{2,2},{18,3},{3,18},{19,19},{4,4},{20,... | collective-permute-start | bytes 1622024 | tf_op jit(solution)/shard_map/ppermute | solution.py:1212
  261.6 31.1 %collective-permute-start.32 = (bf16[528,512]{1,0:T(8,128)(2,1)}, bf16[528,512]{1,0:T(8,128)(2,1)}, u32[]{:S(2)}, u32[]{:S(2)}) collective-permute-start(bf16[528,512]{1,0:T(8,128)(2,1)} %get-tuple-element.223), channel_id=1, source_target_pairs={{16,0},{0,1},{17,16},{1,17},{18,2},{2,3},{19,18},{3,19},{20,4},{4,... | collective-permute-start | bytes 1622024 | tf_op jit(solution)/shard_map/ppermute | solution.py:1213
  299.3 24.1 %collective-permute-start.33 = (bf16[128,2304]{1,0:T(8,128)(2,1)}, bf16[128,2304]{1,0:T(8,128)(2,1)}, u32[]{:S(2)}, u32[]{:S(2)}) collective-permute-start(bf16[128,2304]{1,0:T(8,128)(2,1)} %get-tuple-element.231), channel_id=1, source_target_pairs={{0,2},{2,0},{1,3},{3,1},{4,6},{6,4},{5,7},{7,5},{8,10},{10,8},{9,1... | collective-permute-start | bytes 1769480 | tf_op jit(solution)/shard_map/ppermute | solution.py:1053
  299.7 55.6 %collective-permute-start.41 = (bf16[512,512]{1,0:T(8,128)(2,1)}, bf16[512,512]{1,0:T(8,128)(2,1)}, u32[]{:S(2)}, u32[]{:S(2)}) collective-permute-start(bf16[512,512]{1,0:T(8,128)(2,1)} %get-tuple-element.224.rest_0_), channel_id=1, source_target_pairs={{0,0},{16,1},{1,16},{17,17},{2,2},{18,3},{3,18},{19,19},{4,4},{20,... | collective-permute-start | bytes 1572872 | tf_op jit(solution)/shard_map/ppermute | solution.py:1212
  305.1 50.2 %collective-permute-start.42 = (bf16[512,512]{1,0:T(8,128)(2,1)}, bf16[512,512]{1,0:T(8,128)(2,1)}, u32[]{:S(2)}, u32[]{:S(2)}) collective-permute-start(bf16[512,512]{1,0:T(8,128)(2,1)} %get-tuple-element.225.rest_1_), channel_id=1, source_target_pairs={{16,0},{0,1},{17,16},{1,17},{18,2},{2,3},{19,18},{3,19},{20,4},{4,... | collective-permute-start | bytes 1572872 | tf_op jit(solution)/shard_map/ppermute | solution.py:1213
  (51 other events, 424.1 us)

commit v3 on v2

--- a/solution.py
+++ b/solution.py
@@ -22,7 +22,7 @@
 TN = (((0,), (0,)), ((), ()))
 DEVICE = ("hi", "lo", "fy", "core")
 GROUP = ("lo", "core")
-VMEM_LIMIT = 58 << 20
+VMEM_LIMIT = 63 << 20
 
 
 def dot(a, b, dims):
@@ -76,14 +76,17 @@
 
 
 def gelu_pair(value):
-    bell = jnp.exp(value * value * -0.5)
-    t = 1.0 / (1.0 + jnp.abs(value) * (0.3275911 * 0.7071067811865476))
-    poly = t * (
-        0.127414796 + t * (-0.142248368 + t * (0.7107068705 + t * (-0.7265760135 + t * 0.5307027145)))
-    )
+    def low(number):
+        return jnp.asarray(number, bf16)
+
+    value = value.astype(bf16)
+    bell = jnp.exp(value * value * low(-0.5))
+    t = low(1.0) / (low(1.0) + jnp.abs(value) * low(0.3275911 * 0.7071067811865476))
+    poly = low(0.7107068705) + t * (low(-0.7265760135) + t * low(0.5307027145))
+    poly = t * (low(0.127414796) + t * (low(-0.142248368) + t * poly))
     lower = poly * bell
-    phi = jnp.where(value >= 0, 1.0 - lower, lower)
-    return value * phi, phi + value * (bell * 0.3989422804014327)
+    phi = jnp.where(value >= low(0.0), low(1.0) - lower, lower)
+    return value * phi, phi + value * (bell * low(0.3989422804014327))
 
 
 def whole(shape):
@@ -209,7 +212,8 @@
     )(place, ids, grad_output)
 
 
-def dispatch_kernel(post_ref, rows_ref, *outs, cap):
+def dispatch_kernel(post_ref, rows_ref, *refs, cap, paired, skip):
+    ups, outs = refs[: len(paired)], refs[len(paired) + skip :]
     step = pl.program_id(0)
     hot = one_hot_rows(post_ref[pl.ds(step, 1), :], cap)
     sent = dot(hot, rows_ref[...], NN).astype(bf16)
@@ -217,25 +221,28 @@
 
         @pl.when(step == index)
         def _():
-            outs[index][...] = sent
-
-
-def dispatch_after_kernel(post_ref, rows_ref, *rest, cap, skip):
-    dispatch_kernel(post_ref, rows_ref, *rest[skip:], cap=cap)
-
-
-def dispatch(post, rows, after, experts, cap):
+            outs[index][0:cap] = sent
+            if index in paired:
+                outs[index][cap:] = ups[paired.index(index)][...]
+
+
+def dispatch(post, rows, ups, paired, after, experts, cap):
     width = rows.shape[1]
-    return pl.pallas_call(
-        functools.partial(dispatch_after_kernel, cap=cap, skip=len(after)),
-        grid=(experts,),
-        in_specs=[whole(post.shape), whole(rows.shape)] + [pl.BlockSpec(memory_space=pl.ANY)] * len(after),
-        out_specs=[whole((cap, width))] * experts,
-        out_shape=[jax.ShapeDtypeStruct((cap, width), bf16)] * experts,
-        compiler_params=params(),
-        cost_estimate=cost(32),
-        name="dispatch",
-    )(post, rows, *after)
+    shapes = [((2 if shift in paired else 1) * cap, width) for shift in range(experts)]
+    return list(
+        pl.pallas_call(
+            functools.partial(dispatch_kernel, cap=cap, paired=paired, skip=len(after)),
+            grid=(experts,),
+            in_specs=[whole(post.shape), whole(rows.shape)]
+            + [whole((cap, width))] * len(paired)
+            + [pl.BlockSpec(memory_space=pl.ANY)] * len(after),
+            out_specs=[whole(v) for v in shapes],
+            out_shape=[jax.ShapeDtypeStruct(v, bf16) for v in shapes],
+            compiler_params=params(),
+            cost_estimate=cost(0.02),
+            name="dispatch",
+        )(post, rows, *[ups[shift] for shift in paired], *after)
+    )
 
 
 def forward_kernel(spots_ref, tok_ref, *rest, experts, fsdp, later):
@@ -303,7 +310,7 @@
         mixed_ref[0, :, pl.ds(at, LANES)] = jnp.where(first, parts[0], parts[1]).astype(bf16)
         return peak
 
-    peak = lax.fori_loop(0, HEADS // 2, pair, jnp.full((1, LANES), NEG, f32))
+    peak = lax.fori_loop(0, HEADS // 2, pair, jnp.full((1, LANES), NEG, f32), unroll=True)
     peak_ref[...] = jnp.maximum(peak_ref[...], peak)
     hidden = residual + dot(mixed_ref[0], pack_ref[:, wide : wide + width], NN) + vector(4)
     hidden_ref[0] = hidden
@@ -426,10 +433,9 @@
     bias2[...] += tail[1:2]
     x, up = rows[...], ups[...]
     value, slope = gelu_pair(dot(x, w1[...], NN) + tail[0:1, 0:tile])
-    act = value.astype(bf16)
+    act = value
     acc_out[...] += dot(act, w2[0:tile], NN)
-    raw = slope * dot(up, w2[0:tile], NT)
-    pre = raw.astype(bf16)
+    pre = slope * dot(up, w2[0:tile], NT).astype(bf16)
     acc_row[...] += dot(pre, w1[...], NT)
     part1 = dot(x, pre, TN)
     part2 = dot(act, up, TN)
@@ -532,7 +538,8 @@
         grid_spec=pltpu.PrefetchScalarGridSpec(
             num_scalar_prefetch=1,
             grid=(fsdp,),
-            in_specs=[whole((cap, width))] * (2 * count)
+            in_specs=[whole((cap, width))] * count
+            + [pl.BlockSpec((cap, width), lambda h, _, at=v.shape[0] // cap - 1: (at, 0)) for v in ups]
             + [far] * fsdp
             + [pl.BlockSpec((width, LANES), lambda h, _: (0, 4 * width // LANES))]
             + ([] if first else [far, column, line])
@@ -565,10 +572,49 @@
     )(*operands, *after)
 
 
+def gather_back(places, backs, shifts, slot_sum, effect, cap):
+    lane = iota((1, LANES), 1)
+    for index, ref in zip(shifts, backs):
+        hot = one_hot_cols(places[:, index : index + 1], cap)
+        slot_sum = slot_sum + dot(hot, ref[0:cap], NN)
+        parts = dot(hot, ref[cap : cap + TAIL, 0:cap], NT)
+        effect = jnp.where(lane == index, jnp.sum(parts, axis=1, keepdims=True), effect)
+    return slot_sum, effect
+
+
+def returned_kernel(pos_ref, *refs, cap, shifts):
+    backs, slot_ref, effect_ref = refs[: len(shifts)], refs[-2], refs[-1]
+    _, rows, width = slot_ref.shape
+    slot_ref[0], effect_ref[0] = gather_back(
+        pos_ref[0, 0:rows, :], backs, shifts, jnp.zeros((rows, width), f32), jnp.zeros((rows, LANES), f32), cap
+    )
+
+
+def returned(pos, backs, shifts, rows, cap):
+    images, width = pos.shape[0], backs[0].shape[1]
+
+    def image(shape):
+        return pl.BlockSpec((1,) + shape, lambda i: (i, 0, 0))
+
+    return pl.pallas_call(
+        functools.partial(returned_kernel, cap=cap, shifts=shifts),
+        grid=(images,),
+        in_specs=[image((pos.shape[1], LANES))] + [whole((cap + TAIL, width))] * len(backs),
+        out_specs=[image((rows, width)), image((rows, LANES))],
+        out_shape=[
+            jax.ShapeDtypeStruct((images, rows, width), f32),
+            jax.ShapeDtypeStruct((images, rows, LANES), f32),
+        ],
+        compiler_params=params(),
+        cost_estimate=cost(100),
+        name="returned",
+    )(pos, *backs)
+
+
 def middle_kernel(
-    place_ref, up_ref, wout_ref, misc_ref, pos_ref, mixed_ref, hidden_ref, prob_ref, *rest, cap, experts
+    place_ref, up_ref, wout_ref, misc_ref, pos_ref, mixed_ref, hidden_ref, prob_ref, slot_ref, effect_ref, *rest, cap, experts
 ):
-    backs = rest[:experts]
+    backs = rest[:2]
     hidden_grad_ref, mixed_grad_ref, sums_ref, padded, vectors, router, shifts, acc_out, acc_router = rest[-9:]
     _, seq, width = up_ref.shape
     rows = padded.shape[0]
@@ -589,15 +635,7 @@
     def shift(index, value):
         shifts[index : index + 1, :] += jnp.sum(value, axis=0, keepdims=True)
 
-    lane = iota((1, LANES), 1)
-    places = pos_ref[0, 0:rows, :]
-    slot_sum = jnp.zeros((rows, width), f32)
-    effect = jnp.zeros((rows, LANES), f32)
-    for index in range(experts):
-        hot = one_hot_cols(places[:, index : index + 1], cap)
-        slot_sum = slot_sum + dot(hot, backs[index][0:cap], NN)
-        parts = dot(hot, backs[index][cap : cap + TAIL, 0:cap], NT)
-        effect = jnp.where(lane == index, jnp.sum(parts, axis=1, keepdims=True), effect)
+    slot_sum, effect = gather_back(pos_ref[0, 0:rows, :], backs, (0, 1), slot_ref[0], effect_ref[0], cap)
     prob = prob_ref[0]
     logit_grad = effect - prob * jnp.sum(effect, axis=1, keepdims=True)
     logit_parts = pieces(logit_grad, 2)
@@ -631,7 +669,7 @@
         sums_ref[:, width:] = spare.T
 
 
-def middle(place, grad_output, pack, pos, saved, backs, after, cap, experts):
+def middle(place, grad_output, pack, pos, saved, part_sums, backs, cap, experts):
     images, seq, width = grad_output.shape
     _, mixed, hidden, prob, _ = saved
     rows = mixed.shape[1]
@@ -651,9 +689,10 @@
             image((rows, width)),
             image((rows, width)),
             image((rows, LANES)),
+            image((rows, width)),
+            image((rows, LANES)),
         ]
-        + [whole((cap + TAIL, width))] * experts
-        + [pl.BlockSpec(memory_space=pl.ANY)] * len(after),
+        + [whole((cap + TAIL, width))] * len(backs),
         out_specs=[image((rows, width)), image((rows, width)), whole((width, width + LANES))],
         out_shape=[
             jax.ShapeDtypeStruct((images, rows, width), f32),
@@ -671,7 +710,7 @@
         compiler_params=params(),
         cost_estimate=cost(0.02),
         name="middle",
-    )(place, grad_output, pack, pack, pos, mixed, hidden, prob, *backs, *after)
+    )(place, grad_output, pack, pack, pos, mixed, hidden, prob, *part_sums, *backs)
 
 
 def backward_kernel(
@@ -713,7 +752,7 @@
             qkv_grad_ref[0, :, pl.ds(index_of * width + at, LANES)] = jnp.where(first, left, right).astype(bf16)
         return carry
 
-    lax.fori_loop(0, HEADS // 2, pair, 0)
+    lax.fori_loop(0, HEADS // 2, pair, 0, unroll=True)
     columns[...] += jnp.sum(qkv_grad_ref[0].astype(f32), axis=0, keepdims=True)
     padded[0:seq] = tok_ref[0].astype(f32)
     hat, _ = norm_stats(padded[...])
@@ -867,7 +906,7 @@
 
 def finish_kernel(slot_ref, *refs, number, head_rows, members):
     parts, (own_ref, limit_ref, peak_ref) = refs[:number], refs[number : number + 3]
-    qkv_ref, out_ref, misc_ref, vec_ref, clip_ref, total_ref = refs[number + 3 :]
+    qkv_ref, out_ref, misc_ref, clip_ref, *vec_refs, total_ref = refs[number + 3 :]
     part = own_ref.shape[0]
     for shift, ref in enumerate(parts):
         size = part // number
@@ -889,7 +928,8 @@
     misc = jnp.where(lane == VEC, jnp.sum(base * weight, axis=1, keepdims=True), misc)
     misc = jnp.where(lane == VEC + 1, jnp.sum(columns * weight, axis=1, keepdims=True), misc)
     misc = misc.T
-    vec_ref[...] = misc[VEC : VEC + 8]
+    for index, ref in enumerate(vec_refs):
+        ref[...] = misc[VEC + index : VEC + index + 1]
     misc_ref[...] = misc[0 : misc_ref.shape[0]]
     if members:
         move = jnp.where(
@@ -915,13 +955,13 @@
 def finish(slot, total, own, limit, peak, width, experts, head_rows, members):
     part = own.shape[0]
     operands = [*total, own, limit, peak]
-    shapes = [(part, 3 * width), (part, width), (experts, part), (8, part), (part, 3 * width)]
+    shapes = [(part, 3 * width), (part, width), (experts, part), (part, 3 * width)] + [(1, part)] * 7
     return pl.pallas_call(
         functools.partial(finish_kernel, number=len(total), head_rows=head_rows, members=members),
         grid=(1,),
         in_specs=[pl.BlockSpec(memory_space=pltpu.SMEM)] + [whole(v.shape) for v in operands],
         out_specs=[whole(v) for v in shapes],
-        out_shape=[jax.ShapeDtypeStruct(v, bf16 if i == 4 else f32) for i, v in enumerate(shapes)],
+        out_shape=[jax.ShapeDtypeStruct(v, bf16 if i == 3 else f32) for i, v in enumerate(shapes)],
         scratch_shapes=[pltpu.VMEM((part, total[0].shape[1]), bf16)],
         compiler_params=params(),
         cost_estimate=cost(0.02),
@@ -950,9 +990,9 @@
     )(high, keep, got, *after)
 
 
-def home_sums_kernel(spot_ref, one, two, three, four, _, w1_ref, w2_ref, b1_ref, b2_ref):
+def home_second_kernel(spot_ref, one, two, _, w2_ref, b1_ref, b2_ref):
     tile, width = w2_ref.shape
-    part = w1_ref.shape[0]
+    part = b2_ref.shape[1]
     w2_ref[...] = one[0:tile].astype(f32) + two[0:tile].astype(f32)
     edge = one[tile:].astype(f32) + two[tile:].astype(f32)
     b1_ref[...] = edge[0:1, 0:tile]
@@ -960,28 +1000,31 @@
         jnp.where(spot_ref[0] == index, edge[1:2, index * part : (index + 1) * part], 0.0)
         for index in range(width // part)
     )
-    for index in range(w1_ref.shape[1] // tile):
+
+
+def home_first_kernel(_, one, two, __, w1_ref):
+    part, hidden = w1_ref.shape
+    number = one.shape[0] // part
+    tile = hidden // number
+    for index in range(number):
         rows = slice(index * part, (index + 1) * part)
-        total = three[rows].astype(f32) + four[rows].astype(f32)
+        total = one[rows].astype(f32) + two[rows].astype(f32)
         w1_ref[:, index * tile : (index + 1) * tile] = total[:, 0:tile]
 
 
-def home_sums(spot, second, first, after, tile, part, fsdp):
-    width = second[0].shape[1]
-    shapes = [(part, tile * fsdp), (tile, width), (1, tile), (1, part)]
-    operands = [*second, *first]
+def home_sums(kernel, spot, pair, after, shapes):
     return pl.pallas_call(
-        home_sums_kernel,
+        kernel,
         grid=(1,),
         in_specs=[pl.BlockSpec(memory_space=pltpu.SMEM)]
-        + [whole(v.shape) for v in operands]
+        + [whole(v.shape) for v in pair]
         + [pl.BlockSpec(memory_space=pl.ANY)],
         out_specs=[whole(v) for v in shapes],
         out_shape=[jax.ShapeDtypeStruct(v, f32) for v in shapes],
         compiler_params=params(),
         cost_estimate=cost(0.02),
         name="home_sums",
-    )(spot, *operands, after)
+    )(spot, *pair, after)
 
 
 def add_halves_kernel(fy_ref, keep_ref, got_ref, *rest):
@@ -1030,23 +1073,23 @@
     )(slot, mine, got, *after)
 
 
-def add_parts_kernel(*refs):
-    parts, out_ref = refs[:-1], refs[-1]
+def add_parts_kernel(*refs, number):
+    parts, out_ref = refs[:number], refs[-1]
     out_ref[...] = sum(ref[...].astype(f32) for ref in parts).astype(bf16)
 
 
-def add_parts(parts):
+def add_parts(parts, after=()):
     shape = parts[0].shape
     return pl.pallas_call(
-        add_parts_kernel,
+        functools.partial(add_parts_kernel, number=len(parts)),
         grid=(1,),
-        in_specs=[whole(shape)] * len(parts),
+        in_specs=[whole(shape)] * len(parts) + [pl.BlockSpec(memory_space=pl.ANY)] * len(after),
         out_specs=whole(shape),
         out_shape=jax.ShapeDtypeStruct(shape, bf16),
         compiler_params=params(),
         cost_estimate=cost(0.02),
         name="add_parts",
-    )(*parts)
+    )(*parts, *after)
 
 
 def swap(value, axis):
@@ -1075,9 +1118,11 @@
 def shift_order(experts):
     def key(shift):
         distance = bin(shift >> 1).count("1")
-        return (distance == 0, distance == 1 and shift & 1, distance, shift)
-
-    return sorted(range(experts), key=key)
+        return (shift & 1, distance, shift)
+
+    order = sorted(range(2, experts), key=key)
+    half = len(order) // 2
+    return [order[:half], order[half:], [0, 1]]
 
 
 STRAIGHT = [(0, 0), (1, 2), (2, 1), (3, 3)]
@@ -1133,34 +1178,35 @@
     ids = jnp.pad(route_ids.reshape(images, seq, -1), ((0, 0), (0, stride - seq), (0, 0)), constant_values=-1)
     ids = ids.reshape(images * stride, -1).T
     post, pos, *ups = route(place_ref, ids, grad_output, experts, cap, stride)
-    order = shift_order(experts)
+    groups = shift_order(experts)
     near[1:], post, ups[0] = lax.optimization_barrier((near[1:], post, ups[0]))
-    ups = [value if shift == 0 else exchange(value, shift, experts) for shift, value in enumerate(ups)]
+    for shift in groups[0]:
+        ups[shift] = exchange(ups[shift], shift, experts)
     far += [swap(value, "core") for value in near[1:]]
     homes = [((fy + step) % ways) * 2 for step in range(ways)]
     homes = [home + core for home in homes] + [home + 1 - core for home in homes]
 
-    early = max(1, images * 2 // 5)
+    early = 1
     spots = jnp.stack([place_ref[0], *homes])
-    size = max(1, experts // 4)
-    firsts = [ups[shift] for shift in order[:size]]
+    firsts = [ups[shift] for shift in groups[0]]
     begun = list(forward(spots, tokens, near + far, None, [], 0, early, experts, stride, rows))
     pay, straight, begun[0] = lax.optimization_barrier((pay, straight, begun[0]))
     crossed = lax.ppermute(pay, ("hi", "core"), CROSSED)
     pays = around(straight, "fy", ways)
     pay_homes = [((fy + step) % ways) * 2 + high for step in range(ways)]
     *saved, mid, peak, pack = forward(
-        spots, tokens, [], begun, [straight, *firsts], early, images - early, experts, stride, rows
+        spots, tokens, [], begun, [straight], early, images - early, experts, stride, rows
     )
     mid = mid.reshape(images * stride, width)
-    crossed, mid = lax.optimization_barrier((crossed, mid))
-    seconds = [ups[shift] for shift in order[size : 2 * size]]
-    sent = dispatch(post, mid, [crossed, *pays[1:], *seconds], experts, cap)
+    paired = tuple(shift for group in groups[1:] for shift in group)
+    sent = dispatch(post, mid, ups, paired, [], experts, cap)
+    crossed, sent[0], firsts, *pays[1:] = lax.optimization_barrier((crossed, sent[0], firsts, *pays[1:]))
+    for shift, value in zip(groups[0], firsts):
+        ups[shift] = value
     pays += around(crossed, "fy", ways)
     pay_homes += [((fy + step) % ways) * 2 + 1 - high for step in range(ways)]
     expert_spots = jnp.stack([place_ref[0], fy, *pay_homes])
 
-    groups = [order[at : at + size] for at in range(0, experts, size)]
     arrived = {}
 
     def send(number, after):
@@ -1169,15 +1215,16 @@
             arrived[shift] = value if shift == 0 else exchange(value, shift, experts)
         return after
 
-    send(0, ())
-    send(1, [arrived[shift] for shift in groups[0]])
+    send(0, [sent[0]])
+    first = send(1, [arrived[shift] for shift in groups[0]])
+    arrived.update(zip(groups[0], first))
     old, after = None, []
     backs = {}
     for number, group in enumerate(groups):
         result = expert_call(
             expert_spots,
             [arrived[shift] for shift in group],
-            [ups[shift] for shift in group],
+            [arrived[shift] if shift in paired else ups[shift] for shift in group],
             pays,
             pack,
             old,
@@ -1196,11 +1243,12 @@
             backs[shift] = out[at] if shift == 0 else exchange(out[at], shift, experts)
     backs = [backs[shift] for shift in range(experts)]
     made, *grad = old
-    made, backs = lax.optimization_barrier((made, backs))
     made = lax.all_to_all(made, GROUP, split_axis=0, concat_axis=0, tiled=True)
 
+    shifts = tuple(range(2, experts))
+    part_sums = returned(pos, backs[2:], shifts, rows, cap)
     hidden_grad, mixed_grad, sums = middle(
-        place_ref, grad_output, pack, pos, saved, backs, [], cap, experts
+        place_ref, grad_output, pack, pos, saved, part_sums, backs[:2], cap, experts
     )
     head_rows = 3 * (3 * width // LANES) + 4
     devices = 2 * experts // 2 * fsdp
@@ -1246,23 +1294,29 @@
         mine, theirs = add_halves(fy.reshape(1), keep, got, after)
         theirs, qkv_grad = lax.optimization_barrier((theirs, qkv_grad))
         input_grad = first_norm(tokens, qkv_grad, pack, hidden_grad)
-        parts = split_rows(low.reshape(1), mine, swap(theirs, "fy"), [output, input_grad], near_by)
+        parts = split_rows(low.reshape(1), mine, swap(theirs, "fy"), [input_grad, output, *home_one], near_by)
         total = add_parts(spread(parts))
-        total = add_parts([total, swap(total, "hi")])
+        shapes = [(hidden_part, width), (1, hidden_part), (1, part)]
+        grad_w2, grad_b1, grad_b2 = home_sums(home_second_kernel, spot.reshape(1), home_two, total, shapes)
+        shapes = [(part, hidden_part * fsdp)]
+        (grad_w1,) = home_sums(home_first_kernel, spot.reshape(1), home_one, total, shapes)
+        total = add_parts([total, swap(total, "hi")], [grad_w2, grad_w1])
         total = spread([total] * near_by)
     else:
         sums = split_sum((keep.astype(f32) + got.astype(f32)).astype(bf16), "fy", ways)
         total = [lax.psum(sums, ("hi", "lo"))]
+        shapes = [(hidden_part, width), (1, hidden_part), (1, part)]
+        grad_w2, grad_b1, grad_b2 = home_sums(home_second_kernel, spot.reshape(1), home_two, total[0], shapes)
+        shapes = [(part, hidden_part * fsdp)]
+        (grad_w1,) = home_sums(home_first_kernel, spot.reshape(1), home_one, total[0], shapes)
         input_grad = first_norm(tokens, qkv_grad, pack, hidden_grad)
     if not members:
         peak = jnp.max(lax.all_gather(peak, DEVICE, axis=0, tiled=True), axis=0, keepdims=True)
     limit = jnp.pad(clip_threshold.astype(f32).reshape(1, HEADS), ((0, 0), (0, LANES - HEADS)), constant_values=1.0)
-    grad_qkv, grad_out, grad_router, grads, clipped = finish(
+    grad_qkv, grad_out, grad_router, clipped, *grads = finish(
         low.reshape(1), total, own, limit, peak, width, experts, head_rows, members
     )
-    grad_w1, grad_w2, grad_b1, grad_b2 = home_sums(
-        spot.reshape(1), home_two, home_one, total[0], hidden_part, part, fsdp
-    )
+    grads = [v.reshape(part) for v in grads]
     return (
         output,
         input_grad,

time: 371 us -> 334 us (0.900)
  Pallas kernels: 241 us -> 213 us
  local copies, waits for them, and re-layouts: 12.4 us -> 6.64 us
  starting transfers between devices: 58.2 us -> 54 us
    pallas_call x4 -> x3, Pallas kernels: 104 us -> 87.5 us  [expert_call(): pl.pallas_call(functools.partial(expert_kernel, cap=cap, group=group, fir...]
    pallas_call x2, Pallas kernels: 32.5 us -> 19.1 us  [forward(): pl.pallas_call(functools.partial(forward_kernel, experts=experts, fsdp=le...]
    pallas_call x4 -> x6, Pallas kernels: 16.2 us -> 28.5 us  [the longest x1 11.4 us: dispatch(): pl.pallas_call(functools.partial(dispatch_kernel, cap=cap, paired=paired,...]
    ppermute x2, waiting for transfers between devices: 0.01 us -> 11.3 us  [homeward(): lax.ppermute(crossed, ('hi', 'core'), BACK_CROSSED)]
    ppermute x21 -> x17, waiting for transfers between devices: 31.6 us -> 22.9 us  [exchange(): return lax.ppermute(value, GROUP, [(k, k ^ shift) for k in range(experts)])]
    ppermute x2, starting transfers between devices: 11.2 us -> 3.38 us  [homeward(): lax.ppermute(straight, ('hi', 'core'), BACK)]
    ppermute x1, starting transfers between devices: 1.88 us -> 9.64 us  [shards(): straight = lax.ppermute(pay, ('hi', 'core'), STRAIGHT)]
    pallas_call x1, Pallas kernels: 18.1 us -> 12.5 us  [middle(): pl.pallas_call(functools.partial(middle_kernel, cap=cap, experts=experts)...]
  transfers between devices with their start and end apart: 44 -> 40, of which waited for: 13 -> 15; matrix products, arithmetic and copies ran while one was open for 1% -> 1% of each run, Pallas kernels for 57% -> 61%
where the time goes in v3:
time: 334 us; the launch traced here: 328 us
  Pallas kernels  213 us (64%)
  starting transfers between devices  54 us (16%)
  waiting for transfers between devices  52.7 us (16%)
  local copies, waits for them, and re-layouts  6.64 us (2%)
    pallas_call x3, Pallas kernels, expert_call(): pl.pallas_call(functools.partial(expert_kernel, cap=cap, group=group, fir...  87.5 us
    ppermute x17, waiting for transfers between devices, exchange(): return lax.ppermute(value, GROUP, [(k, k ^ shift) for k in range(experts)])  22.9 us
    pallas_call x1, Pallas kernels, backward(): pl.pallas_call(functools.partial(backward_kernel, head_rows=head_rows, me...  22.6 us
    pallas_call x2, Pallas kernels, forward(): pl.pallas_call(functools.partial(forward_kernel, experts=experts, fsdp=le...  19.1 us
    ppermute x17, starting transfers between devices, exchange(): return lax.ppermute(value, GROUP, [(k, k ^ shift) for k in range(experts)])  18.4 us
    pallas_call x1, Pallas kernels, middle(): pl.pallas_call(functools.partial(middle_kernel, cap=cap, experts=experts)...  12.5 us
    ppermute x6, waiting for transfers between devices, spread(): lax.ppermute(value, 'lo', [(j, j ^ k) for j in range(near_by)])  11.8 us
    pallas_call x1, Pallas kernels, dispatch(): pl.pallas_call(functools.partial(dispatch_kernel, cap=cap, paired=paired,...  11.4 us
  transfers between devices with their start and end apart: 40, of which 15 were waited for; matrix products, arithmetic and copies ran while one was open for 1% of the time, Pallas kernels for 61%

profile of v3, /device:TPU:0, one launch (start us, length us, event | category | flops | bytes accessed | tf_op | source)
XLA Modules:
  0.0 328.2 jit_solution(13763567991752182606)
XLA Ops:
  0.7 2.8 pack.1
  3.5 3.0 collective-permute-start
  6.4 9.6 %collective-permute-start.3 = (bf16[1040,512]{1,0:T(8,128)(2,1)}, bf16[1040,512]{1,0:T(8,128)(2,1)}, u32[]{:S(2)}, u32[]{:S(2)}) collective-permute-start(bf16[1040,512]{1,0:T(8,128)(2,1)} %get-tuple-element.149), channel_id=1, source_target_pairs={{0,0},{1,16},{16,1},{17,17},{2,2},{3,18},{18,3},{19,19},{4,4},{5,2... | collective-permute-start | bytes 3194888 | tf_op jit(solution)/shard_map/ppermute | solution.py:1176
  17.5 10.3 %route.1 = (f32[8,1280]{1,0:T(8,128)}, f32[5,256,128]{2,1,0:T(8,128)}, bf16[432,512]{1,0:T(8,128)(2,1)}, bf16[432,512]{1,0:T(8,128)(2,1)}, bf16[432,512]{1,0:T(8...) custom-call(s32[1]{0:T(128)} %bitcast.place_ref, ...), custom_call_target="tpu_custom_call" | custom-call | flops 20000000 | tf_op jit(solution)/shard_map/route/pallas_call | solution.py:198
  32.5 5.7 %attend.2 = (bf16[5,208,1536]{2,1,0:T(8,128)(2,1)}, bf16[5,208,512]{2,1,0:T(8,128)(2,1)}, f32[5,208,512]{2,1,0:T(8,128)}, f32[5,208,128]{2,1,0:T(8,128)}, bf16[5...) custom-call(s32[5]{0:T(128)} %stack.46.spots_ref, ...), custom_call_target="tpu_custom_call" | custom-call | flops 20000000 | tf_op jit(solution)/shard_map/attend/pallas_call | solution.py:360
  41.0 13.4 %attend.3 = (bf16[5,208,1536]{2,1,0:T(8,128)(2,1)}, bf16[5,208,512]{2,1,0:T(8,128)(2,1)}, f32[5,208,512]{2,1,0:T(8,128)}, f32[5,208,128]{2,1,0:T(8,128)}, bf16[5...) custom-call(s32[5]{0:T(128)} %stack.46.spots_ref, ...), custom_call_target="tpu_custom_call", output_to_operand_aliasing={{0}: (4, {}), {1}: (5, {}), {2}: (6, {}), {3}: (7, {}), {4}... | custom-call | flops 80000000000 | tf_op jit(solution)/shard_map/attend/pallas_call | solution.py:360
  54.3 11.4 %dispatch.1 = (bf16[864,512]{1,0:T(8,128)(2,1)}, bf16[864,512]{1,0:T(8,128)(2,1)}, bf16[432,512]{1,0:T(8,128)(2,1)}, bf16[864,512]{1,0:T(8,128)(2,1)}, bf16[432,...) custom-call(f32[8,1280]{1,0:T(8,128)} %get-tuple-element.150.post_ref, ...), custom_call_target="tpu_custom_call" | custom-call | flops 20000000 | tf_op jit(solution)/shard_map/dispatch/pallas_call | solution.py:233
  71.5 8.3 %collective-permute-done.9.refs_0_ = bf16[432,512]{1,0:T(8,128)(2,1)S(1)} collective-permute-done((bf16[432,512]{1,0:T(8,128)(2,1)}, bf16[432,512]{1,0:T(8,128)(2,1)S(1)}, u32[]{:S(2)}, u32[]{:S(2)}) %collective-permute-start.9) | collective-permute-done | bytes 442400 | tf_op jit(solution)/shard_map/ppermute | solution.py:1115
  79.8 2.3 collective-permute-done.10.refs_1_
  82.2 7.9 %collective-permute-done.11.refs_2_ = bf16[432,512]{1,0:T(8,128)(2,1)S(1)} collective-permute-done((bf16[432,512]{1,0:T(8,128)(2,1)}, bf16[432,512]{1,0:T(8,128)(2,1)S(1)}, u32[]{:S(2)}, u32[]{:S(2)}) %collective-permute-start.11) | collective-permute-done | bytes 442400 | tf_op jit(solution)/shard_map/ppermute | solution.py:1115
  92.6 30.9 %expert.3 = (bf16[448,512]{1,0:T(8,128)(2,1)}, bf16[448,512]{1,0:T(8,128)(2,1)}, bf16[448,512]{1,0:T(8,128)(2,1)}, bf16[8,432,512]{2,1,0:T(8,128)(2,1)}, f32[512,2048]{1,0:T(8,128)}, /*index=5*/f32[4,528,512]{2,1,0:T(8,128)}) custom-call(s32[6]{0:T(128)} %stack.52.place_ref, bf16[432,512]{1,0:T(8,128)(2,1)} %copy-done.13, bf16[432,512]{1,0:T(8,128)(2,1)} %copy-done.14, ...), custom_call_target="tpu_custom_call" | custom-call | flops 96000000000 | tf_op jit(solution)/shard_map/expert/pallas_call | solution.py:526
  128.0 3.1 collective-permute-done.16.refs_2_.refs_5_
  131.1 31.8 %expert.4 = (bf16[448,512]{1,0:T(8,128)(2,1)}, bf16[448,512]{1,0:T(8,128)(2,1)}, bf16[448,512]{1,0:T(8,128)(2,1)}, bf16[8,432,512]{2,1,0:T(8,128)(2,1)}, f32[512,2048]{1,0:T(8,128)}, /*index=5*/f32[4,528,512]{2,1,0:T(8,128)}) custom-call(s32[6]{0:T(128)} %stack.52.place_ref, ...), custom_call_target="tpu_custom_call", output_to_operand_aliasing={{3}: (12, {})} | custom-call | flops 96000000000 | tf_op jit(solution)/shard_map/expert/pallas_call | solution.py:526
  165.1 2.6 collective-permute-start.22
  167.7 24.8 %expert.5 = (bf16[448,512]{1,0:T(8,128)(2,1)}, bf16[448,512]{1,0:T(8,128)(2,1)}, bf16[8,432,512]{2,1,0:T(8,128)(2,1)}, bf16[2,528,512]{2,1,0:T(8,128)(2,1)}, bf1...) custom-call(s32[6]{0:T(128)} %stack.52.place_ref, ...), custom_call_target="tpu_custom_call", output_to_operand_aliasing={{2}: (10, {})} | custom-call | flops 96000000000 | tf_op jit(solution)/shard_map/expert/pallas_call | solution.py:526
  192.6 4.6 %all-to-all-start = ((bf16[8,432,512]{2,1,0:T(8,128)(2,1)}), bf16[8,432,512]{2,1,0:T(8,128)(2,1)}, u32[]{:S(2)}, u32[]{:S(2)}) async-start(bf16[8,432,512]{2,1,0:T(8,128)(2,1)} %get-tuple-element.197), calls=%async_computation | async-start | bytes 7077888 | tf_op jit(solution)/shard_map/all_to_all | solution.py:1246
  199.1 9.0 %returned.1 = (f32[5,208,512]{2,1,0:T(8,128)}, f32[5,208,128]{2,1,0:T(8,128)}) custom-call(f32[5,256,128]{2,1,0:T(8,128)} %get-tuple-element.132.pos_ref, bf16[448,512]{1,0:T(8,128)(2,1)} %collective-permute-done.17.refs_12_.refs_0_, bf16[448,512]{1,0:T(8,128)(2,1)} %collective-permute-done.20.refs_1_, ...), custom_call_target="tpu_custom_call" | custom-call | flops 99999997952 | tf_op jit(solution)/shard_map/returned/pallas_call | solution.py:599
  208.9 12.5 %middle.1 = (f32[5,208,512]{2,1,0:T(8,128)}, bf16[5,208,512]{2,1,0:T(8,128)(2,1)}, f32[512,640]{1,0:T(8,128)}) custom-call(s32[1]{0:T(128)} %bitcast.place_ref, bf16[5,197,512]{2,1,0:T(8,128)(2,1)} %up_ref.3, bf16[512,2176]{1,0:T(8,128)(2,1)} %get-tuple-element.137.rest_0_.refs_10_.refs_8_.wout_ref.misc_ref.wqkv_ref, ...), custom_call_target="tpu_custom_call" | custom-call | flops 20000000 | tf_op jit(solution)/shard_map/middle/pallas_call | solution.py:680
  221.5 2.4 collective-permute-done.25.got_ref
  223.9 2.7 half_sums.2
  230.4 22.6 %attend_back.1 = (bf16[5,208,1536]{2,1,0:T(8,128)(2,1)}, bf16[2,128,2304]{2,1,0:T(8,128)(2,1)}, bf16[2,128,2304]{2,1,0:T(8,128)(2,1)}) custom-call(s32[2]{0:T(128)} %pad_add_fusion.spots_ref, bf16[5,197,512]{2,1,0:T(8,128)(2,1)} %tok_ref.7, bf16[5,208,1536]{2,1,0:T(8,128)(2,1)} %get-tuple-element.198.qkv_ref, ...), custom_call_target="tpu_custom_call" | custom-call | flops 50000000 | tf_op jit(solution)/shard_map/attend_back/pallas_call | solution.py:802
  253.1 3.6 %collective-permute-done.28.rest_1_.two = bf16[528,512]{1,0:T(8,128)(2,1)} collective-permute-done((bf16[528,512]{1,0:T(8,128)(2,1)}, bf16[528,512]{1,0:T(8,128)(2,1)}, u32[]{:S(2)}, u32[]{:S(2)}) %collective-permute-start.28) | collective-permute-done | bytes 540704 | tf_op jit(solution)/shard_map/ppermute | solution.py:1261
  256.7 2.7 half_sums.3
  259.4 2.8 add_halves.1
  265.0 8.0 %first_norm.1.refs_0_ = f32[5,197,512]{2,1,0:T(8,128)} custom-call(bf16[5,197,512]{2,1,0:T(8,128)(2,1)} %tok_ref.7, bf16[5,208,1536]{2,1,0:T(8,128)(2,1)} %get-tuple-element.225.qkv_grad_ref, bf16[512,2176]{1,0:T(8,128)(2,1)} %get-tuple-element.137.rest_0_.refs_10_.refs_8_.wout_ref.misc_ref.wqkv_ref, ...), custom_call_target="tpu_custom_call" | custom-call | flops 20000000 | tf_op jit(solution)/shard_map/first_norm/pallas_call | solution.py:855
  273.0 8.5 %combine.1.refs_1_ = bf16[5,197,512]{2,1,0:T(8,128)(2,1)} custom-call(s32[1]{0:T(128)} %bitcast.place_ref, f32[5,256,128]{2,1,0:T(8,128)} %get-tuple-element.132.pos_ref, f32[5,208,512]{2,1,0:T(8,128)} %get-tuple-element.148.hidden_ref, bf16[8,432,512]{2,1,0:T(8,128)(2,1)} %all-to-all-done.made_ref), custom_call_target="tpu_custom_call" | custom-call | flops 20000000 | tf_op jit(solution)/shard_map/combine/pallas_call | solution.py:890
  281.4 7.7 %collective-permute-done.31.refs_3_.two = bf16[512,512]{1,0:T(8,128)(2,1)} collective-permute-done((bf16[512,512]{1,0:T(8,128)(2,1)}, bf16[512,512]{1,0:T(8,128)(2,1)}, u32[]{:S(2)}, u32[]{:S(2)}) %collective-permute-start.31) | collective-permute-done | bytes 524320 | tf_op jit(solution)/shard_map/ppermute | solution.py:1261
  289.1 2.3 split_rows.1
  294.9 2.9 collective-permute-done.32.refs_1_
  308.5 4.2 %collective-permute-done.35.refs_1_ = bf16[32,2304]{1,0:T(8,128)(2,1)S(1)} collective-permute-done((bf16[32,2304]{1,0:T(8,128)(2,1)}, bf16[32,2304]{1,0:T(8,128)(2,1)S(1)}, u32[]{:S(2)}, u32[]{:S(2)}) %collective-permute-start.35) | collective-permute-done | bytes 147488 | tf_op jit(solution)/shard_map/ppermute | solution.py:1096
  319.1 2.7 collective-permute-done.36.refs_1_
  325.2 2.8 finish.1
  (112 shorter events, 57.0 us)
Async XLA Ops:
  3.5 24.3 %collective-permute-start = (bf16[128,2176]{1,0:T(8,128)(2,1)}, bf16[128,2176]{1,0:T(8,128)(2,1)S(1)}, u32[]{:S(2)}, u32[]{:S(2)}) collective-permute-start(bf16[128,2176]{1,0:T(8,128)(2,1)} %get-tuple-element.133.rest_0_.refs_4_), channel_id=1, source_target_pairs={{2,0},{0,2},{3,1},{1,3},{6,4},{4,6},{7,5},{5,7},{10,8},{8,10},{11,... | collective-permute-start | bytes 1671176 | tf_op jit(solution)/shard_map/ppermute | solution.py:1101
  6.4 31.7 %collective-permute-start.3 = (bf16[1040,512]{1,0:T(8,128)(2,1)}, bf16[1040,512]{1,0:T(8,128)(2,1)}, u32[]{:S(2)}, u32[]{:S(2)}) collective-permute-start(bf16[1040,512]{1,0:T(8,128)(2,1)} %get-tuple-element.149), channel_id=1, source_target_pairs={{0,0},{1,16},{16,1},{17,17},{2,2},{3,18},{18,3},{19,19},{4,4},{5,2... | collective-permute-start | bytes 3194888 | tf_op jit(solution)/shard_map/ppermute | solution.py:1176
  16.1 16.0 %collective-permute-start.1 = (bf16[128,2176]{1,0:T(8,128)(2,1)}, bf16[128,2176]{1,0:T(8,128)(2,1)}, u32[]{:S(2)}, u32[]{:S(2)}) collective-permute-start(bf16[128,2176]{1,0:T(8,128)(2,1)} %get-tuple-element.133.rest_0_.refs_4_), channel_id=1, source_target_pairs={{0,1},{1,0},{2,3},{3,2},{4,5},{5,4},{6,7},{7,6},{8,9},{9,8},{10,11... | collective-permute-start | bytes 1671176 | tf_op jit(solution)/shard_map/ppermute | solution.py:1096
  28.4 37.3 %collective-permute-start.5 = (bf16[432,512]{1,0:T(8,128)(2,1)}, bf16[432,512]{1,0:T(8,128)(2,1)}, u32[]{:S(2)}, u32[]{:S(2)}) collective-permute-start(bf16[432,512]{1,0:T(8,128)(2,1)} %get-tuple-element.158), channel_id=1, source_target_pairs={{0,4},{1,5},{4,0},{5,1},{8,12},{9,13},{12,8},{13,9},{2,6},{3,7},{6... | collective-permute-start | bytes 1327112 | tf_op jit(solution)/shard_map/ppermute | solution.py:1115
  29.9 35.8 %collective-permute-start.6 = (bf16[432,512]{1,0:T(8,128)(2,1)}, bf16[432,512]{1,0:T(8,128)(2,1)}, u32[]{:S(2)}, u32[]{:S(2)}) collective-permute-start(bf16[432,512]{1,0:T(8,128)(2,1)} %get-tuple-element.159), channel_id=1, source_target_pairs={{0,8},{1,9},{4,12},{5,13},{8,0},{9,1},{12,4},{13,5},{2,10},{3,11},... | collective-permute-start | bytes 1327112 | tf_op jit(solution)/shard_map/ppermute | solution.py:1115
  32.1 34.8 %collective-permute-start.7 = (bf16[432,512]{1,0:T(8,128)(2,1)}, bf16[432,512]{1,0:T(8,128)(2,1)}, u32[]{:S(2)}, u32[]{:S(2)}) collective-permute-start(bf16[432,512]{1,0:T(8,128)(2,1)} %get-tuple-element.160), channel_id=1, source_target_pairs={{0,12},{1,13},{4,8},{5,9},{8,4},{9,5},{12,0},{13,1},{2,14},{3,15},... | collective-permute-start | bytes 1327112 | tf_op jit(solution)/shard_map/ppermute | solution.py:1115
  38.2 28.7 %collective-permute-start.4 = (bf16[1040,512]{1,0:T(8,128)(2,1)}, bf16[1040,512]{1,0:T(8,128)(2,1)}, u32[]{:S(2)}, u32[]{:S(2)}) collective-permute-start(bf16[1040,512]{1,0:T(8,128)(2,1)} %get-tuple-element.149), channel_id=1, source_target_pairs={{0,16},{1,0},{16,17},{17,1},{2,18},{3,2},{18,19},{19,3},{4,20},{5,... | collective-permute-start | bytes 3194888 | tf_op jit(solution)/shard_map/ppermute | solution.py:1194
  40.5 26.4 %collective-permute-start.8 = (bf16[1040,512]{1,0:T(8,128)(2,1)}, bf16[1040,512]{1,0:T(8,128)(2,1)}, u32[]{:S(2)}, u32[]{:S(2)}) collective-permute-start(bf16[1040,512]{1,0:T(8,128)(2,1)} %collective-permute-done.3.rest_8_.refs_6_.refs_4_), channel_id=1, source_target_pairs={{2,0},{0,2},{3,1},{1,3},{6,4},{4,6},{7,5},{5,7},{10,8},{8,10},{11,... | collective-permute-start | bytes 3194888 | tf_op jit(solution)/shard_map/ppermute | solution.py:1101
  66.9 25.8 %collective-permute-start.12 = (bf16[1040,512]{1,0:T(8,128)(2,1)}, bf16[1040,512]{1,0:T(8,128)(2,1)}, u32[]{:S(2)}, u32[]{:S(2)}) collective-permute-start(bf16[1040,512]{1,0:T(8,128)(2,1)} %collective-permute-done.4.refs_8_.refs_6_), channel_id=1, source_target_pairs={{2,0},{0,2},{3,1},{1,3},{6,4},{4,6},{7,5},{5,7},{10,8},{8,10},{11,... | collective-permute-start | bytes 3194888 | tf_op jit(solution)/shard_map/ppermute | solution.py:1101
  67.4 12.4 %collective-permute-start.9 = (bf16[432,512]{1,0:T(8,128)(2,1)}, bf16[432,512]{1,0:T(8,128)(2,1)S(1)}, u32[]{:S(2)}, u32[]{:S(2)}) collective-permute-start(bf16[432,512]{1,0:T(8,128)(2,1)} %get-tuple-element.169), channel_id=1, source_target_pairs={{0,4},{1,5},{4,0},{5,1},{8,12},{9,13},{12,8},{13,9},{2,6},{3,7},{6... | collective-permute-start | bytes 1327112 | tf_op jit(solution)/shard_map/ppermute | solution.py:1115
  68.8 13.3 %collective-permute-start.10 = (bf16[432,512]{1,0:T(8,128)(2,1)}, bf16[432,512]{1,0:T(8,128)(2,1)S(1)}, u32[]{:S(2)}, u32[]{:S(2)}) collective-permute-start(bf16[432,512]{1,0:T(8,128)(2,1)} %get-tuple-element.170), channel_id=1, source_target_pairs={{0,8},{1,9},{4,12},{5,13},{8,0},{9,1},{12,4},{13,5},{2,10},{3,11},... | collective-permute-start | bytes 1327112 | tf_op jit(solution)/shard_map/ppermute | solution.py:1115
  70.4 19.7 %collective-permute-start.11 = (bf16[432,512]{1,0:T(8,128)(2,1)}, bf16[432,512]{1,0:T(8,128)(2,1)S(1)}, u32[]{:S(2)}, u32[]{:S(2)}) collective-permute-start(bf16[432,512]{1,0:T(8,128)(2,1)} %get-tuple-element.171), channel_id=1, source_target_pairs={{0,12},{1,13},{4,8},{5,9},{8,4},{9,5},{12,0},{13,1},{2,14},{3,15},... | collective-permute-start | bytes 1327112 | tf_op jit(solution)/shard_map/ppermute | solution.py:1115
  90.1 35.1 %collective-permute-start.14 = (bf16[864,512]{1,0:T(8,128)(2,1)}, bf16[864,512]{1,0:T(8,128)(2,1)}, u32[]{:S(2)}, u32[]{:S(2)}) collective-permute-start(bf16[864,512]{1,0:T(8,128)(2,1)} %get-tuple-element.185), channel_id=1, source_target_pairs={{0,5},{1,4},{4,1},{5,0},{8,13},{9,12},{12,9},{13,8},{2,7},{3,6},{6... | collective-permute-start | bytes 2654216 | tf_op jit(solution)/shard_map/ppermute | solution.py:1115
  90.9 35.1 %collective-permute-start.15 = (bf16[864,512]{1,0:T(8,128)(2,1)}, bf16[864,512]{1,0:T(8,128)(2,1)}, u32[]{:S(2)}, u32[]{:S(2)}) collective-permute-start(bf16[864,512]{1,0:T(8,128)(2,1)} %get-tuple-element.186), channel_id=1, source_target_pairs={{0,9},{1,8},{4,13},{5,12},{8,1},{9,0},{12,5},{13,4},{2,11},{3,10},... | collective-permute-start | bytes 2654216 | tf_op jit(solution)/shard_map/ppermute | solution.py:1115
  91.4 39.7 %collective-permute-start.16 = (bf16[864,512]{1,0:T(8,128)(2,1)}, bf16[864,512]{1,0:T(8,128)(2,1)}, u32[]{:S(2)}, u32[]{:S(2)}) collective-permute-start(bf16[864,512]{1,0:T(8,128)(2,1)} %get-tuple-element.187), channel_id=1, source_target_pairs={{0,13},{1,12},{4,9},{5,8},{8,5},{9,4},{12,1},{13,0},{2,15},{3,14},... | collective-permute-start | bytes 2654216 | tf_op jit(solution)/shard_map/ppermute | solution.py:1115
  123.6 44.2 %collective-permute-start.13 = (bf16[864,512]{1,0:T(8,128)(2,1)S(1)}, bf16[864,512]{1,0:T(8,128)(2,1)}, u32[]{:S(2)}, u32[]{:S(2)}) collective-permute-start(bf16[864,512]{1,0:T(8,128)(2,1)S(1)} %copy-done.11), channel_id=1, source_target_pairs={{0,1},{1,0},{4,5},{5,4},{8,9},{9,8},{12,13},{13,12},{2,3},{3,2},{6... | collective-permute-start | bytes 2654216 | tf_op jit(solution)/shard_map/ppermute | solution.py:1115
  124.5 40.6 %collective-permute-start.17 = (bf16[448,512]{1,0:T(8,128)(2,1)}, bf16[448,512]{1,0:T(8,128)(2,1)}, u32[]{:S(2)}, u32[]{:S(2)}) collective-permute-start(bf16[448,512]{1,0:T(8,128)(2,1)} %get-tuple-element.194), channel_id=1, source_target_pairs={{0,4},{1,5},{4,0},{5,1},{8,12},{9,13},{12,8},{13,9},{2,6},{3,7},{6... | collective-permute-start | bytes 1376264 | tf_op jit(solution)/shard_map/ppermute | solution.py:1115
  125.2 39.9 %collective-permute-start.18 = (bf16[448,512]{1,0:T(8,128)(2,1)}, bf16[448,512]{1,0:T(8,128)(2,1)}, u32[]{:S(2)}, u32[]{:S(2)}) collective-permute-start(bf16[448,512]{1,0:T(8,128)(2,1)} %get-tuple-element.195), channel_id=1, source_target_pairs={{0,8},{1,9},{4,12},{5,13},{8,0},{9,1},{12,4},{13,5},{2,10},{3,11},... | collective-permute-start | bytes 1376264 | tf_op jit(solution)/shard_map/ppermute | solution.py:1115
  126.0 41.8 %collective-permute-start.19 = (bf16[448,512]{1,0:T(8,128)(2,1)}, bf16[448,512]{1,0:T(8,128)(2,1)}, u32[]{:S(2)}, u32[]{:S(2)}) collective-permute-start(bf16[448,512]{1,0:T(8,128)(2,1)} %get-tuple-element.196), channel_id=1, source_target_pairs={{0,12},{1,13},{4,8},{5,9},{8,4},{9,5},{12,0},{13,1},{2,14},{3,15},... | collective-permute-start | bytes 1376264 | tf_op jit(solution)/shard_map/ppermute | solution.py:1115
  162.9 36.2 %collective-permute-start.20 = (bf16[448,512]{1,0:T(8,128)(2,1)}, bf16[448,512]{1,0:T(8,128)(2,1)}, u32[]{:S(2)}, u32[]{:S(2)}) collective-permute-start(bf16[448,512]{1,0:T(8,128)(2,1)} %get-tuple-element.202), channel_id=1, source_target_pairs={{0,5},{1,4},{4,1},{5,0},{8,13},{9,12},{12,9},{13,8},{2,7},{3,6},{6... | collective-permute-start | bytes 1376264 | tf_op jit(solution)/shard_map/ppermute | solution.py:1115
  165.1 34.0 %collective-permute-start.21 = (bf16[448,512]{1,0:T(8,128)(2,1)}, bf16[448,512]{1,0:T(8,128)(2,1)}, u32[]{:S(2)}, u32[]{:S(2)}) collective-permute-start(bf16[448,512]{1,0:T(8,128)(2,1)} %get-tuple-element.203), channel_id=1, source_target_pairs={{0,9},{1,8},{4,13},{5,12},{8,1},{9,0},{12,5},{13,4},{2,11},{3,10},... | collective-permute-start | bytes 1376264 | tf_op jit(solution)/shard_map/ppermute | solution.py:1115
  165.1 34.0 %collective-permute-start.22 = (bf16[448,512]{1,0:T(8,128)(2,1)}, bf16[448,512]{1,0:T(8,128)(2,1)}, u32[]{:S(2)}, u32[]{:S(2)}) collective-permute-start(bf16[448,512]{1,0:T(8,128)(2,1)} %get-tuple-element.204), channel_id=1, source_target_pairs={{0,13},{1,12},{4,9},{5,8},{8,5},{9,4},{12,1},{13,0},{2,15},{3,14},... | collective-permute-start | bytes 1376264 | tf_op jit(solution)/shard_map/ppermute | solution.py:1115
  192.6 80.4 %all-to-all-start = ((bf16[8,432,512]{2,1,0:T(8,128)(2,1)}), bf16[8,432,512]{2,1,0:T(8,128)(2,1)}, u32[]{:S(2)}, u32[]{:S(2)}) async-start(bf16[8,432,512]{2,1,0:T(8,128)(2,1)} %get-tuple-element.197), calls=%async_computation | async-start | bytes 7077888 | tf_op jit(solution)/shard_map/all_to_all | solution.py:1246
  197.2 10.9 %collective-permute-start.23 = (bf16[448,512]{1,0:T(8,128)(2,1)S(1)}, bf16[448,512]{1,0:T(8,128)(2,1)S(1)}, u32[]{:S(2)}, u32[]{:S(2)}) collective-permute-start(bf16[448,512]{1,0:T(8,128)(2,1)S(1)} %copy-done.12), channel_id=1, source_target_pairs={{0,1},{1,0},{4,5},{5,4},{8,9},{9,8},{12,13},{13,12},{2,3},{3,2},{6... | collective-permute-start | bytes 1376264 | tf_op jit(solution)/shard_map/ppermute | solution.py:1115
  197.6 26.3 %collective-permute-start.25 = (bf16[2,528,512]{2,1,0:T(8,128)(2,1)}, bf16[2,528,512]{2,1,0:T(8,128)(2,1)}, u32[]{:S(2)}, u32[]{:S(2)}) collective-permute-start(bf16[2,528,512]{2,1,0:T(8,128)(2,1)} %get-tuple-element.217), channel_id=1, source_target_pairs={{0,2},{2,0},{1,3},{3,1},{4,6},{6,4},{5,7},{7,5},{8,10},{10,8},{9,1... | collective-permute-start | bytes 3244040 | tf_op jit(solution)/shard_map/ppermute | solution.py:1096
  226.6 30.1 %collective-permute-start.26 = (bf16[2,512,512]{2,1,0:T(8,128)(2,1)}, bf16[2,512,512]{2,1,0:T(8,128)(2,1)}, u32[]{:S(2)}, u32[]{:S(2)}) collective-permute-start(bf16[2,512,512]{2,1,0:T(8,128)(2,1)} %get-tuple-element.219), channel_id=1, source_target_pairs={{0,2},{2,0},{1,3},{3,1},{4,6},{6,4},{5,7},{7,5},{8,10},{10,8},{9,1... | collective-permute-start | bytes 3145736 | tf_op jit(solution)/shard_map/ppermute | solution.py:1096
  228.1 25.0 %collective-permute-start.27 = (bf16[528,512]{1,0:T(8,128)(2,1)}, bf16[528,512]{1,0:T(8,128)(2,1)S(1)}, u32[]{:S(2)}, u32[]{:S(2)}) collective-permute-start(bf16[528,512]{1,0:T(8,128)(2,1)} %get-tuple-element.218), channel_id=1, source_target_pairs={{0,0},{16,1},{1,16},{17,17},{2,2},{18,3},{3,18},{19,19},{4,4},{20,... | collective-permute-start | bytes 1622024 | tf_op jit(solution)/shard_map/ppermute | solution.py:1260
  229.8 26.9 %collective-permute-start.28 = (bf16[528,512]{1,0:T(8,128)(2,1)}, bf16[528,512]{1,0:T(8,128)(2,1)}, u32[]{:S(2)}, u32[]{:S(2)}) collective-permute-start(bf16[528,512]{1,0:T(8,128)(2,1)} %get-tuple-element.220), channel_id=1, source_target_pairs={{16,0},{0,1},{17,16},{1,17},{18,2},{2,3},{19,18},{3,19},{20,4},{4,... | collective-permute-start | bytes 1622024 | tf_op jit(solution)/shard_map/ppermute | solution.py:1261
  262.2 26.9 %collective-permute-start.29 = (bf16[128,2304]{1,0:T(8,128)(2,1)}, bf16[128,2304]{1,0:T(8,128)(2,1)}, u32[]{:S(2)}, u32[]{:S(2)}) collective-permute-start(bf16[128,2304]{1,0:T(8,128)(2,1)} %get-tuple-element.228), channel_id=1, source_target_pairs={{0,2},{2,0},{1,3},{3,1},{4,6},{6,4},{5,7},{7,5},{8,10},{10,8},{9,1... | collective-permute-start | bytes 1769480 | tf_op jit(solution)/shard_map/ppermute | solution.py:1096
  262.8 18.7 %collective-permute-start.30 = (bf16[512,512]{1,0:T(8,128)(2,1)}, bf16[512,512]{1,0:T(8,128)(2,1)S(1)}, u32[]{:S(2)}, u32[]{:S(2)}) collective-permute-start(bf16[512,512]{1,0:T(8,128)(2,1)} %get-tuple-element.221.rest_0_), channel_id=1, source_target_pairs={{0,0},{16,1},{1,16},{17,17},{2,2},{18,3},{3,18},{19,19},{4,4},{20,... | collective-permute-start | bytes 1572872 | tf_op jit(solution)/shard_map/ppermute | solution.py:1260
  264.4 24.7 %collective-permute-start.31 = (bf16[512,512]{1,0:T(8,128)(2,1)}, bf16[512,512]{1,0:T(8,128)(2,1)}, u32[]{:S(2)}, u32[]{:S(2)}) collective-permute-start(bf16[512,512]{1,0:T(8,128)(2,1)} %get-tuple-element.222.rest_1_), channel_id=1, source_target_pairs={{16,0},{0,1},{17,16},{1,17},{18,2},{2,3},{19,18},{3,19},{20,4},{4,... | collective-permute-start | bytes 1572872 | tf_op jit(solution)/shard_map/ppermute | solution.py:1261
  303.9 8.8 %collective-permute-start.35 = (bf16[32,2304]{1,0:T(8,128)(2,1)}, bf16[32,2304]{1,0:T(8,128)(2,1)S(1)}, u32[]{:S(2)}, u32[]{:S(2)}) collective-permute-start(bf16[32,2304]{1,0:T(8,128)(2,1)} %add_parts.2._.__.refs_0_), channel_id=1, source_target_pairs={{0,16},{16,0},{1,17},{17,1},{2,18},{18,2},{3,19},{19,3},{4,20},{20... | collective-permute-start | bytes 442376 | tf_op jit(solution)/shard_map/ppermute | solution.py:1096
  (25 other events, 151.1 us)

commit v4 on v3

--- a/solution.py
+++ b/solution.py
@@ -22,7 +22,8 @@
 TN = (((0,), (0,)), ((), ()))
 DEVICE = ("hi", "lo", "fy", "core")
 GROUP = ("lo", "core")
-VMEM_LIMIT = 63 << 20
+PLACE, FY, CORE, NUMBER, HIGH, SPOT, SAME, LOW, HOMES = range(9)
+VMEM_LIMIT = 64 << 20
 
 
 def dot(a, b, dims):
@@ -117,7 +118,7 @@
     tail[...] = jnp.zeros_like(tail)
     tail[0:1, 0 : b1.shape[1]] = b1[...].astype(f32)
     copies = jnp.concatenate([b2[...].astype(f32)] * (width // part), axis=1)
-    tail[1:2] = jnp.where(iota((1, width), 1) // part == spot_ref[0], copies, 0.0)
+    tail[1:2] = jnp.where(iota((1, width), 1) // part == spot_ref[SPOT], copies, 0.0)
     tall = hidden + TAIL
     pay_ref[hidden:tall] = tail[...].astype(bf16)
     for index in range(width // part):
@@ -157,8 +158,8 @@
     return jnp.where(slots == column, 1.0, 0.0).astype(bf16)
 
 
-def route_kernel(place_ref, ids_ref, up_ref, post_ref, pos_ref, *rest, cap, stride):
-    outs, gathered = rest[:-1], rest[-1]
+def route_kernel(place_ref, ids_ref, up_ref, hot_ref, pos_ref, *rest, cap, stride):
+    outs, gathered, post_ref = rest[:-2], rest[-2], rest[-1]
     experts = post_ref.shape[0]
     images, seq, width = up_ref.shape
     step = pl.program_id(0)
@@ -170,7 +171,8 @@
         carry = jnp.zeros((experts, 1), f32)
         gathered[...] = jnp.zeros_like(gathered)
         for image in range(images):
-            ids = ids_ref[:, image * stride : (image + 1) * stride]
+            ids = ids_ref[:, image * seq : (image + 1) * seq]
+            ids = jnp.concatenate([ids, jnp.full((ids.shape[0], stride - seq), -1, i32)], axis=1)
             hit = jnp.zeros((experts, stride), jnp.bool_)
             for choice in range(ids_ref.shape[0]):
                 hit = hit | (ids[choice : choice + 1] == expert)
@@ -184,6 +186,7 @@
             gathered[image * stride : image * stride + seq] = up_ref[image]
 
     hot = one_hot_rows(post_ref[pl.ds(step, 1), :], cap)
+    hot_ref[0] = hot
     made = dot(hot, gathered[...], NN).astype(bf16)
     for index in range(experts):
 
@@ -199,50 +202,54 @@
         functools.partial(route_kernel, cap=cap, stride=stride),
         grid=(experts,),
         in_specs=[pl.BlockSpec(memory_space=pltpu.SMEM), whole(ids.shape), whole(grad_output.shape)],
-        out_specs=[whole((experts, total)), whole((images, stride, LANES))] + [whole((cap, width))] * experts,
+        out_specs=[pl.BlockSpec((1, cap, total), lambda s: (s, 0, 0)), whole((images, stride, LANES))]
+        + [whole((cap, width))] * experts,
         out_shape=[
-            jax.ShapeDtypeStruct((experts, total), f32),
+            jax.ShapeDtypeStruct((experts, cap, total), bf16),
             jax.ShapeDtypeStruct((images, stride, LANES), f32),
         ]
         + [jax.ShapeDtypeStruct((cap, width), bf16)] * experts,
-        scratch_shapes=[pltpu.VMEM((total, width), bf16)],
+        scratch_shapes=[pltpu.VMEM((total, width), bf16), pltpu.VMEM((experts, total), f32)],
         compiler_params=params(),
         cost_estimate=cost(0.02),
         name="route",
     )(place, ids, grad_output)
 
 
-def dispatch_kernel(post_ref, rows_ref, *refs, cap, paired, skip):
-    ups, outs = refs[: len(paired)], refs[len(paired) + skip :]
+def dispatch_kernel(_, hot_ref, rows_ref, *refs, cap, shifts, paired):
+    pairs = [shift for shift in shifts if shift in paired]
+    ups, outs = refs[: len(pairs)], refs[len(pairs) :]
     step = pl.program_id(0)
-    hot = one_hot_rows(post_ref[pl.ds(step, 1), :], cap)
-    sent = dot(hot, rows_ref[...], NN).astype(bf16)
-    for index in range(len(outs)):
+    sent = dot(hot_ref[0], rows_ref[...], NN).astype(bf16)
+    for index, shift in enumerate(shifts):
 
         @pl.when(step == index)
         def _():
             outs[index][0:cap] = sent
-            if index in paired:
-                outs[index][cap:] = ups[paired.index(index)][...]
-
-
-def dispatch(post, rows, ups, paired, after, experts, cap):
+            if shift in pairs:
+                outs[index][cap:] = ups[pairs.index(shift)][...]
+
+
+def dispatch(hot, rows, ups, shifts, paired):
+    _, cap, total = hot.shape
     width = rows.shape[1]
-    shapes = [((2 if shift in paired else 1) * cap, width) for shift in range(experts)]
-    return list(
-        pl.pallas_call(
-            functools.partial(dispatch_kernel, cap=cap, paired=paired, skip=len(after)),
-            grid=(experts,),
-            in_specs=[whole(post.shape), whole(rows.shape)]
-            + [whole((cap, width))] * len(paired)
-            + [pl.BlockSpec(memory_space=pl.ANY)] * len(after),
+    shapes = [((2 if shift in paired else 1) * cap, width) for shift in shifts]
+    pairs = [ups[shift] for shift in shifts if shift in paired]
+    outs = pl.pallas_call(
+        functools.partial(dispatch_kernel, cap=cap, shifts=tuple(shifts), paired=paired),
+        grid_spec=pltpu.PrefetchScalarGridSpec(
+            num_scalar_prefetch=1,
+            grid=(len(shifts),),
+            in_specs=[pl.BlockSpec((1, cap, total), lambda s, table: (table[s], 0, 0)), whole(rows.shape)]
+            + [whole((cap, width))] * len(pairs),
             out_specs=[whole(v) for v in shapes],
-            out_shape=[jax.ShapeDtypeStruct(v, bf16) for v in shapes],
-            compiler_params=params(),
-            cost_estimate=cost(0.02),
-            name="dispatch",
-        )(post, rows, *[ups[shift] for shift in paired], *after)
-    )
+        ),
+        out_shape=[jax.ShapeDtypeStruct(v, bf16) for v in shapes],
+        compiler_params=params(),
+        cost_estimate=cost(0.02),
+        name="dispatch",
+    )(jnp.array(shifts, i32), hot, rows, *pairs)
+    return dict(zip(shifts, outs))
 
 
 def forward_kernel(spots_ref, tok_ref, *rest, experts, fsdp, later):
@@ -264,7 +271,7 @@
         if not later:
             part = shards_of[0].shape[0]
             for index, ref in enumerate(shards_of):
-                pack_ref[pl.ds(pl.multiple_of(spots_ref[1 + index] * part, part), part), :] = ref[...]
+                pack_ref[pl.ds(pl.multiple_of(spots_ref[HOMES + fsdp + index] * part, part), part), :] = ref[...]
         misc = pack_ref[:, wide + width :]
         vectors[...] = misc.astype(f32).T
         router[...] = dot(misc, router_order(spots_ref[0], experts), NN).astype(bf16)
@@ -400,7 +407,7 @@
     def _():
         loads = []
         for index, ref in enumerate(pays):
-            at = place_ref[2 + index]
+            at = place_ref[HOMES + index]
             loads.append(pltpu.make_async_copy(ref.at[0:tall], w2s.at[at], sems_w.at[index, fsdp]))
             for block in range(fsdp):
                 start = tall + block * chunk
@@ -450,7 +457,7 @@
         if tile < width:
             part1 = jnp.concatenate([part1, jnp.zeros((width, width - tile), f32)], axis=1)
         if split:
-            for ref, fy in ((out1, place_ref[1]), (out2, 1 - place_ref[1])):
+            for ref, fy in ((out1, place_ref[FY]), (out2, 1 - place_ref[FY])):
 
                 @pl.when((step >> 1) == fy)
                 def _():
@@ -460,7 +467,7 @@
             at = pl.multiple_of(step * chunk, TAIL)
             for index in range(fsdp):
                 block = part1[index * chunk : (index + 1) * chunk].astype(bf16)
-                for ref, fy in ((out3[0], place_ref[1]), (out3[1], 1 - place_ref[1])):
+                for ref, fy in ((out3[0], place_ref[FY]), (out3[1], 1 - place_ref[FY])):
 
                     @pl.when(index // 2 == fy)
                     def _():
@@ -779,10 +786,10 @@
             for order, piece in enumerate(pieces(jnp.broadcast_to(top, (TAIL, LANES)), 3)):
                 move = jnp.where(iota((LANES, LANES), 1) == iota((LANES, LANES), 0) + order * HEADS, 1.0, 0.0)
                 rows_of = rows_of + dot(piece, move.astype(bf16), NN)
-            spare[pl.ds(head_rows + spots_ref[1], 1), :] = rows_of[0:1]
+            spare[pl.ds(head_rows + spots_ref[NUMBER], 1), :] = rows_of[0:1]
         extra = spare[...].astype(bf16)
         for fy in range(keep_ref.shape[0]):
-            for ref, core in ((keep_ref, spots_ref[0]), (give_ref, 1 - spots_ref[0])):
+            for ref, core in ((keep_ref, spots_ref[CORE]), (give_ref, 1 - spots_ref[CORE])):
                 at = pl.multiple_of((2 * fy + core) * part, part)
                 ref[fy, :, 0:wide] = acc_qkv[pl.ds(at, part), :].astype(bf16)
                 ref[fy, :, wide : wide + width] = sums_ref[pl.ds(at, part), 0:width].astype(bf16)
@@ -910,7 +917,7 @@
     part = own_ref.shape[0]
     for shift, ref in enumerate(parts):
         size = part // number
-        total_ref[pl.ds(pl.multiple_of((slot_ref[0] ^ shift) * size, size), size), :] = ref[...]
+        total_ref[pl.ds(pl.multiple_of((slot_ref[LOW] ^ shift) * size, size), size), :] = ref[...]
     width = out_ref.shape[1]
     wide = 3 * width
     number = wide // LANES
@@ -941,7 +948,7 @@
         peak = jnp.max(peaks, axis=0, keepdims=True)
     else:
         peak = peak_ref[...]
-    limit = limit_ref[...]
+    limit = jnp.concatenate([limit_ref[...].astype(f32), jnp.ones((1, LANES - HEADS), f32)], axis=1)
     root = jnp.sqrt(limit / jnp.maximum(peak, limit))
     place = iota((1, width), 1) // (width // HEADS)
     scale = jnp.zeros((1, width), f32)
@@ -971,7 +978,7 @@
 
 def half_sums_kernel(high_ref, keep_ref, got_ref, *rest):
     straight_ref, crossed_ref = rest[-2:]
-    for ref, core in ((straight_ref, high_ref[0]), (crossed_ref, 1 - high_ref[0])):
+    for ref, core in ((straight_ref, high_ref[HIGH]), (crossed_ref, 1 - high_ref[HIGH])):
         ref[...] = (keep_ref[core].astype(f32) + got_ref[core].astype(f32)).astype(bf16)
 
 
@@ -990,25 +997,29 @@
     )(high, keep, got, *after)
 
 
-def home_second_kernel(spot_ref, one, two, _, w2_ref, b1_ref, b2_ref):
+def both_halves(spot_ref, one, two, own, rows):
+    straight = jnp.where(spot_ref[SAME] == 1, own[rows].astype(f32), one[rows].astype(f32))
+    return straight + two[rows].astype(f32)
+
+
+def home_second_kernel(spot_ref, one, two, own, _, w2_ref, b1_ref, b2_ref):
     tile, width = w2_ref.shape
     part = b2_ref.shape[1]
-    w2_ref[...] = one[0:tile].astype(f32) + two[0:tile].astype(f32)
-    edge = one[tile:].astype(f32) + two[tile:].astype(f32)
+    w2_ref[...] = both_halves(spot_ref, one, two, own, slice(0, tile))
+    edge = both_halves(spot_ref, one, two, own, slice(tile, tile + TAIL))
     b1_ref[...] = edge[0:1, 0:tile]
     b2_ref[...] = sum(
-        jnp.where(spot_ref[0] == index, edge[1:2, index * part : (index + 1) * part], 0.0)
+        jnp.where(spot_ref[SPOT] == index, edge[1:2, index * part : (index + 1) * part], 0.0)
         for index in range(width // part)
     )
 
 
-def home_first_kernel(_, one, two, __, w1_ref):
+def home_first_kernel(spot_ref, one, two, own, _, w1_ref):
     part, hidden = w1_ref.shape
     number = one.shape[0] // part
     tile = hidden // number
     for index in range(number):
-        rows = slice(index * part, (index + 1) * part)
-        total = one[rows].astype(f32) + two[rows].astype(f32)
+        total = both_halves(spot_ref, one, two, own, slice(index * part, (index + 1) * part))
         w1_ref[:, index * tile : (index + 1) * tile] = total[:, 0:tile]
 
 
@@ -1029,7 +1040,7 @@
 
 def add_halves_kernel(fy_ref, keep_ref, got_ref, *rest):
     mine_ref, theirs_ref = rest[-2:]
-    for ref, half in ((mine_ref, fy_ref[0]), (theirs_ref, 1 - fy_ref[0])):
+    for ref, half in ((mine_ref, fy_ref[FY]), (theirs_ref, 1 - fy_ref[FY])):
         ref[...] = (keep_ref[half].astype(f32) + got_ref[half].astype(f32)).astype(bf16)
 
 
@@ -1053,7 +1064,7 @@
     total[...] = (mine_ref[...].astype(f32) + got_ref[...].astype(f32)).astype(bf16)
     size = outs[0].shape[0]
     for shift, ref in enumerate(outs):
-        ref[...] = total[pl.ds(pl.multiple_of((slot_ref[0] ^ shift) * size, size), size), :]
+        ref[...] = total[pl.ds(pl.multiple_of((slot_ref[LOW] ^ shift) * size, size), size), :]
 
 
 def split_rows(slot, mine, got, after, number):
@@ -1118,14 +1129,14 @@
 def shift_order(experts):
     def key(shift):
         distance = bin(shift >> 1).count("1")
-        return (shift & 1, distance, shift)
+        return (shift & 1, -distance, shift)
 
     order = sorted(range(2, experts), key=key)
     half = len(order) // 2
     return [order[:half], order[half:], [0, 1]]
 
 
-STRAIGHT = [(0, 0), (1, 2), (2, 1), (3, 3)]
+STRAIGHT = [(1, 2), (2, 1)]
 CROSSED = [(0, 2), (1, 0), (2, 3), (3, 1)]
 BACK = [(b, a) for a, b in STRAIGHT]
 BACK_CROSSED = [(b, a) for a, b in CROSSED]
@@ -1163,49 +1174,60 @@
     part = w_qkv.shape[0]
     hidden_part = expert_w2.shape[1]
     high, low, fy, core = (lax.axis_index(name).astype(i32) for name in DEVICE)
-    place_ref = (low * 2 + core).reshape(1)
     spot = fy * 2 + core
+    homes = [((fy + step) % ways) * 2 for step in range(ways)]
+    spots = jnp.stack(
+        [
+            low * 2 + core,
+            fy,
+            core,
+            ((high * (experts // 2) + low) * ways + fy) * 2 + core,
+            high,
+            spot,
+            (high == core).astype(i32),
+            low,
+            *[home + high for home in homes],
+            *[home + 1 - high for home in homes],
+            *[home + core for home in homes],
+            *[home + 1 - core for home in homes],
+        ]
+    )
 
     vectors = (ln1_gain, ln1_bias, q_bias, v_bias, out_bias, ln2_gain, ln2_bias)
     own, pay = pack_parameters(
-        spot.reshape(1), w_qkv, w_out, w_router, vectors, expert_w1[0], expert_w2[0], expert_b1, expert_b2
+        spots, w_qkv, w_out, w_router, vectors, expert_w1[0], expert_w2[0], expert_b1, expert_b2
     )
 
     near = around(own, "fy", ways)
     far = [swap(own, "core")]
     straight = lax.ppermute(pay, ("hi", "core"), STRAIGHT)
 
-    ids = jnp.pad(route_ids.reshape(images, seq, -1), ((0, 0), (0, stride - seq), (0, 0)), constant_values=-1)
-    ids = ids.reshape(images * stride, -1).T
-    post, pos, *ups = route(place_ref, ids, grad_output, experts, cap, stride)
+    hot, pos, *ups = route(spots, route_ids.T, grad_output, experts, cap, stride)
     groups = shift_order(experts)
-    near[1:], post, ups[0] = lax.optimization_barrier((near[1:], post, ups[0]))
+    near[1:], hot, ups[0] = lax.optimization_barrier((near[1:], hot, ups[0]))
     for shift in groups[0]:
         ups[shift] = exchange(ups[shift], shift, experts)
     far += [swap(value, "core") for value in near[1:]]
-    homes = [((fy + step) % ways) * 2 for step in range(ways)]
-    homes = [home + core for home in homes] + [home + 1 - core for home in homes]
-
     early = 1
-    spots = jnp.stack([place_ref[0], *homes])
     firsts = [ups[shift] for shift in groups[0]]
     begun = list(forward(spots, tokens, near + far, None, [], 0, early, experts, stride, rows))
     pay, straight, begun[0] = lax.optimization_barrier((pay, straight, begun[0]))
+    straight = jnp.where(high == core, pay, straight)
     crossed = lax.ppermute(pay, ("hi", "core"), CROSSED)
     pays = around(straight, "fy", ways)
-    pay_homes = [((fy + step) % ways) * 2 + high for step in range(ways)]
     *saved, mid, peak, pack = forward(
         spots, tokens, [], begun, [straight], early, images - early, experts, stride, rows
     )
     mid = mid.reshape(images * stride, width)
     paired = tuple(shift for group in groups[1:] for shift in group)
-    sent = dispatch(post, mid, ups, paired, [], experts, cap)
-    crossed, sent[0], firsts, *pays[1:] = lax.optimization_barrier((crossed, sent[0], firsts, *pays[1:]))
+    sent = dispatch(hot, mid, ups, groups[0], paired)
+    sent.update(dispatch(hot, mid, ups, [shift for group in groups[1:] for shift in group], paired))
+    ready = [sent[shift] for shift in groups[0]]
+    crossed, ready, firsts, *pays[1:] = lax.optimization_barrier((crossed, ready, firsts, *pays[1:]))
+    sent.update(zip(groups[0], ready))
     for shift, value in zip(groups[0], firsts):
         ups[shift] = value
     pays += around(crossed, "fy", ways)
-    pay_homes += [((fy + step) % ways) * 2 + 1 - high for step in range(ways)]
-    expert_spots = jnp.stack([place_ref[0], fy, *pay_homes])
 
     arrived = {}
 
@@ -1215,14 +1237,14 @@
             arrived[shift] = value if shift == 0 else exchange(value, shift, experts)
         return after
 
-    send(0, [sent[0]])
+    send(0, ())
     first = send(1, [arrived[shift] for shift in groups[0]])
     arrived.update(zip(groups[0], first))
     old, after = None, []
     backs = {}
     for number, group in enumerate(groups):
         result = expert_call(
-            expert_spots,
+            spots,
             [arrived[shift] for shift in group],
             [arrived[shift] if shift in paired else ups[shift] for shift in group],
             pays,
@@ -1248,22 +1270,21 @@
     shifts = tuple(range(2, experts))
     part_sums = returned(pos, backs[2:], shifts, rows, cap)
     hidden_grad, mixed_grad, sums = middle(
-        place_ref, grad_output, pack, pos, saved, part_sums, backs[:2], cap, experts
+        spots, grad_output, pack, pos, saved, part_sums, backs[:2], cap, experts
     )
     head_rows = 3 * (3 * width // LANES) + 4
     devices = 2 * experts // 2 * fsdp
     members = devices if head_rows + devices <= part else 0
-    device = ((high * (experts // 2) + low) * ways + fy) * 2 + core
-    spots = jnp.stack([core, device])
+
     def homeward(straight, crossed):
         return [
             lax.ppermute(straight, ("hi", "core"), BACK),
             lax.ppermute(crossed, ("hi", "core"), BACK_CROSSED),
+            straight,
         ]
 
-    which = high.reshape(1)
     if len(grad) == 4:
-        sums_two = list(half_sums(which, grad[0], swap(grad[1], "fy"), [sums], 0.02))
+        sums_two = list(half_sums(spots, grad[0], swap(grad[1], "fy"), [sums], 0.02))
         home_two = homeward(*sums_two)
         grad[3], sums_two[0] = lax.optimization_barrier((grad[3], sums_two[0]))
         got_one = swap(grad[3], "fy")
@@ -1279,9 +1300,9 @@
     got = swap(give, "core")
     after = []
     if len(grad) == 4:
-        after = half_sums(which, grad[2], got_one, home_two, 40)
+        after = half_sums(spots, grad[2], got_one, home_two[:2], 40)
         home_one = homeward(*after)
-    output = combine_output(place_ref, pos, saved[2], made, seq)
+    output = combine_output(spots, pos, saved[2], made, seq)
     near_by = experts // 2
     if ways == 2 and part % (TAIL * near_by) == 0:
 
@@ -1291,30 +1312,30 @@
                 for k, value in enumerate(values)
             ]
 
-        mine, theirs = add_halves(fy.reshape(1), keep, got, after)
+        mine, theirs = add_halves(spots, keep, got, after)
         theirs, qkv_grad = lax.optimization_barrier((theirs, qkv_grad))
         input_grad = first_norm(tokens, qkv_grad, pack, hidden_grad)
-        parts = split_rows(low.reshape(1), mine, swap(theirs, "fy"), [input_grad, output, *home_one], near_by)
+        parts = split_rows(spots, mine, swap(theirs, "fy"), [input_grad, output, *home_one[:2]], near_by)
         total = add_parts(spread(parts))
         shapes = [(hidden_part, width), (1, hidden_part), (1, part)]
-        grad_w2, grad_b1, grad_b2 = home_sums(home_second_kernel, spot.reshape(1), home_two, total, shapes)
+        grad_w2, grad_b1, grad_b2 = home_sums(home_second_kernel, spots, home_two, total, shapes)
         shapes = [(part, hidden_part * fsdp)]
-        (grad_w1,) = home_sums(home_first_kernel, spot.reshape(1), home_one, total, shapes)
+        (grad_w1,) = home_sums(home_first_kernel, spots, home_one, total, shapes)
         total = add_parts([total, swap(total, "hi")], [grad_w2, grad_w1])
         total = spread([total] * near_by)
     else:
         sums = split_sum((keep.astype(f32) + got.astype(f32)).astype(bf16), "fy", ways)
         total = [lax.psum(sums, ("hi", "lo"))]
         shapes = [(hidden_part, width), (1, hidden_part), (1, part)]
-        grad_w2, grad_b1, grad_b2 = home_sums(home_second_kernel, spot.reshape(1), home_two, total[0], shapes)
+        grad_w2, grad_b1, grad_b2 = home_sums(home_second_kernel, spots, home_two, total[0], shapes)
         shapes = [(part, hidden_part * fsdp)]
-        (grad_w1,) = home_sums(home_first_kernel, spot.reshape(1), home_one, total[0], shapes)
+        (grad_w1,) = home_sums(home_first_kernel, spots, home_one, total[0], shapes)
         input_grad = first_norm(tokens, qkv_grad, pack, hidden_grad)
     if not members:
         peak = jnp.max(lax.all_gather(peak, DEVICE, axis=0, tiled=True), axis=0, keepdims=True)
-    limit = jnp.pad(clip_threshold.astype(f32).reshape(1, HEADS), ((0, 0), (0, LANES - HEADS)), constant_values=1.0)
+    limit = clip_threshold.reshape(1, HEADS)
     grad_qkv, grad_out, grad_router, clipped, *grads = finish(
-        low.reshape(1), total, own, limit, peak, width, experts, head_rows, members
+        spots, total, own, limit, peak, width, experts, head_rows, members
     )
     grads = [v.reshape(part) for v in grads]
     return (

time: 334 us -> 329 us (0.985)
  waiting for transfers between devices: 52.7 us -> 42.8 us
  Pallas kernels: 213 us -> 220 us
  local copies, waits for them, and re-layouts: 6.64 us -> 0.67 us
  starting transfers between devices: 54 us -> 57.4 us
    ppermute x7, starting transfers between devices: 4.17 us -> 16.9 us  [swap(): return lax.ppermute(value, axis, [(0, 1), (1, 0)])]
    ppermute x1, starting transfers between devices: 9.64 us -> 1.67 us  [shards(): straight = lax.ppermute(pay, ('hi', 'core'), STRAIGHT)]
    ppermute x2, waiting for transfers between devices: 11.3 us -> 3.6 us  [homeward(): lax.ppermute(crossed, ('hi', 'core'), BACK_CROSSED)]
    pallas_call x1 -> x2, Pallas kernels: 11.4 us -> 16.3 us  [dispatch(): pl.pallas_call(functools.partial(dispatch_kernel, cap=cap, shifts=tuple(s...]
    unnamed x36 -> x0, local copies, waits for them, and re-layouts: 4.13 us -> none
  transfers between devices with their start and end apart: 40 -> 40, of which waited for: 15 -> 16; matrix products, arithmetic and copies ran while one was open for 1% -> 1% of each run, Pallas kernels for 61% -> 64%
where the time goes in v4:
time: 329 us; the launch traced here: 324 us
  Pallas kernels  220 us (67%)
  starting transfers between devices  57.4 us (17%)
  waiting for transfers between devices  42.8 us (13%)
    pallas_call x3, Pallas kernels, expert_call(): pl.pallas_call(functools.partial(expert_kernel, cap=cap, group=group, fir...  87.5 us
    pallas_call x1, Pallas kernels, backward(): pl.pallas_call(functools.partial(backward_kernel, head_rows=head_rows, me...  22.6 us
    ppermute x17, waiting for transfers between devices, exchange(): return lax.ppermute(value, GROUP, [(k, k ^ shift) for k in range(experts)])  21.3 us
    pallas_call x2, Pallas kernels, forward(): pl.pallas_call(functools.partial(forward_kernel, experts=experts, fsdp=le...  19.1 us
    ppermute x7, starting transfers between devices, swap(): return lax.ppermute(value, axis, [(0, 1), (1, 0)])  16.9 us
    pallas_call x2, Pallas kernels, dispatch(): pl.pallas_call(functools.partial(dispatch_kernel, cap=cap, shifts=tuple(s...  16.3 us
    ppermute x17, starting transfers between devices, exchange(): return lax.ppermute(value, GROUP, [(k, k ^ shift) for k in range(experts)])  16.3 us
    pallas_call x1, Pallas kernels, middle(): pl.pallas_call(functools.partial(middle_kernel, cap=cap, experts=experts)...  12.6 us
  transfers between devices with their start and end apart: 40, of which 16 were waited for; matrix products, arithmetic and copies ran while one was open for 1% of the time, Pallas kernels for 64%

profile of v4, /device:TPU:0, one launch (start us, length us, event | category | flops | bytes accessed | tf_op | source)
XLA Modules:
  0.0 323.8 jit_solution(15535181028573403916)
XLA Ops:
  1.4 2.8 pack.1
  4.2 3.0 collective-permute-start
  8.8 3.0 collective-permute-start.1
  11.8 11.2 %route.1 = (bf16[8,432,1280]{2,1,0:T(8,128)(2,1)}, f32[5,256,128]{2,1,0:T(8,128)}, bf16[432,512]{1,0:T(8,128)(2,1)}, bf16[432,512]{1,0:T(8,128)(2,1)}, bf16[432,...) custom-call(s32[16]{0:T(128)} %stack.71.place_ref.spot_ref.spots_ref, ...), custom_call_target="tpu_custom_call" | custom-call | flops 20000000 | tf_op jit(solution)/shard_map/route/pallas_call | solution.py:201
  23.1 2.5 collective-permute-start.5
  26.6 5.7 %attend.2 = (bf16[5,208,1536]{2,1,0:T(8,128)(2,1)}, bf16[5,208,512]{2,1,0:T(8,128)(2,1)}, f32[5,208,512]{2,1,0:T(8,128)}, f32[5,208,128]{2,1,0:T(8,128)}, bf16[5...) custom-call(s32[16]{0:T(128)} %stack.71.place_ref.spot_ref.spots_ref.hi, ...), custom_call_target="tpu_custom_call" | custom-call | flops 20000000 | tf_op jit(solution)/shard_map/attend/pallas_call | solution.py:367
  32.3 4.0 %collective-permute-start.4 = (bf16[1040,512]{1,0:T(8,128)(2,1)}, bf16[1040,512]{1,0:T(8,128)(2,1)}, u32[]{:S(2)}, u32[]{:S(2)}) collective-permute-start(bf16[1040,512]{1,0:T(8,128)(2,1)} %get-tuple-element.149), channel_id=1, source_target_pairs={{0,16},{1,0},{16,17},{17,1},{2,18},{3,2},{18,19},{19,3},{4,20},{5,... | collective-permute-start | bytes 3194888 | tf_op jit(solution)/shard_map/ppermute | solution.py:1216
  39.2 13.4 %attend.3 = (bf16[5,208,1536]{2,1,0:T(8,128)(2,1)}, bf16[5,208,512]{2,1,0:T(8,128)(2,1)}, f32[5,208,512]{2,1,0:T(8,128)}, f32[5,208,128]{2,1,0:T(8,128)}, bf16[5...) custom-call(s32[16]{0:T(128)} %stack.71.place_ref.spot_ref.spots_ref, ...), custom_call_target="tpu_custom_call", output_to_operand_aliasing={{0}: (4, {}), {1}: (5, {}), {2}: (6, {}), {3}: (7, {}), {4}... | custom-call | flops 80000000000 | tf_op jit(solution)/shard_map/attend/pallas_call | solution.py:367
  52.6 6.2 %dispatch.3 = (bf16[432,512]{1,0:T(8,128)(2,1)}, bf16[432,512]{1,0:T(8,128)(2,1)}, bf16[432,512]{1,0:T(8,128)(2,1)}) custom-call(s32[3]{0:T(128)} %constant.39.clone._, bf16[8,432,1280]{2,1,0:T(8,128)(2,1)} %get-tuple-element.152.hot_ref, bf16[1280,512]{1,0:T(8,128)(2,1)} %bitcast.39), custom_call_target="tpu_custom_call" | custom-call | flops 20000000 | tf_op jit(solution)/shard_map/dispatch/pallas_call | solution.py:238
  58.9 7.8 %collective-permute-done.7.refs_5_ = bf16[432,512]{1,0:T(8,128)(2,1)} collective-permute-done((bf16[432,512]{1,0:T(8,128)(2,1)}, bf16[432,512]{1,0:T(8,128)(2,1)}, u32[]{:S(2)}, u32[]{:S(2)}) %collective-permute-start.7) | collective-permute-done | bytes 442400 | tf_op jit(solution)/shard_map/ppermute | solution.py:1126
  70.7 10.1 %dispatch.2 = (bf16[864,512]{1,0:T(8,128)(2,1)}, bf16[864,512]{1,0:T(8,128)(2,1)}, bf16[864,512]{1,0:T(8,128)(2,1)}, bf16[864,512]{1,0:T(8,128)(2,1)}, bf16[864,512]{1,0:T(8,128)(2,1)}) custom-call(s32[5]{0:T(128)} %constant.40.clone._, bf16[8,432,1280]{2,1,0:T(8,128)(2,1)} %get-tuple-element.152.hot_ref, bf16[1280,512]{1,0:T(8,128)(2,1)} %bitcast.40, ...), custom_call_target="tpu_custom_call" | custom-call | flops 20000000 | tf_op jit(solution)/shard_map/dispatch/pallas_call | solution.py:238
  81.5 7.6 %collective-permute-done.10.refs_1_ = bf16[432,512]{1,0:T(8,128)(2,1)} collective-permute-done((bf16[432,512]{1,0:T(8,128)(2,1)}, bf16[432,512]{1,0:T(8,128)(2,1)}, u32[]{:S(2)}, u32[]{:S(2)}) %collective-permute-start.10) | collective-permute-done | bytes 442400 | tf_op jit(solution)/shard_map/ppermute | solution.py:1126
  92.5 31.1 %expert.3 = (bf16[448,512]{1,0:T(8,128)(2,1)}, bf16[448,512]{1,0:T(8,128)(2,1)}, bf16[448,512]{1,0:T(8,128)(2,1)}, bf16[8,432,512]{2,1,0:T(8,128)(2,1)}, f32[512,2048]{1,0:T(8,128)}, /*index=5*/f32[4,528,512]{2,1,0:T(8,128)}) custom-call(s32[16]{0:T(128)} %stack.71.place_ref.spot_ref.spots_ref.high_ref.fy_ref.slot_ref, ...), custom_call_target="tpu_custom_call" | custom-call | flops 96000000000 | tf_op jit(solution)/shard_map/expert/pallas_call | solution.py:533
  127.2 4.5 %collective-permute-done.15.refs_1_.refs_4_ = bf16[864,512]{1,0:T(8,128)(2,1)} collective-permute-done((bf16[864,512]{1,0:T(8,128)(2,1)}, bf16[864,512]{1,0:T(8,128)(2,1)}, u32[]{:S(2)}, u32[]{:S(2)}) %collective-permute-start.15) | collective-permute-done | bytes 884768 | tf_op jit(solution)/shard_map/ppermute | solution.py:1126
  132.2 31.5 %expert.4 = (bf16[448,512]{1,0:T(8,128)(2,1)}, bf16[448,512]{1,0:T(8,128)(2,1)}, bf16[448,512]{1,0:T(8,128)(2,1)}, bf16[8,432,512]{2,1,0:T(8,128)(2,1)}, f32[512,2048]{1,0:T(8,128)}, /*index=5*/f32[4,528,512]{2,1,0:T(8,128)}) custom-call(s32[16]{0:T(128)} %stack.71.place_ref.spot_ref.spots_ref.high_ref.fy_ref.slot_ref, ...), custom_call_target="tpu_custom_call", output_to_operand_aliasing={{3}: (12, {})} | custom-call | flops 96000000000 | tf_op jit(solution)/shard_map/expert/pallas_call | solution.py:533
  166.6 24.8 %expert.5 = (bf16[448,512]{1,0:T(8,128)(2,1)}, bf16[448,512]{1,0:T(8,128)(2,1)}, bf16[8,432,512]{2,1,0:T(8,128)(2,1)}, bf16[2,528,512]{2,1,0:T(8,128)(2,1)}, bf1...) custom-call(s32[16]{0:T(128)} %stack.71.place_ref.spot_ref.spots_ref, ...), custom_call_target="tpu_custom_call", output_to_operand_aliasing={{2}: (10, {})} | custom-call | flops 96000000000 | tf_op jit(solution)/shard_map/expert/pallas_call | solution.py:533
  191.4 4.5 %all-to-all-start = ((bf16[8,432,512]{2,1,0:T(8,128)(2,1)}), bf16[8,432,512]{2,1,0:T(8,128)(2,1)}, u32[]{:S(2)}, u32[]{:S(2)}) async-start(bf16[8,432,512]{2,1,0:T(8,128)(2,1)} %get-tuple-element.201), calls=%async_computation | async-start | bytes 7077888 | tf_op jit(solution)/shard_map/all_to_all | solution.py:1268
  198.0 9.0 %returned.1 = (f32[5,208,512]{2,1,0:T(8,128)}, f32[5,208,128]{2,1,0:T(8,128)}) custom-call(f32[5,256,128]{2,1,0:T(8,128)} %get-tuple-element.134.pos_ref, bf16[448,512]{1,0:T(8,128)(2,1)} %collective-permute-done.18.refs_13_.refs_0_, bf16[448,512]{1,0:T(8,128)(2,1)} %collective-permute-done.20.refs_1_, ...), custom_call_target="tpu_custom_call" | custom-call | flops 99999997952 | tf_op jit(solution)/shard_map/returned/pallas_call | solution.py:606
  207.1 12.6 %middle.1 = (f32[5,208,512]{2,1,0:T(8,128)}, bf16[5,208,512]{2,1,0:T(8,128)(2,1)}, f32[512,640]{1,0:T(8,128)}) custom-call(s32[16]{0:T(128)} %stack.71.place_ref.spot_ref.spots_ref.high_ref.fy_ref.slot_ref, bf16[5,197,512]{2,1,0:T(8,128)(2,1)} %up_ref.3, bf16[512,2176]{1,0:T(8,128)(2,1)} %get-tuple-element.139.rest_0_.refs_10_.refs_8_.wout_ref.misc_ref.wqkv_ref, ...), custom_call_target="tpu_custom_call" | custom-call | flops 20000000 | tf_op jit(solution)/shard_map/middle/pallas_call | solution.py:687
  219.7 3.0 collective-permute-done.25.got_ref
  222.7 2.7 half_sums.2
  228.4 22.6 %attend_back.1 = (bf16[5,208,1536]{2,1,0:T(8,128)(2,1)}, bf16[2,128,2304]{2,1,0:T(8,128)(2,1)}, bf16[2,128,2304]{2,1,0:T(8,128)(2,1)}) custom-call(s32[16]{0:T(128)} %stack.71.place_ref.spot_ref.spots_ref.high_ref.fy_ref.slot_ref, bf16[5,197,512]{2,1,0:T(8,128)(2,1)} %tok_ref.7, bf16[5,208,1536]{2,1,0:T(8,128)(2,1)} %get-tuple-element.202.qkv_ref, ...), custom_call_target="tpu_custom_call" | custom-call | flops 50000000 | tf_op jit(solution)/shard_map/attend_back/pallas_call | solution.py:809
  250.9 3.6 %collective-permute-start.24 = (bf16[2,128,2304]{2,1,0:T(8,128)(2,1)}, bf16[2,128,2304]{2,1,0:T(8,128)(2,1)}, u32[]{:S(2)}, u32[]{:S(2)}) collective-permute-start(bf16[2,128,2304]{2,1,0:T(8,128)(2,1)} %get-tuple-element.217), channel_id=1, source_target_pairs={{0,1},{1,0},{2,3},{3,2},{4,5},{5,4},{6,7},{7,6},{8,9},{9,8},{10,11... | collective-permute-start | bytes 3538952 | tf_op jit(solution)/shard_map/ppermute | solution.py:1107
  254.6 2.7 half_sums.3
  257.4 2.8 add_halves.1
  262.3 8.0 %first_norm.1.refs_0_ = f32[5,197,512]{2,1,0:T(8,128)} custom-call(bf16[5,197,512]{2,1,0:T(8,128)(2,1)} %tok_ref.7, bf16[5,208,1536]{2,1,0:T(8,128)(2,1)} %get-tuple-element.229.qkv_grad_ref, bf16[512,2176]{1,0:T(8,128)(2,1)} %get-tuple-element.139.rest_0_.refs_10_.refs_8_.wout_ref.misc_ref.wqkv_ref, ...), custom_call_target="tpu_custom_call" | custom-call | flops 20000000 | tf_op jit(solution)/shard_map/first_norm/pallas_call | solution.py:862
  270.3 8.5 %combine.1.refs_1_ = bf16[5,197,512]{2,1,0:T(8,128)(2,1)} custom-call(s32[16]{0:T(128)} %stack.71.place_ref.spot_ref.spots_ref.high_ref.fy_ref.slot_ref, f32[5,256,128]{2,1,0:T(8,128)} %get-tuple-element.134.pos_ref, f32[5,208,512]{2,1,0:T(8,128)} %get-tuple-element.151.hidden_ref, bf16[8,432,512]{2,1,0:T(8,128)(2,1)} %all-to-all-done.made_ref), custom_call_target="tpu_custom_call" | custom-call | flops 20000000 | tf_op jit(solution)/shard_map/combine/pallas_call | solution.py:897
  278.8 3.6 %collective-permute-done.31.refs_3_.two = bf16[512,512]{1,0:T(8,128)(2,1)} collective-permute-done((bf16[512,512]{1,0:T(8,128)(2,1)}, bf16[512,512]{1,0:T(8,128)(2,1)}, u32[]{:S(2)}, u32[]{:S(2)}) %collective-permute-start.31) | collective-permute-done | bytes 524320 | tf_op jit(solution)/shard_map/ppermute | solution.py:1282
  295.1 6.7 %collective-permute-start.35 = (bf16[32,2304]{1,0:T(8,128)(2,1)}, bf16[32,2304]{1,0:T(8,128)(2,1)}, u32[]{:S(2)}, u32[]{:S(2)}) collective-permute-start(bf16[32,2304]{1,0:T(8,128)(2,1)} %add_parts.2._.refs_0_), channel_id=1, source_target_pairs={{0,16},{16,0},{1,17},{17,1},{2,18},{18,2},{3,19},{19,3},{4,20},{20... | collective-permute-start | bytes 442376 | tf_op jit(solution)/shard_map/ppermute | solution.py:1107
  301.8 2.5 home_sums.2
  314.4 4.5 %collective-permute-done.38.refs_3_ = bf16[32,2304]{1,0:T(8,128)(2,1)} collective-permute-done((bf16[32,2304]{1,0:T(8,128)(2,1)}, bf16[32,2304]{1,0:T(8,128)(2,1)}, u32[]{:S(2)}, u32[]{:S(2)}) %collective-permute-start.38) | collective-permute-done | bytes 147488 | tf_op jit(solution)/shard_map/ppermute | solution.py:1311
  320.8 2.8 finish.1
  (73 shorter events, 53.4 us)
Async XLA Ops:
  4.2 18.8 %collective-permute-start = (bf16[128,2176]{1,0:T(8,128)(2,1)}, bf16[128,2176]{1,0:T(8,128)(2,1)}, u32[]{:S(2)}, u32[]{:S(2)}) collective-permute-start(bf16[128,2176]{1,0:T(8,128)(2,1)} %get-tuple-element.135.rest_0_.refs_4_), channel_id=1, source_target_pairs={{2,0},{0,2},{3,1},{1,3},{6,4},{4,6},{7,5},{5,7},{10,8},{8,10},{11,... | collective-permute-start | bytes 1671176 | tf_op jit(solution)/shard_map/ppermute | solution.py:1112
  7.1 25.2 %collective-permute-start.3 = (bf16[1040,512]{1,0:T(8,128)(2,1)}, bf16[1040,512]{1,0:T(8,128)(2,1)}, u32[]{:S(2)}, u32[]{:S(2)}) collective-permute-start(bf16[1040,512]{1,0:T(8,128)(2,1)} %get-tuple-element.149), channel_id=1, source_target_pairs={{1,16},{16,1},{3,18},{18,3},{5,20},{20,5},{7,22},{22,7},{9,24},{24... | collective-permute-start | bytes 3194888 | tf_op jit(solution)/shard_map/ppermute | solution.py:1203
  8.8 17.4 %collective-permute-start.1 = (bf16[128,2176]{1,0:T(8,128)(2,1)}, bf16[128,2176]{1,0:T(8,128)(2,1)}, u32[]{:S(2)}, u32[]{:S(2)}) collective-permute-start(bf16[128,2176]{1,0:T(8,128)(2,1)} %get-tuple-element.135.rest_0_.refs_4_), channel_id=1, source_target_pairs={{0,1},{1,0},{2,3},{3,2},{4,5},{5,4},{6,7},{7,6},{8,9},{9,8},{10,11... | collective-permute-start | bytes 1671176 | tf_op jit(solution)/shard_map/ppermute | solution.py:1107
  23.1 35.8 %collective-permute-start.5 = (bf16[432,512]{1,0:T(8,128)(2,1)}, bf16[432,512]{1,0:T(8,128)(2,1)}, u32[]{:S(2)}, u32[]{:S(2)}) collective-permute-start(bf16[432,512]{1,0:T(8,128)(2,1)} %get-tuple-element.167), channel_id=1, source_target_pairs={{0,12},{1,13},{4,8},{5,9},{8,4},{9,5},{12,0},{13,1},{2,14},{3,15},... | collective-permute-start | bytes 1327112 | tf_op jit(solution)/shard_map/ppermute | solution.py:1126
  25.6 33.3 %collective-permute-start.6 = (bf16[432,512]{1,0:T(8,128)(2,1)}, bf16[432,512]{1,0:T(8,128)(2,1)}, u32[]{:S(2)}, u32[]{:S(2)}) collective-permute-start(bf16[432,512]{1,0:T(8,128)(2,1)} %get-tuple-element.168), channel_id=1, source_target_pairs={{0,4},{1,5},{4,0},{5,1},{8,12},{9,13},{12,8},{13,9},{2,6},{3,7},{6... | collective-permute-start | bytes 1327112 | tf_op jit(solution)/shard_map/ppermute | solution.py:1126
  26.2 40.5 %collective-permute-start.7 = (bf16[432,512]{1,0:T(8,128)(2,1)}, bf16[432,512]{1,0:T(8,128)(2,1)}, u32[]{:S(2)}, u32[]{:S(2)}) collective-permute-start(bf16[432,512]{1,0:T(8,128)(2,1)} %get-tuple-element.169), channel_id=1, source_target_pairs={{0,8},{1,9},{4,12},{5,13},{8,0},{9,1},{12,4},{13,5},{2,10},{3,11},... | collective-permute-start | bytes 1327112 | tf_op jit(solution)/shard_map/ppermute | solution.py:1126
  32.3 34.4 %collective-permute-start.4 = (bf16[1040,512]{1,0:T(8,128)(2,1)}, bf16[1040,512]{1,0:T(8,128)(2,1)}, u32[]{:S(2)}, u32[]{:S(2)}) collective-permute-start(bf16[1040,512]{1,0:T(8,128)(2,1)} %get-tuple-element.149), channel_id=1, source_target_pairs={{0,16},{1,0},{16,17},{17,1},{2,18},{3,2},{18,19},{19,3},{4,20},{5,... | collective-permute-start | bytes 3194888 | tf_op jit(solution)/shard_map/ppermute | solution.py:1216
  38.7 28.0 %collective-permute-start.8 = (bf16[1040,512]{1,0:T(8,128)(2,1)}, bf16[1040,512]{1,0:T(8,128)(2,1)}, u32[]{:S(2)}, u32[]{:S(2)}) collective-permute-start(bf16[1040,512]{1,0:T(8,128)(2,1)} %broadcast_select_fusion.rest_8_.refs_6_.refs_4_), channel_id=1, source_target_pairs={{2,0},{0,2},{3,1},{1,3},{6,4},{4,6},{7,5},{5,7},{10,8},{8,10},{11,... | collective-permute-start | bytes 3194888 | tf_op jit(solution)/shard_map/ppermute | solution.py:1112
  66.7 25.8 %collective-permute-start.12 = (bf16[1040,512]{1,0:T(8,128)(2,1)}, bf16[1040,512]{1,0:T(8,128)(2,1)}, u32[]{:S(2)}, u32[]{:S(2)}) collective-permute-start(bf16[1040,512]{1,0:T(8,128)(2,1)} %collective-permute-done.4.refs_8_.refs_6_), channel_id=1, source_target_pairs={{2,0},{0,2},{3,1},{1,3},{6,4},{4,6},{7,5},{5,7},{10,8},{8,10},{11,... | collective-permute-start | bytes 3194888 | tf_op jit(solution)/shard_map/ppermute | solution.py:1112
  67.2 14.3 %collective-permute-start.9 = (bf16[432,512]{1,0:T(8,128)(2,1)}, bf16[432,512]{1,0:T(8,128)(2,1)}, u32[]{:S(2)}, u32[]{:S(2)}) collective-permute-start(bf16[432,512]{1,0:T(8,128)(2,1)} %get-tuple-element.173), channel_id=1, source_target_pairs={{0,12},{1,13},{4,8},{5,9},{8,4},{9,5},{12,0},{13,1},{2,14},{3,15},... | collective-permute-start | bytes 1327112 | tf_op jit(solution)/shard_map/ppermute | solution.py:1126
  67.7 21.4 %collective-permute-start.10 = (bf16[432,512]{1,0:T(8,128)(2,1)}, bf16[432,512]{1,0:T(8,128)(2,1)}, u32[]{:S(2)}, u32[]{:S(2)}) collective-permute-start(bf16[432,512]{1,0:T(8,128)(2,1)} %get-tuple-element.174), channel_id=1, source_target_pairs={{0,4},{1,5},{4,0},{5,1},{8,12},{9,13},{12,8},{13,9},{2,6},{3,7},{6... | collective-permute-start | bytes 1327112 | tf_op jit(solution)/shard_map/ppermute | solution.py:1126
  68.7 21.1 %collective-permute-start.11 = (bf16[432,512]{1,0:T(8,128)(2,1)}, bf16[432,512]{1,0:T(8,128)(2,1)}, u32[]{:S(2)}, u32[]{:S(2)}) collective-permute-start(bf16[432,512]{1,0:T(8,128)(2,1)} %get-tuple-element.175), channel_id=1, source_target_pairs={{0,8},{1,9},{4,12},{5,13},{8,0},{9,1},{12,4},{13,5},{2,10},{3,11},... | collective-permute-start | bytes 1327112 | tf_op jit(solution)/shard_map/ppermute | solution.py:1126
  89.8 35.9 %collective-permute-start.14 = (bf16[864,512]{1,0:T(8,128)(2,1)}, bf16[864,512]{1,0:T(8,128)(2,1)}, u32[]{:S(2)}, u32[]{:S(2)}) collective-permute-start(bf16[864,512]{1,0:T(8,128)(2,1)} %get-tuple-element.189), channel_id=1, source_target_pairs={{0,13},{1,12},{4,9},{5,8},{8,5},{9,4},{12,1},{13,0},{2,15},{3,14},... | collective-permute-start | bytes 2654216 | tf_op jit(solution)/shard_map/ppermute | solution.py:1126
  89.9 41.8 %collective-permute-start.15 = (bf16[864,512]{1,0:T(8,128)(2,1)}, bf16[864,512]{1,0:T(8,128)(2,1)}, u32[]{:S(2)}, u32[]{:S(2)}) collective-permute-start(bf16[864,512]{1,0:T(8,128)(2,1)} %get-tuple-element.190), channel_id=1, source_target_pairs={{0,5},{1,4},{4,1},{5,0},{8,13},{9,12},{12,9},{13,8},{2,7},{3,6},{6... | collective-permute-start | bytes 2654216 | tf_op jit(solution)/shard_map/ppermute | solution.py:1126
  91.3 40.9 %collective-permute-start.16 = (bf16[864,512]{1,0:T(8,128)(2,1)}, bf16[864,512]{1,0:T(8,128)(2,1)}, u32[]{:S(2)}, u32[]{:S(2)}) collective-permute-start(bf16[864,512]{1,0:T(8,128)(2,1)} %get-tuple-element.191), channel_id=1, source_target_pairs={{0,9},{1,8},{4,13},{5,12},{8,1},{9,0},{12,5},{13,4},{2,11},{3,10},... | collective-permute-start | bytes 2654216 | tf_op jit(solution)/shard_map/ppermute | solution.py:1126
  123.6 40.4 %collective-permute-start.17 = (bf16[448,512]{1,0:T(8,128)(2,1)}, bf16[448,512]{1,0:T(8,128)(2,1)}, u32[]{:S(2)}, u32[]{:S(2)}) collective-permute-start(bf16[448,512]{1,0:T(8,128)(2,1)} %get-tuple-element.198), channel_id=1, source_target_pairs={{0,12},{1,13},{4,8},{5,9},{8,4},{9,5},{12,0},{13,1},{2,14},{3,15},... | collective-permute-start | bytes 1376264 | tf_op jit(solution)/shard_map/ppermute | solution.py:1126
  124.3 40.4 %collective-permute-start.18 = (bf16[448,512]{1,0:T(8,128)(2,1)}, bf16[448,512]{1,0:T(8,128)(2,1)}, u32[]{:S(2)}, u32[]{:S(2)}) collective-permute-start(bf16[448,512]{1,0:T(8,128)(2,1)} %get-tuple-element.199), channel_id=1, source_target_pairs={{0,4},{1,5},{4,0},{5,1},{8,12},{9,13},{12,8},{13,9},{2,6},{3,7},{6... | collective-permute-start | bytes 1376264 | tf_op jit(solution)/shard_map/ppermute | solution.py:1126
  125.7 40.9 %collective-permute-start.19 = (bf16[448,512]{1,0:T(8,128)(2,1)}, bf16[448,512]{1,0:T(8,128)(2,1)}, u32[]{:S(2)}, u32[]{:S(2)}) collective-permute-start(bf16[448,512]{1,0:T(8,128)(2,1)} %get-tuple-element.200), channel_id=1, source_target_pairs={{0,8},{1,9},{4,12},{5,13},{8,0},{9,1},{12,4},{13,5},{2,10},{3,11},... | collective-permute-start | bytes 1376264 | tf_op jit(solution)/shard_map/ppermute | solution.py:1126
  131.7 35.0 %collective-permute-start.13 = (bf16[864,512]{1,0:T(8,128)(2,1)}, bf16[864,512]{1,0:T(8,128)(2,1)}, u32[]{:S(2)}, u32[]{:S(2)}) collective-permute-start(bf16[864,512]{1,0:T(8,128)(2,1)} %get-tuple-element.188), channel_id=1, source_target_pairs={{0,1},{1,0},{4,5},{5,4},{8,9},{9,8},{12,13},{13,12},{2,3},{3,2},{6... | collective-permute-start | bytes 2654216 | tf_op jit(solution)/shard_map/ppermute | solution.py:1126
  163.7 34.3 %collective-permute-start.20 = (bf16[448,512]{1,0:T(8,128)(2,1)}, bf16[448,512]{1,0:T(8,128)(2,1)}, u32[]{:S(2)}, u32[]{:S(2)}) collective-permute-start(bf16[448,512]{1,0:T(8,128)(2,1)} %get-tuple-element.206), channel_id=1, source_target_pairs={{0,5},{1,4},{4,1},{5,0},{8,13},{9,12},{12,9},{13,8},{2,7},{3,6},{6... | collective-permute-start | bytes 1376264 | tf_op jit(solution)/shard_map/ppermute | solution.py:1126
  164.1 34.0 %collective-permute-start.21 = (bf16[448,512]{1,0:T(8,128)(2,1)}, bf16[448,512]{1,0:T(8,128)(2,1)}, u32[]{:S(2)}, u32[]{:S(2)}) collective-permute-start(bf16[448,512]{1,0:T(8,128)(2,1)} %get-tuple-element.207), channel_id=1, source_target_pairs={{0,9},{1,8},{4,13},{5,12},{8,1},{9,0},{12,5},{13,4},{2,11},{3,10},... | collective-permute-start | bytes 1376264 | tf_op jit(solution)/shard_map/ppermute | solution.py:1126
  164.7 33.4 %collective-permute-start.22 = (bf16[448,512]{1,0:T(8,128)(2,1)}, bf16[448,512]{1,0:T(8,128)(2,1)}, u32[]{:S(2)}, u32[]{:S(2)}) collective-permute-start(bf16[448,512]{1,0:T(8,128)(2,1)} %get-tuple-element.208), channel_id=1, source_target_pairs={{0,13},{1,12},{4,9},{5,8},{8,5},{9,4},{12,1},{13,0},{2,15},{3,14},... | collective-permute-start | bytes 1376264 | tf_op jit(solution)/shard_map/ppermute | solution.py:1126
  191.4 78.8 %all-to-all-start = ((bf16[8,432,512]{2,1,0:T(8,128)(2,1)}), bf16[8,432,512]{2,1,0:T(8,128)(2,1)}, u32[]{:S(2)}, u32[]{:S(2)}) async-start(bf16[8,432,512]{2,1,0:T(8,128)(2,1)} %get-tuple-element.201), calls=%async_computation | async-start | bytes 7077888 | tf_op jit(solution)/shard_map/all_to_all | solution.py:1268
  195.9 11.1 %collective-permute-start.23 = (bf16[448,512]{1,0:T(8,128)(2,1)}, bf16[448,512]{1,0:T(8,128)(2,1)}, u32[]{:S(2)}, u32[]{:S(2)}) collective-permute-start(bf16[448,512]{1,0:T(8,128)(2,1)} %get-tuple-element.212), channel_id=1, source_target_pairs={{0,1},{1,0},{4,5},{5,4},{8,9},{9,8},{12,13},{13,12},{2,3},{3,2},{6... | collective-permute-start | bytes 1376264 | tf_op jit(solution)/shard_map/ppermute | solution.py:1126
  196.5 26.2 %collective-permute-start.25 = (bf16[2,528,512]{2,1,0:T(8,128)(2,1)}, bf16[2,528,512]{2,1,0:T(8,128)(2,1)}, u32[]{:S(2)}, u32[]{:S(2)}) collective-permute-start(bf16[2,528,512]{2,1,0:T(8,128)(2,1)} %get-tuple-element.221), channel_id=1, source_target_pairs={{0,2},{2,0},{1,3},{3,1},{4,6},{6,4},{5,7},{7,5},{8,10},{10,8},{9,1... | collective-permute-start | bytes 3244040 | tf_op jit(solution)/shard_map/ppermute | solution.py:1107
  225.4 29.1 %collective-permute-start.26 = (bf16[2,512,512]{2,1,0:T(8,128)(2,1)}, bf16[2,512,512]{2,1,0:T(8,128)(2,1)}, u32[]{:S(2)}, u32[]{:S(2)}) collective-permute-start(bf16[2,512,512]{2,1,0:T(8,128)(2,1)} %get-tuple-element.223), channel_id=1, source_target_pairs={{0,2},{2,0},{1,3},{3,1},{4,6},{6,4},{5,7},{7,5},{8,10},{10,8},{9,1... | collective-permute-start | bytes 3145736 | tf_op jit(solution)/shard_map/ppermute | solution.py:1107
  226.9 27.6 %collective-permute-start.28 = (bf16[528,512]{1,0:T(8,128)(2,1)}, bf16[528,512]{1,0:T(8,128)(2,1)}, u32[]{:S(2)}, u32[]{:S(2)}) collective-permute-start(bf16[528,512]{1,0:T(8,128)(2,1)} %get-tuple-element.224), channel_id=1, source_target_pairs={{16,0},{0,1},{17,16},{1,17},{18,2},{2,3},{19,18},{3,19},{20,4},{4,... | collective-permute-start | bytes 1622024 | tf_op jit(solution)/shard_map/ppermute | solution.py:1282
  226.9 27.6 %collective-permute-start.27 = (bf16[528,512]{1,0:T(8,128)(2,1)}, bf16[528,512]{1,0:T(8,128)(2,1)}, u32[]{:S(2)}, u32[]{:S(2)}) collective-permute-start(bf16[528,512]{1,0:T(8,128)(2,1)} %get-tuple-element.222.own), channel_id=1, source_target_pairs={{16,1},{1,16},{18,3},{3,18},{20,5},{5,20},{22,7},{7,22},{24,9},{9,... | collective-permute-start | bytes 1622024 | tf_op jit(solution)/shard_map/ppermute | solution.py:1281
  260.2 22.2 %collective-permute-start.29 = (bf16[128,2304]{1,0:T(8,128)(2,1)}, bf16[128,2304]{1,0:T(8,128)(2,1)}, u32[]{:S(2)}, u32[]{:S(2)}) collective-permute-start(bf16[128,2304]{1,0:T(8,128)(2,1)} %get-tuple-element.232), channel_id=1, source_target_pairs={{0,2},{2,0},{1,3},{3,1},{4,6},{6,4},{5,7},{7,5},{8,10},{10,8},{9,1... | collective-permute-start | bytes 1769480 | tf_op jit(solution)/shard_map/ppermute | solution.py:1107
  260.7 21.6 %collective-permute-start.31 = (bf16[512,512]{1,0:T(8,128)(2,1)}, bf16[512,512]{1,0:T(8,128)(2,1)}, u32[]{:S(2)}, u32[]{:S(2)}) collective-permute-start(bf16[512,512]{1,0:T(8,128)(2,1)} %get-tuple-element.226.rest_1_), channel_id=1, source_target_pairs={{16,0},{0,1},{17,16},{1,17},{18,2},{2,3},{19,18},{3,19},{20,4},{4,... | collective-permute-start | bytes 1572872 | tf_op jit(solution)/shard_map/ppermute | solution.py:1282
  260.8 21.6 %collective-permute-start.30 = (bf16[512,512]{1,0:T(8,128)(2,1)}, bf16[512,512]{1,0:T(8,128)(2,1)}, u32[]{:S(2)}, u32[]{:S(2)}) collective-permute-start(bf16[512,512]{1,0:T(8,128)(2,1)} %get-tuple-element.225.rest_0_.own), channel_id=1, source_target_pairs={{16,1},{1,16},{18,3},{3,18},{20,5},{5,20},{22,7},{7,22},{24,9},{9,... | collective-permute-start | bytes 1572872 | tf_op jit(solution)/shard_map/ppermute | solution.py:1281
  295.1 14.1 %collective-permute-start.35 = (bf16[32,2304]{1,0:T(8,128)(2,1)}, bf16[32,2304]{1,0:T(8,128)(2,1)}, u32[]{:S(2)}, u32[]{:S(2)}) collective-permute-start(bf16[32,2304]{1,0:T(8,128)(2,1)} %add_parts.2._.refs_0_), channel_id=1, source_target_pairs={{0,16},{16,0},{1,17},{17,1},{2,18},{18,2},{3,19},{19,3},{4,20},{20... | collective-permute-start | bytes 442376 | tf_op jit(solution)/shard_map/ppermute | solution.py:1107
  (8 other events, 53.2 us)

commit v5 on v4

--- a/solution.py
+++ b/solution.py
@@ -917,7 +917,8 @@
     part = own_ref.shape[0]
     for shift, ref in enumerate(parts):
         size = part // number
-        total_ref[pl.ds(pl.multiple_of((slot_ref[LOW] ^ shift) * size, size), size), :] = ref[...]
+        at = (slot_ref[LOW] ^ shift) * size if number > 1 else 0
+        total_ref[pl.ds(pl.multiple_of(at, size), size), :] = ref[...]
     width = out_ref.shape[1]
     wide = 3 * width
     number = wide // LANES

time: 329 us -> 329 us (level)
  no operation moved by 1% of the time
where the time goes in v5:
time: 329 us; the launch traced here: 324 us
  Pallas kernels  220 us (67%)
  starting transfers between devices  57.4 us (17%)
  waiting for transfers between devices  42.8 us (13%)
    pallas_call x3, Pallas kernels, expert_call(): pl.pallas_call(functools.partial(expert_kernel, cap=cap, group=group, fir...  87.5 us
    pallas_call x1, Pallas kernels, backward(): pl.pallas_call(functools.partial(backward_kernel, head_rows=head_rows, me...  22.6 us
    ppermute x17, waiting for transfers between devices, exchange(): return lax.ppermute(value, GROUP, [(k, k ^ shift) for k in range(experts)])  21.3 us
    pallas_call x2, Pallas kernels, forward(): pl.pallas_call(functools.partial(forward_kernel, experts=experts, fsdp=le...  19.1 us
    ppermute x7, starting transfers between devices, swap(): return lax.ppermute(value, axis, [(0, 1), (1, 0)])  16.9 us
    pallas_call x2, Pallas kernels, dispatch(): pl.pallas_call(functools.partial(dispatch_kernel, cap=cap, shifts=tuple(s...  16.3 us
    ppermute x17, starting transfers between devices, exchange(): return lax.ppermute(value, GROUP, [(k, k ^ shift) for k in range(experts)])  16.3 us
    pallas_call x1, Pallas kernels, middle(): pl.pallas_call(functools.partial(middle_kernel, cap=cap, experts=experts)...  12.6 us
  transfers between devices with their start and end apart: 40, of which 16 were waited for; matrix products, arithmetic and copies ran while one was open for 1% of the time, Pallas kernels for 64%

profile of v5, /device:TPU:0, one launch (start us, length us, event | category | flops | bytes accessed | tf_op | source)
XLA Modules:
  0.0 323.8 jit_solution(7628426451725271212)
XLA Ops:
  1.4 2.8 pack.1
  4.2 3.0 collective-permute-start
  8.8 3.0 collective-permute-start.1
  11.8 11.2 %route.1 = (bf16[8,432,1280]{2,1,0:T(8,128)(2,1)}, f32[5,256,128]{2,1,0:T(8,128)}, bf16[432,512]{1,0:T(8,128)(2,1)}, bf16[432,512]{1,0:T(8,128)(2,1)}, bf16[432,...) custom-call(s32[16]{0:T(128)} %stack.71.place_ref.spot_ref.spots_ref, ...), custom_call_target="tpu_custom_call" | custom-call | flops 20000000 | tf_op jit(solution)/shard_map/route/pallas_call | solution.py:201
  23.1 2.5 collective-permute-start.5
  26.6 5.7 %attend.2 = (bf16[5,208,1536]{2,1,0:T(8,128)(2,1)}, bf16[5,208,512]{2,1,0:T(8,128)(2,1)}, f32[5,208,512]{2,1,0:T(8,128)}, f32[5,208,128]{2,1,0:T(8,128)}, bf16[5...) custom-call(s32[16]{0:T(128)} %stack.71.place_ref.spot_ref.spots_ref.hi, ...), custom_call_target="tpu_custom_call" | custom-call | flops 20000000 | tf_op jit(solution)/shard_map/attend/pallas_call | solution.py:367
  32.3 4.0 %collective-permute-start.4 = (bf16[1040,512]{1,0:T(8,128)(2,1)}, bf16[1040,512]{1,0:T(8,128)(2,1)}, u32[]{:S(2)}, u32[]{:S(2)}) collective-permute-start(bf16[1040,512]{1,0:T(8,128)(2,1)} %get-tuple-element.149), channel_id=1, source_target_pairs={{0,16},{1,0},{16,17},{17,1},{2,18},{3,2},{18,19},{19,3},{4,20},{5,... | collective-permute-start | bytes 3194888 | tf_op jit(solution)/shard_map/ppermute | solution.py:1217
  39.2 13.4 %attend.3 = (bf16[5,208,1536]{2,1,0:T(8,128)(2,1)}, bf16[5,208,512]{2,1,0:T(8,128)(2,1)}, f32[5,208,512]{2,1,0:T(8,128)}, f32[5,208,128]{2,1,0:T(8,128)}, bf16[5...) custom-call(s32[16]{0:T(128)} %stack.71.place_ref.spot_ref.spots_ref, ...), custom_call_target="tpu_custom_call", output_to_operand_aliasing={{0}: (4, {}), {1}: (5, {}), {2}: (6, {}), {3}: (7, {}), {4}... | custom-call | flops 80000000000 | tf_op jit(solution)/shard_map/attend/pallas_call | solution.py:367
  52.6 6.2 %dispatch.3 = (bf16[432,512]{1,0:T(8,128)(2,1)}, bf16[432,512]{1,0:T(8,128)(2,1)}, bf16[432,512]{1,0:T(8,128)(2,1)}) custom-call(s32[3]{0:T(128)} %constant.39.clone._, bf16[8,432,1280]{2,1,0:T(8,128)(2,1)} %get-tuple-element.152.hot_ref, bf16[1280,512]{1,0:T(8,128)(2,1)} %bitcast.39), custom_call_target="tpu_custom_call" | custom-call | flops 20000000 | tf_op jit(solution)/shard_map/dispatch/pallas_call | solution.py:238
  58.9 7.8 %collective-permute-done.7.refs_5_ = bf16[432,512]{1,0:T(8,128)(2,1)} collective-permute-done((bf16[432,512]{1,0:T(8,128)(2,1)}, bf16[432,512]{1,0:T(8,128)(2,1)}, u32[]{:S(2)}, u32[]{:S(2)}) %collective-permute-start.7) | collective-permute-done | bytes 442400 | tf_op jit(solution)/shard_map/ppermute | solution.py:1127
  70.7 10.1 %dispatch.2 = (bf16[864,512]{1,0:T(8,128)(2,1)}, bf16[864,512]{1,0:T(8,128)(2,1)}, bf16[864,512]{1,0:T(8,128)(2,1)}, bf16[864,512]{1,0:T(8,128)(2,1)}, bf16[864,512]{1,0:T(8,128)(2,1)}) custom-call(s32[5]{0:T(128)} %constant.40.clone._, bf16[8,432,1280]{2,1,0:T(8,128)(2,1)} %get-tuple-element.152.hot_ref, bf16[1280,512]{1,0:T(8,128)(2,1)} %bitcast.40, ...), custom_call_target="tpu_custom_call" | custom-call | flops 20000000 | tf_op jit(solution)/shard_map/dispatch/pallas_call | solution.py:238
  81.5 7.6 %collective-permute-done.10.refs_1_ = bf16[432,512]{1,0:T(8,128)(2,1)} collective-permute-done((bf16[432,512]{1,0:T(8,128)(2,1)}, bf16[432,512]{1,0:T(8,128)(2,1)}, u32[]{:S(2)}, u32[]{:S(2)}) %collective-permute-start.10) | collective-permute-done | bytes 442400 | tf_op jit(solution)/shard_map/ppermute | solution.py:1127
  92.5 31.1 %expert.3 = (bf16[448,512]{1,0:T(8,128)(2,1)}, bf16[448,512]{1,0:T(8,128)(2,1)}, bf16[448,512]{1,0:T(8,128)(2,1)}, bf16[8,432,512]{2,1,0:T(8,128)(2,1)}, f32[512,2048]{1,0:T(8,128)}, /*index=5*/f32[4,528,512]{2,1,0:T(8,128)}) custom-call(s32[16]{0:T(128)} %stack.71.place_ref.spot_ref.spots_ref.high_ref.fy_ref.slot_ref, ...), custom_call_target="tpu_custom_call" | custom-call | flops 96000000000 | tf_op jit(solution)/shard_map/expert/pallas_call | solution.py:533
  127.2 4.5 %collective-permute-done.15.refs_1_.refs_4_ = bf16[864,512]{1,0:T(8,128)(2,1)} collective-permute-done((bf16[864,512]{1,0:T(8,128)(2,1)}, bf16[864,512]{1,0:T(8,128)(2,1)}, u32[]{:S(2)}, u32[]{:S(2)}) %collective-permute-start.15) | collective-permute-done | bytes 884768 | tf_op jit(solution)/shard_map/ppermute | solution.py:1127
  132.2 31.5 %expert.4 = (bf16[448,512]{1,0:T(8,128)(2,1)}, bf16[448,512]{1,0:T(8,128)(2,1)}, bf16[448,512]{1,0:T(8,128)(2,1)}, bf16[8,432,512]{2,1,0:T(8,128)(2,1)}, f32[512,2048]{1,0:T(8,128)}, /*index=5*/f32[4,528,512]{2,1,0:T(8,128)}) custom-call(s32[16]{0:T(128)} %stack.71.place_ref.spot_ref.spots_ref.high_ref.fy_ref.slot_ref, ...), custom_call_target="tpu_custom_call", output_to_operand_aliasing={{3}: (12, {})} | custom-call | flops 96000000000 | tf_op jit(solution)/shard_map/expert/pallas_call | solution.py:533
  166.6 24.8 %expert.5 = (bf16[448,512]{1,0:T(8,128)(2,1)}, bf16[448,512]{1,0:T(8,128)(2,1)}, bf16[8,432,512]{2,1,0:T(8,128)(2,1)}, bf16[2,528,512]{2,1,0:T(8,128)(2,1)}, bf1...) custom-call(s32[16]{0:T(128)} %stack.71.place_ref.spot_ref.spots_ref, ...), custom_call_target="tpu_custom_call", output_to_operand_aliasing={{2}: (10, {})} | custom-call | flops 96000000000 | tf_op jit(solution)/shard_map/expert/pallas_call | solution.py:533
  191.4 4.5 %all-to-all-start = ((bf16[8,432,512]{2,1,0:T(8,128)(2,1)}), bf16[8,432,512]{2,1,0:T(8,128)(2,1)}, u32[]{:S(2)}, u32[]{:S(2)}) async-start(bf16[8,432,512]{2,1,0:T(8,128)(2,1)} %get-tuple-element.201), calls=%async_computation | async-start | bytes 7077888 | tf_op jit(solution)/shard_map/all_to_all | solution.py:1269
  198.0 9.0 %returned.1 = (f32[5,208,512]{2,1,0:T(8,128)}, f32[5,208,128]{2,1,0:T(8,128)}) custom-call(f32[5,256,128]{2,1,0:T(8,128)} %get-tuple-element.134.pos_ref, bf16[448,512]{1,0:T(8,128)(2,1)} %collective-permute-done.18.refs_13_.refs_0_, bf16[448,512]{1,0:T(8,128)(2,1)} %collective-permute-done.20.refs_1_, ...), custom_call_target="tpu_custom_call" | custom-call | flops 99999997952 | tf_op jit(solution)/shard_map/returned/pallas_call | solution.py:606
  207.1 12.6 %middle.1 = (f32[5,208,512]{2,1,0:T(8,128)}, bf16[5,208,512]{2,1,0:T(8,128)(2,1)}, f32[512,640]{1,0:T(8,128)}) custom-call(s32[16]{0:T(128)} %stack.71.place_ref.spot_ref.spots_ref.high_ref.fy_ref.slot_ref, bf16[5,197,512]{2,1,0:T(8,128)(2,1)} %up_ref.3, bf16[512,2176]{1,0:T(8,128)(2,1)} %get-tuple-element.139.rest_0_.refs_10_.refs_8_.wout_ref.misc_ref.wqkv_ref, ...), custom_call_target="tpu_custom_call" | custom-call | flops 20000000 | tf_op jit(solution)/shard_map/middle/pallas_call | solution.py:687
  219.7 3.0 collective-permute-done.25.got_ref
  222.7 2.7 half_sums.2
  228.4 22.6 %attend_back.1 = (bf16[5,208,1536]{2,1,0:T(8,128)(2,1)}, bf16[2,128,2304]{2,1,0:T(8,128)(2,1)}, bf16[2,128,2304]{2,1,0:T(8,128)(2,1)}) custom-call(s32[16]{0:T(128)} %stack.71.place_ref.spot_ref.spots_ref.high_ref.fy_ref.slot_ref, bf16[5,197,512]{2,1,0:T(8,128)(2,1)} %tok_ref.7, bf16[5,208,1536]{2,1,0:T(8,128)(2,1)} %get-tuple-element.202.qkv_ref, ...), custom_call_target="tpu_custom_call" | custom-call | flops 50000000 | tf_op jit(solution)/shard_map/attend_back/pallas_call | solution.py:809
  250.9 3.6 %collective-permute-start.24 = (bf16[2,128,2304]{2,1,0:T(8,128)(2,1)}, bf16[2,128,2304]{2,1,0:T(8,128)(2,1)}, u32[]{:S(2)}, u32[]{:S(2)}) collective-permute-start(bf16[2,128,2304]{2,1,0:T(8,128)(2,1)} %get-tuple-element.217), channel_id=1, source_target_pairs={{0,1},{1,0},{2,3},{3,2},{4,5},{5,4},{6,7},{7,6},{8,9},{9,8},{10,11... | collective-permute-start | bytes 3538952 | tf_op jit(solution)/shard_map/ppermute | solution.py:1108
  254.6 2.7 half_sums.3
  257.4 2.8 add_halves.1
  262.3 8.0 %first_norm.1.refs_0_ = f32[5,197,512]{2,1,0:T(8,128)} custom-call(bf16[5,197,512]{2,1,0:T(8,128)(2,1)} %tok_ref.7, bf16[5,208,1536]{2,1,0:T(8,128)(2,1)} %get-tuple-element.229.qkv_grad_ref, bf16[512,2176]{1,0:T(8,128)(2,1)} %get-tuple-element.139.rest_0_.refs_10_.refs_8_.wout_ref.misc_ref.wqkv_ref, ...), custom_call_target="tpu_custom_call" | custom-call | flops 20000000 | tf_op jit(solution)/shard_map/first_norm/pallas_call | solution.py:862
  270.3 8.5 %combine.1.refs_1_ = bf16[5,197,512]{2,1,0:T(8,128)(2,1)} custom-call(s32[16]{0:T(128)} %stack.71.place_ref.spot_ref.spots_ref.high_ref.fy_ref.slot_ref, f32[5,256,128]{2,1,0:T(8,128)} %get-tuple-element.134.pos_ref, f32[5,208,512]{2,1,0:T(8,128)} %get-tuple-element.151.hidden_ref, bf16[8,432,512]{2,1,0:T(8,128)(2,1)} %all-to-all-done.made_ref), custom_call_target="tpu_custom_call" | custom-call | flops 20000000 | tf_op jit(solution)/shard_map/combine/pallas_call | solution.py:897
  278.8 3.6 %collective-permute-done.31.refs_3_.two = bf16[512,512]{1,0:T(8,128)(2,1)} collective-permute-done((bf16[512,512]{1,0:T(8,128)(2,1)}, bf16[512,512]{1,0:T(8,128)(2,1)}, u32[]{:S(2)}, u32[]{:S(2)}) %collective-permute-start.31) | collective-permute-done | bytes 524320 | tf_op jit(solution)/shard_map/ppermute | solution.py:1283
  295.1 6.7 %collective-permute-start.35 = (bf16[32,2304]{1,0:T(8,128)(2,1)}, bf16[32,2304]{1,0:T(8,128)(2,1)}, u32[]{:S(2)}, u32[]{:S(2)}) collective-permute-start(bf16[32,2304]{1,0:T(8,128)(2,1)} %add_parts.2._.refs_0_), channel_id=1, source_target_pairs={{0,16},{16,0},{1,17},{17,1},{2,18},{18,2},{3,19},{19,3},{4,20},{20... | collective-permute-start | bytes 442376 | tf_op jit(solution)/shard_map/ppermute | solution.py:1108
  301.8 2.5 home_sums.2
  314.4 4.5 %collective-permute-done.38.refs_3_ = bf16[32,2304]{1,0:T(8,128)(2,1)} collective-permute-done((bf16[32,2304]{1,0:T(8,128)(2,1)}, bf16[32,2304]{1,0:T(8,128)(2,1)}, u32[]{:S(2)}, u32[]{:S(2)}) %collective-permute-start.38) | collective-permute-done | bytes 147488 | tf_op jit(solution)/shard_map/ppermute | solution.py:1312
  320.8 2.8 finish.1
  (73 shorter events, 53.4 us)
Async XLA Ops:
  4.2 18.8 %collective-permute-start = (bf16[128,2176]{1,0:T(8,128)(2,1)}, bf16[128,2176]{1,0:T(8,128)(2,1)}, u32[]{:S(2)}, u32[]{:S(2)}) collective-permute-start(bf16[128,2176]{1,0:T(8,128)(2,1)} %get-tuple-element.135.rest_0_.refs_4_), channel_id=1, source_target_pairs={{2,0},{0,2},{3,1},{1,3},{6,4},{4,6},{7,5},{5,7},{10,8},{8,10},{11,... | collective-permute-start | bytes 1671176 | tf_op jit(solution)/shard_map/ppermute | solution.py:1113
  7.1 25.2 %collective-permute-start.3 = (bf16[1040,512]{1,0:T(8,128)(2,1)}, bf16[1040,512]{1,0:T(8,128)(2,1)}, u32[]{:S(2)}, u32[]{:S(2)}) collective-permute-start(bf16[1040,512]{1,0:T(8,128)(2,1)} %get-tuple-element.149), channel_id=1, source_target_pairs={{1,16},{16,1},{3,18},{18,3},{5,20},{20,5},{7,22},{22,7},{9,24},{24... | collective-permute-start | bytes 3194888 | tf_op jit(solution)/shard_map/ppermute | solution.py:1204
  8.8 17.4 %collective-permute-start.1 = (bf16[128,2176]{1,0:T(8,128)(2,1)}, bf16[128,2176]{1,0:T(8,128)(2,1)}, u32[]{:S(2)}, u32[]{:S(2)}) collective-permute-start(bf16[128,2176]{1,0:T(8,128)(2,1)} %get-tuple-element.135.rest_0_.refs_4_), channel_id=1, source_target_pairs={{0,1},{1,0},{2,3},{3,2},{4,5},{5,4},{6,7},{7,6},{8,9},{9,8},{10,11... | collective-permute-start | bytes 1671176 | tf_op jit(solution)/shard_map/ppermute | solution.py:1108
  23.1 35.8 %collective-permute-start.5 = (bf16[432,512]{1,0:T(8,128)(2,1)}, bf16[432,512]{1,0:T(8,128)(2,1)}, u32[]{:S(2)}, u32[]{:S(2)}) collective-permute-start(bf16[432,512]{1,0:T(8,128)(2,1)} %get-tuple-element.167), channel_id=1, source_target_pairs={{0,12},{1,13},{4,8},{5,9},{8,4},{9,5},{12,0},{13,1},{2,14},{3,15},... | collective-permute-start | bytes 1327112 | tf_op jit(solution)/shard_map/ppermute | solution.py:1127
  25.6 33.3 %collective-permute-start.6 = (bf16[432,512]{1,0:T(8,128)(2,1)}, bf16[432,512]{1,0:T(8,128)(2,1)}, u32[]{:S(2)}, u32[]{:S(2)}) collective-permute-start(bf16[432,512]{1,0:T(8,128)(2,1)} %get-tuple-element.168), channel_id=1, source_target_pairs={{0,4},{1,5},{4,0},{5,1},{8,12},{9,13},{12,8},{13,9},{2,6},{3,7},{6... | collective-permute-start | bytes 1327112 | tf_op jit(solution)/shard_map/ppermute | solution.py:1127
  26.2 40.5 %collective-permute-start.7 = (bf16[432,512]{1,0:T(8,128)(2,1)}, bf16[432,512]{1,0:T(8,128)(2,1)}, u32[]{:S(2)}, u32[]{:S(2)}) collective-permute-start(bf16[432,512]{1,0:T(8,128)(2,1)} %get-tuple-element.169), channel_id=1, source_target_pairs={{0,8},{1,9},{4,12},{5,13},{8,0},{9,1},{12,4},{13,5},{2,10},{3,11},... | collective-permute-start | bytes 1327112 | tf_op jit(solution)/shard_map/ppermute | solution.py:1127
  32.3 34.4 %collective-permute-start.4 = (bf16[1040,512]{1,0:T(8,128)(2,1)}, bf16[1040,512]{1,0:T(8,128)(2,1)}, u32[]{:S(2)}, u32[]{:S(2)}) collective-permute-start(bf16[1040,512]{1,0:T(8,128)(2,1)} %get-tuple-element.149), channel_id=1, source_target_pairs={{0,16},{1,0},{16,17},{17,1},{2,18},{3,2},{18,19},{19,3},{4,20},{5,... | collective-permute-start | bytes 3194888 | tf_op jit(solution)/shard_map/ppermute | solution.py:1217
  38.7 28.0 %collective-permute-start.8 = (bf16[1040,512]{1,0:T(8,128)(2,1)}, bf16[1040,512]{1,0:T(8,128)(2,1)}, u32[]{:S(2)}, u32[]{:S(2)}) collective-permute-start(bf16[1040,512]{1,0:T(8,128)(2,1)} %broadcast_select_fusion.rest_8_.refs_6_.refs_4_), channel_id=1, source_target_pairs={{2,0},{0,2},{3,1},{1,3},{6,4},{4,6},{7,5},{5,7},{10,8},{8,10},{11,... | collective-permute-start | bytes 3194888 | tf_op jit(solution)/shard_map/ppermute | solution.py:1113
  66.7 25.8 %collective-permute-start.12 = (bf16[1040,512]{1,0:T(8,128)(2,1)}, bf16[1040,512]{1,0:T(8,128)(2,1)}, u32[]{:S(2)}, u32[]{:S(2)}) collective-permute-start(bf16[1040,512]{1,0:T(8,128)(2,1)} %collective-permute-done.4.refs_8_.refs_6_), channel_id=1, source_target_pairs={{2,0},{0,2},{3,1},{1,3},{6,4},{4,6},{7,5},{5,7},{10,8},{8,10},{11,... | collective-permute-start | bytes 3194888 | tf_op jit(solution)/shard_map/ppermute | solution.py:1113
  67.2 14.3 %collective-permute-start.9 = (bf16[432,512]{1,0:T(8,128)(2,1)}, bf16[432,512]{1,0:T(8,128)(2,1)}, u32[]{:S(2)}, u32[]{:S(2)}) collective-permute-start(bf16[432,512]{1,0:T(8,128)(2,1)} %get-tuple-element.173), channel_id=1, source_target_pairs={{0,12},{1,13},{4,8},{5,9},{8,4},{9,5},{12,0},{13,1},{2,14},{3,15},... | collective-permute-start | bytes 1327112 | tf_op jit(solution)/shard_map/ppermute | solution.py:1127
  67.7 21.4 %collective-permute-start.10 = (bf16[432,512]{1,0:T(8,128)(2,1)}, bf16[432,512]{1,0:T(8,128)(2,1)}, u32[]{:S(2)}, u32[]{:S(2)}) collective-permute-start(bf16[432,512]{1,0:T(8,128)(2,1)} %get-tuple-element.174), channel_id=1, source_target_pairs={{0,4},{1,5},{4,0},{5,1},{8,12},{9,13},{12,8},{13,9},{2,6},{3,7},{6... | collective-permute-start | bytes 1327112 | tf_op jit(solution)/shard_map/ppermute | solution.py:1127
  68.7 21.1 %collective-permute-start.11 = (bf16[432,512]{1,0:T(8,128)(2,1)}, bf16[432,512]{1,0:T(8,128)(2,1)}, u32[]{:S(2)}, u32[]{:S(2)}) collective-permute-start(bf16[432,512]{1,0:T(8,128)(2,1)} %get-tuple-element.175), channel_id=1, source_target_pairs={{0,8},{1,9},{4,12},{5,13},{8,0},{9,1},{12,4},{13,5},{2,10},{3,11},... | collective-permute-start | bytes 1327112 | tf_op jit(solution)/shard_map/ppermute | solution.py:1127
  89.8 35.9 %collective-permute-start.14 = (bf16[864,512]{1,0:T(8,128)(2,1)}, bf16[864,512]{1,0:T(8,128)(2,1)}, u32[]{:S(2)}, u32[]{:S(2)}) collective-permute-start(bf16[864,512]{1,0:T(8,128)(2,1)} %get-tuple-element.189), channel_id=1, source_target_pairs={{0,13},{1,12},{4,9},{5,8},{8,5},{9,4},{12,1},{13,0},{2,15},{3,14},... | collective-permute-start | bytes 2654216 | tf_op jit(solution)/shard_map/ppermute | solution.py:1127
  89.9 41.8 %collective-permute-start.15 = (bf16[864,512]{1,0:T(8,128)(2,1)}, bf16[864,512]{1,0:T(8,128)(2,1)}, u32[]{:S(2)}, u32[]{:S(2)}) collective-permute-start(bf16[864,512]{1,0:T(8,128)(2,1)} %get-tuple-element.190), channel_id=1, source_target_pairs={{0,5},{1,4},{4,1},{5,0},{8,13},{9,12},{12,9},{13,8},{2,7},{3,6},{6... | collective-permute-start | bytes 2654216 | tf_op jit(solution)/shard_map/ppermute | solution.py:1127
  91.3 40.9 %collective-permute-start.16 = (bf16[864,512]{1,0:T(8,128)(2,1)}, bf16[864,512]{1,0:T(8,128)(2,1)}, u32[]{:S(2)}, u32[]{:S(2)}) collective-permute-start(bf16[864,512]{1,0:T(8,128)(2,1)} %get-tuple-element.191), channel_id=1, source_target_pairs={{0,9},{1,8},{4,13},{5,12},{8,1},{9,0},{12,5},{13,4},{2,11},{3,10},... | collective-permute-start | bytes 2654216 | tf_op jit(solution)/shard_map/ppermute | solution.py:1127
  123.6 40.4 %collective-permute-start.17 = (bf16[448,512]{1,0:T(8,128)(2,1)}, bf16[448,512]{1,0:T(8,128)(2,1)}, u32[]{:S(2)}, u32[]{:S(2)}) collective-permute-start(bf16[448,512]{1,0:T(8,128)(2,1)} %get-tuple-element.198), channel_id=1, source_target_pairs={{0,12},{1,13},{4,8},{5,9},{8,4},{9,5},{12,0},{13,1},{2,14},{3,15},... | collective-permute-start | bytes 1376264 | tf_op jit(solution)/shard_map/ppermute | solution.py:1127
  124.3 40.4 %collective-permute-start.18 = (bf16[448,512]{1,0:T(8,128)(2,1)}, bf16[448,512]{1,0:T(8,128)(2,1)}, u32[]{:S(2)}, u32[]{:S(2)}) collective-permute-start(bf16[448,512]{1,0:T(8,128)(2,1)} %get-tuple-element.199), channel_id=1, source_target_pairs={{0,4},{1,5},{4,0},{5,1},{8,12},{9,13},{12,8},{13,9},{2,6},{3,7},{6... | collective-permute-start | bytes 1376264 | tf_op jit(solution)/shard_map/ppermute | solution.py:1127
  125.7 40.9 %collective-permute-start.19 = (bf16[448,512]{1,0:T(8,128)(2,1)}, bf16[448,512]{1,0:T(8,128)(2,1)}, u32[]{:S(2)}, u32[]{:S(2)}) collective-permute-start(bf16[448,512]{1,0:T(8,128)(2,1)} %get-tuple-element.200), channel_id=1, source_target_pairs={{0,8},{1,9},{4,12},{5,13},{8,0},{9,1},{12,4},{13,5},{2,10},{3,11},... | collective-permute-start | bytes 1376264 | tf_op jit(solution)/shard_map/ppermute | solution.py:1127
  131.7 35.0 %collective-permute-start.13 = (bf16[864,512]{1,0:T(8,128)(2,1)}, bf16[864,512]{1,0:T(8,128)(2,1)}, u32[]{:S(2)}, u32[]{:S(2)}) collective-permute-start(bf16[864,512]{1,0:T(8,128)(2,1)} %get-tuple-element.188), channel_id=1, source_target_pairs={{0,1},{1,0},{4,5},{5,4},{8,9},{9,8},{12,13},{13,12},{2,3},{3,2},{6... | collective-permute-start | bytes 2654216 | tf_op jit(solution)/shard_map/ppermute | solution.py:1127
  163.7 34.3 %collective-permute-start.20 = (bf16[448,512]{1,0:T(8,128)(2,1)}, bf16[448,512]{1,0:T(8,128)(2,1)}, u32[]{:S(2)}, u32[]{:S(2)}) collective-permute-start(bf16[448,512]{1,0:T(8,128)(2,1)} %get-tuple-element.206), channel_id=1, source_target_pairs={{0,5},{1,4},{4,1},{5,0},{8,13},{9,12},{12,9},{13,8},{2,7},{3,6},{6... | collective-permute-start | bytes 1376264 | tf_op jit(solution)/shard_map/ppermute | solution.py:1127
  164.1 34.0 %collective-permute-start.21 = (bf16[448,512]{1,0:T(8,128)(2,1)}, bf16[448,512]{1,0:T(8,128)(2,1)}, u32[]{:S(2)}, u32[]{:S(2)}) collective-permute-start(bf16[448,512]{1,0:T(8,128)(2,1)} %get-tuple-element.207), channel_id=1, source_target_pairs={{0,9},{1,8},{4,13},{5,12},{8,1},{9,0},{12,5},{13,4},{2,11},{3,10},... | collective-permute-start | bytes 1376264 | tf_op jit(solution)/shard_map/ppermute | solution.py:1127
  164.7 33.4 %collective-permute-start.22 = (bf16[448,512]{1,0:T(8,128)(2,1)}, bf16[448,512]{1,0:T(8,128)(2,1)}, u32[]{:S(2)}, u32[]{:S(2)}) collective-permute-start(bf16[448,512]{1,0:T(8,128)(2,1)} %get-tuple-element.208), channel_id=1, source_target_pairs={{0,13},{1,12},{4,9},{5,8},{8,5},{9,4},{12,1},{13,0},{2,15},{3,14},... | collective-permute-start | bytes 1376264 | tf_op jit(solution)/shard_map/ppermute | solution.py:1127
  191.4 78.8 %all-to-all-start = ((bf16[8,432,512]{2,1,0:T(8,128)(2,1)}), bf16[8,432,512]{2,1,0:T(8,128)(2,1)}, u32[]{:S(2)}, u32[]{:S(2)}) async-start(bf16[8,432,512]{2,1,0:T(8,128)(2,1)} %get-tuple-element.201), calls=%async_computation | async-start | bytes 7077888 | tf_op jit(solution)/shard_map/all_to_all | solution.py:1269
  195.9 11.1 %collective-permute-start.23 = (bf16[448,512]{1,0:T(8,128)(2,1)}, bf16[448,512]{1,0:T(8,128)(2,1)}, u32[]{:S(2)}, u32[]{:S(2)}) collective-permute-start(bf16[448,512]{1,0:T(8,128)(2,1)} %get-tuple-element.212), channel_id=1, source_target_pairs={{0,1},{1,0},{4,5},{5,4},{8,9},{9,8},{12,13},{13,12},{2,3},{3,2},{6... | collective-permute-start | bytes 1376264 | tf_op jit(solution)/shard_map/ppermute | solution.py:1127
  196.5 26.2 %collective-permute-start.25 = (bf16[2,528,512]{2,1,0:T(8,128)(2,1)}, bf16[2,528,512]{2,1,0:T(8,128)(2,1)}, u32[]{:S(2)}, u32[]{:S(2)}) collective-permute-start(bf16[2,528,512]{2,1,0:T(8,128)(2,1)} %get-tuple-element.221), channel_id=1, source_target_pairs={{0,2},{2,0},{1,3},{3,1},{4,6},{6,4},{5,7},{7,5},{8,10},{10,8},{9,1... | collective-permute-start | bytes 3244040 | tf_op jit(solution)/shard_map/ppermute | solution.py:1108
  225.4 29.1 %collective-permute-start.26 = (bf16[2,512,512]{2,1,0:T(8,128)(2,1)}, bf16[2,512,512]{2,1,0:T(8,128)(2,1)}, u32[]{:S(2)}, u32[]{:S(2)}) collective-permute-start(bf16[2,512,512]{2,1,0:T(8,128)(2,1)} %get-tuple-element.223), channel_id=1, source_target_pairs={{0,2},{2,0},{1,3},{3,1},{4,6},{6,4},{5,7},{7,5},{8,10},{10,8},{9,1... | collective-permute-start | bytes 3145736 | tf_op jit(solution)/shard_map/ppermute | solution.py:1108
  226.9 27.6 %collective-permute-start.28 = (bf16[528,512]{1,0:T(8,128)(2,1)}, bf16[528,512]{1,0:T(8,128)(2,1)}, u32[]{:S(2)}, u32[]{:S(2)}) collective-permute-start(bf16[528,512]{1,0:T(8,128)(2,1)} %get-tuple-element.224), channel_id=1, source_target_pairs={{16,0},{0,1},{17,16},{1,17},{18,2},{2,3},{19,18},{3,19},{20,4},{4,... | collective-permute-start | bytes 1622024 | tf_op jit(solution)/shard_map/ppermute | solution.py:1283
  226.9 27.6 %collective-permute-start.27 = (bf16[528,512]{1,0:T(8,128)(2,1)}, bf16[528,512]{1,0:T(8,128)(2,1)}, u32[]{:S(2)}, u32[]{:S(2)}) collective-permute-start(bf16[528,512]{1,0:T(8,128)(2,1)} %get-tuple-element.222.own), channel_id=1, source_target_pairs={{16,1},{1,16},{18,3},{3,18},{20,5},{5,20},{22,7},{7,22},{24,9},{9,... | collective-permute-start | bytes 1622024 | tf_op jit(solution)/shard_map/ppermute | solution.py:1282
  260.2 22.2 %collective-permute-start.29 = (bf16[128,2304]{1,0:T(8,128)(2,1)}, bf16[128,2304]{1,0:T(8,128)(2,1)}, u32[]{:S(2)}, u32[]{:S(2)}) collective-permute-start(bf16[128,2304]{1,0:T(8,128)(2,1)} %get-tuple-element.232), channel_id=1, source_target_pairs={{0,2},{2,0},{1,3},{3,1},{4,6},{6,4},{5,7},{7,5},{8,10},{10,8},{9,1... | collective-permute-start | bytes 1769480 | tf_op jit(solution)/shard_map/ppermute | solution.py:1108
  260.7 21.6 %collective-permute-start.31 = (bf16[512,512]{1,0:T(8,128)(2,1)}, bf16[512,512]{1,0:T(8,128)(2,1)}, u32[]{:S(2)}, u32[]{:S(2)}) collective-permute-start(bf16[512,512]{1,0:T(8,128)(2,1)} %get-tuple-element.226.rest_1_), channel_id=1, source_target_pairs={{16,0},{0,1},{17,16},{1,17},{18,2},{2,3},{19,18},{3,19},{20,4},{4,... | collective-permute-start | bytes 1572872 | tf_op jit(solution)/shard_map/ppermute | solution.py:1283
  260.8 21.6 %collective-permute-start.30 = (bf16[512,512]{1,0:T(8,128)(2,1)}, bf16[512,512]{1,0:T(8,128)(2,1)}, u32[]{:S(2)}, u32[]{:S(2)}) collective-permute-start(bf16[512,512]{1,0:T(8,128)(2,1)} %get-tuple-element.225.rest_0_.own), channel_id=1, source_target_pairs={{16,1},{1,16},{18,3},{3,18},{20,5},{5,20},{22,7},{7,22},{24,9},{9,... | collective-permute-start | bytes 1572872 | tf_op jit(solution)/shard_map/ppermute | solution.py:1282
  295.1 14.1 %collective-permute-start.35 = (bf16[32,2304]{1,0:T(8,128)(2,1)}, bf16[32,2304]{1,0:T(8,128)(2,1)}, u32[]{:S(2)}, u32[]{:S(2)}) collective-permute-start(bf16[32,2304]{1,0:T(8,128)(2,1)} %add_parts.2._.refs_0_), channel_id=1, source_target_pairs={{0,16},{16,0},{1,17},{17,1},{2,18},{18,2},{3,19},{19,3},{4,20},{20... | collective-permute-start | bytes 442376 | tf_op jit(solution)/shard_map/ppermute | solution.py:1108
  (8 other events, 53.2 us)
